TPU v7x, 32 devices: a whole 2x2x4 slice. The times are simulated.
32 devices in a mesh: dp: 8 (over z, x), ctx: 4 (over y, core).
Axes of the slice: x: 2, y: 2, z: 4, core: 2. Of those that a mesh axis runs over, the one named last changes fastest.
Arguments:
- activations: bfloat16 [8, 512, 1024], P('dp', 'ctx'), may hold values from -6 to 6
- cotangent: bfloat16 [8, 512, 1024], P('dp', 'ctx'), may hold values from -6 to 6
- live_slots: int32 [8], P('dp'), may hold values 0 or 1
- doc_lengths: int32 [8, 4], P('dp'), may hold values from 1 to 320, 512 in all within a row
- inproj: float32 [1024, 3072], P(('dp', 'ctx')), may hold values from -0.1875 to 0.1875
- mom_inproj: float32 [1024, 3072], P(('dp', 'ctx')), may hold values from -4 to 4
- sqr_inproj: float32 [1024, 3072], P(('dp', 'ctx')), may hold values from 0.1 to 10
- gateproj: float32 [1024, 8], P(('dp', 'ctx')), may hold values from -0.1875 to 0.1875
- mom_gateproj: float32 [1024, 8], P(('dp', 'ctx')), may hold values from -4 to 4
- sqr_gateproj: float32 [1024, 8], P(('dp', 'ctx')), may hold values from 0.1 to 10
- outproj: float32 [1024, 1024], P(None, ('dp', 'ctx')), may hold values from -0.375 to 0.375
- mom_outproj: float32 [1024, 1024], P(None, ('dp', 'ctx')), may hold values from -4 to 4
- sqr_outproj: float32 [1024, 1024], P(None, ('dp', 'ctx')), may hold values from 0.1 to 10
- mlp_gate: float32 [1024, 2816], P(('dp', 'ctx')), may hold values from -0.1875 to 0.1875
- mom_mlp_gate: float32 [1024, 2816], P(('dp', 'ctx')), may hold values from -4 to 4
- sqr_mlp_gate: float32 [1024, 2816], P(('dp', 'ctx')), may hold values from 0.1 to 10
- mlp_up: float32 [1024, 2816], P(('dp', 'ctx')), may hold values from -0.1875 to 0.1875
- mom_mlp_up: float32 [1024, 2816], P(('dp', 'ctx')), may hold values from -4 to 4
- sqr_mlp_up: float32 [1024, 2816], P(('dp', 'ctx')), may hold values from 0.1 to 10
- mlp_down: float32 [2816, 1024], P(None, ('dp', 'ctx')), may hold values from -0.21875 to 0.21875
- mom_mlp_down: float32 [2816, 1024], P(None, ('dp', 'ctx')), may hold values from -4 to 4
- sqr_mlp_down: float32 [2816, 1024], P(None, ('dp', 'ctx')), may hold values from 0.1 to 10
- vectors: float32 [10240], P(('dp', 'ctx')), may hold values from 0.25 to 1.25
- mom_vectors: float32 [10240], P(('dp', 'ctx')), may hold values from -4 to 4
- sqr_vectors: float32 [10240], P(('dp', 'ctx')), may hold values from 0.1 to 10
- headvec: float32 [264], replicated, may hold values from -9 to 2, as said below
- mom_headvec: float32 [264], replicated, may hold values from -4 to 4
- sqr_headvec: float32 [264], replicated, may hold values from 0.1 to 10
Outputs:
- block_out: bfloat16 [8, 512, 1024], P('dp', 'ctx')
- input_grad: bfloat16 [8, 512, 1024], P('dp', 'ctx')
- grad_inproj: float32 [1024, 3072], P(('dp', 'ctx'))
- grad_gateproj: float32 [1024, 8], P(('dp', 'ctx'))
- grad_outproj: float32 [1024, 1024], P(None, ('dp', 'ctx'))
- grad_mlp_gate: float32 [1024, 2816], P(('dp', 'ctx'))
- grad_mlp_up: float32 [1024, 2816], P(('dp', 'ctx'))
- grad_mlp_down: float32 [2816, 1024], P(None, ('dp', 'ctx'))
- grad_vectors: float32 [10240], P(('dp', 'ctx'))
- grad_headvec: float32 [264], replicated
- new_inproj: float32 [1024, 3072], P(('dp', 'ctx'))
- newmom_inproj: float32 [1024, 3072], P(('dp', 'ctx'))
- newsqr_inproj: float32 [1024, 3072], P(('dp', 'ctx'))
- new_gateproj: float32 [1024, 8], P(('dp', 'ctx'))
- newmom_gateproj: float32 [1024, 8], P(('dp', 'ctx'))
- newsqr_gateproj: float32 [1024, 8], P(('dp', 'ctx'))
- new_outproj: float32 [1024, 1024], P(None, ('dp', 'ctx'))
- newmom_outproj: float32 [1024, 1024], P(None, ('dp', 'ctx'))
- newsqr_outproj: float32 [1024, 1024], P(None, ('dp', 'ctx'))
- new_mlp_gate: float32 [1024, 2816], P(('dp', 'ctx'))
- newmom_mlp_gate: float32 [1024, 2816], P(('dp', 'ctx'))
- newsqr_mlp_gate: float32 [1024, 2816], P(('dp', 'ctx'))
- new_mlp_up: float32 [1024, 2816], P(('dp', 'ctx'))
- newmom_mlp_up: float32 [1024, 2816], P(('dp', 'ctx'))
- newsqr_mlp_up: float32 [1024, 2816], P(('dp', 'ctx'))
- new_mlp_down: float32 [2816, 1024], P(None, ('dp', 'ctx'))
- newmom_mlp_down: float32 [2816, 1024], P(None, ('dp', 'ctx'))
- newsqr_mlp_down: float32 [2816, 1024], P(None, ('dp', 'ctx'))
- new_vectors: float32 [10240], P(('dp', 'ctx'))
- newmom_vectors: float32 [10240], P(('dp', 'ctx'))
- newsqr_vectors: float32 [10240], P(('dp', 'ctx'))
- new_headvec: float32 [264], replicated
- newmom_headvec: float32 [264], replicated
- newsqr_headvec: float32 [264], replicated
Inputs may be any that keep to these rules, and one draw needn't show every extreme that they name: `doc_lengths`: each row holds 4 document lengths summing to 512, the largest exactly 320. `headvec`: gains in the first 256 entries, then 4 log scales, then 4 offsets.
All inputs are finite; a program needn't handle non-finite values. No bound on the sum of `live_slots` on one device may be relied on, other than what follows from the above.
Results may differ from a plain program's by a relative error of at most 0.014.
The roundings to bfloat16 on the way count: a program that leaves them out, or rounds other values in their place, can miss the bound.
Values may be sent and summed in bfloat16 or wider, within the bound.
No kernel may reach another device: no remote copies, remote signals or barrier semaphores. Data moves between devices by JAX's collectives and lax.ppermute only.
A program may use at most 256 MiB of HBM per device.

v0:
```python
import jax
import jax.numpy as jnp
from jax import lax
from jax.sharding import PartitionSpec as P

D = 1024
H = 4
DK = 128
DV = 256
CONV = 4
GROUP = 64
STEP = 5
CONVC = 2048


NORM_EPS = 1e-06
exact_mode = lax.Precision.HIGHEST
beta_one = 0.9
beta_two = 0.999
learn_rate = 0.01
weight_decay = 0.1
adam_eps = 1e-08


def from_behind(value, axis, steps):
    count = lax.axis_size(axis)
    initial, last = (max(0, -steps), min(count, count - steps))
    return lax.ppermute(value, axis, [(source, source + steps) for source in range(initial, last)])


def doc_positions(lengths, first, count):
    ends = jnp.cumsum(lengths, axis=-1)
    starts = ends - lengths
    places = first + jnp.arange(count, dtype=jnp.int32)
    owner = jnp.max(
        jnp.where(starts[:, None, :] <= places[None, :, None], starts[:, None, :], 0), axis=-1
    )
    return places[None, :] - owner


def group_step(state, queries, keys_in, values, betas, log_decay, positions):
    width = queries.shape[2]
    cumul = jnp.cumsum(log_decay, axis=-1)
    order_index = jnp.arange(width, dtype=jnp.int32)
    distance = order_index[:, None] - order_index[None, :]
    same_doc = (distance >= 0)[None, None] & (positions[:, None, :, None] >= distance[None, None])
    decays = jnp.exp(jnp.minimum(cumul[..., :, None] - cumul[..., None, :], 0.0)) * same_doc.astype(
        jnp.float32
    )
    carried = jnp.exp(cumul) * (positions[:, None, :] >= order_index[None, None, :] + 1).astype(
        jnp.float32
    )
    key_dots = jnp.einsum("shtk,shik->shti", keys_in, keys_in, precision=exact_mode)
    lower = betas[..., :, None] * decays * key_dots * (distance > 0).astype(jnp.float32)
    key_state = jnp.einsum("shtk,shvk->shtv", keys_in, state, precision=exact_mode)
    targets = betas[..., None] * values - (betas * carried)[..., None] * key_state
    written = jax.scipy.linalg.solve_triangular(
        jnp.eye(width, dtype=jnp.float32) + lower, targets, lower=True, unit_diagonal=True
    )
    query_dots = jnp.einsum("shtk,shik->shti", queries, keys_in, precision=exact_mode)
    query_state = jnp.einsum("shtk,shvk->shtv", queries, state, precision=exact_mode)
    outputs = carried[..., None] * query_state + jnp.einsum(
        "shti,shiv->shtv", decays * query_dots, written, precision=exact_mode
    )
    final_row = decays[..., width - 1, :]
    new_state = carried[..., width - 1][..., None, None] * state + jnp.einsum(
        "shiv,shik->shvk", written, final_row[..., None] * keys_in, precision=exact_mode
    )
    return (new_state, outputs)


def pre_core(proj_ext, beta_decay, conv_taps, log_scale, offsets, positions):
    slots, length = positions.shape
    convolved = jnp.zeros((slots, length, proj_ext.shape[2]), jnp.float32)
    for tap in range(CONV):
        valid = (positions >= CONV - 1 - tap).astype(jnp.float32)[..., None]
        convolved = convolved + conv_taps[tap] * proj_ext[:, tap : tap + length, :] * valid
    acts = jax.nn.silu(convolved)
    width_q = H * DK
    queries = acts[..., :width_q].reshape(slots, length, H, DK)
    keys_in = acts[..., width_q : 2 * width_q].reshape(slots, length, H, DK)
    values = acts[..., 2 * width_q :].reshape(slots, length, H, DV)
    queries = (
        queries * lax.rsqrt(jnp.sum(queries * queries, -1, keepdims=True) + NORM_EPS) * DK ** (-0.5)
    )
    keys_in = keys_in * lax.rsqrt(jnp.sum(keys_in * keys_in, -1, keepdims=True) + NORM_EPS)
    betas = jax.nn.sigmoid(beta_decay[..., :H])
    log_decay = -jnp.exp(log_scale) * jax.nn.softplus(beta_decay[..., H:] + offsets)
    queries = jnp.transpose(queries, (0, 2, 1, 3))
    keys_in = jnp.transpose(keys_in, (0, 2, 1, 3))
    values = jnp.transpose(values, (0, 2, 1, 3))
    betas = jnp.transpose(betas, (0, 2, 1))
    log_decay = jnp.transpose(log_decay, (0, 2, 1))
    values_aug = jnp.concatenate([values, jnp.zeros((slots, H, length, DK), jnp.float32)], axis=-1)
    ident = jnp.broadcast_to(jnp.eye(DK, dtype=jnp.float32), (slots, H, DK, DK))
    state = jnp.concatenate([jnp.zeros((slots, H, DV, DK), jnp.float32), ident], axis=2)
    pieces = []
    for offset in range(0, length, GROUP):
        part = slice(offset, offset + GROUP)
        state, outputs = group_step(
            state,
            queries[:, :, part],
            keys_in[:, :, part],
            values_aug[:, :, part],
            betas[:, :, part],
            log_decay[:, :, part],
            positions[:, part],
        )
        pieces.append(outputs)
    outs_all = jnp.concatenate(pieces, axis=2)
    return (state[:, :, DV:, :], state[:, :, :DV, :], outs_all[..., :DV], outs_all[..., DV:])


def post_core(local_out, query_mix, state_in, gate, head_gain):
    slots, heads, length, _ = local_out.shape
    full = local_out + jnp.einsum("shtk,shvk->shtv", query_mix, state_in, precision=exact_mode)
    full = full * lax.rsqrt(jnp.mean(full * full, -1, keepdims=True) + NORM_EPS) * head_gain
    full = jnp.transpose(full, (0, 2, 1, 3)).reshape(slots, length, heads * DV)
    return full * jax.nn.silu(gate)


def adamw(weights, moment, square, grads):
    new_moment = beta_one * moment + (1.0 - beta_one) * grads
    new_square = beta_two * square + (1.0 - beta_two) * grads * grads
    corrected = new_moment / (1.0 - beta_one**STEP)
    scaled = new_square / (1.0 - beta_two**STEP)
    new_weights = weights - learn_rate * (
        corrected / (jnp.sqrt(scaled) + adam_eps) + weight_decay * weights
    )
    return (new_weights, new_moment, new_square)


def local(
    activations,
    cotangent,
    live_slots,
    doc_lengths,
    inproj,
    mom_inproj,
    sqr_inproj,
    gateproj,
    mom_gateproj,
    sqr_gateproj,
    outproj,
    mom_outproj,
    sqr_outproj,
    mlp_gate,
    mom_mlp_gate,
    sqr_mlp_gate,
    mlp_up,
    mom_mlp_up,
    sqr_mlp_up,
    mlp_down,
    mom_mlp_down,
    sqr_mlp_down,
    vectors,
    mom_vectors,
    sqr_vectors,
    headvec,
    mom_headvec,
    sqr_headvec,
):
    full_in, full_ab, full_out, full_wg, full_wu, full_wd, vec_used = (
        lax.all_gather(inproj.astype(jnp.bfloat16), ("dp", "ctx"), axis=0, tiled=True),
        lax.all_gather(gateproj.astype(jnp.bfloat16), ("dp", "ctx"), axis=0, tiled=True),
        lax.all_gather(outproj.astype(jnp.bfloat16), ("dp", "ctx"), axis=1, tiled=True),
        lax.all_gather(mlp_gate.astype(jnp.bfloat16), ("dp", "ctx"), axis=0, tiled=True),
        lax.all_gather(mlp_up.astype(jnp.bfloat16), ("dp", "ctx"), axis=0, tiled=True),
        lax.all_gather(mlp_down.astype(jnp.bfloat16), ("dp", "ctx"), axis=1, tiled=True),
        lax.all_gather(vectors.astype(jnp.bfloat16), ("dp", "ctx"), axis=0, tiled=True),
    )
    vec_float = vec_used.astype(jnp.float32)
    norm_gain = vec_float[:D]
    conv_taps = vec_float[D : D + CONV * CONVC].reshape(CONV, CONVC)
    mlp_gain = vec_float[D + CONV * CONVC :]
    head_gain = headvec[:DV]
    log_scale = headvec[DV : DV + H]
    offsets = headvec[DV + H :]
    slots, length = (activations.shape[0], activations.shape[1])
    n_ctx = lax.axis_size("ctx")
    positions = doc_positions(doc_lengths, lax.axis_index("ctx") * length, length)
    live_f = live_slots.astype(jnp.float32)[:, None, None]
    xfull = activations.astype(jnp.float32)
    inv_rms = lax.rsqrt(jnp.mean(xfull * xfull, -1, keepdims=True) + NORM_EPS)
    unit = xfull * inv_rms
    normed = (unit * norm_gain).astype(jnp.bfloat16)
    proj = jnp.einsum("spd,dc->spc", normed, full_in, preferred_element_type=jnp.float32)
    beta_decay = jnp.einsum("spd,dc->spc", normed, full_ab, preferred_element_type=jnp.float32)
    rim_rows = from_behind(normed[:, length - (CONV - 1) :, :], "ctx", 1)
    rim_proj = jnp.einsum(
        "spd,dc->spc", rim_rows, full_in[:, :CONVC], preferred_element_type=jnp.float32
    )
    proj_ext = jnp.concatenate([rim_proj, proj[..., :CONVC]], axis=1)
    gate = proj[..., CONVC:]

    def local_core(ext_in, bd_in, taps_in, scale_in, offs_in):
        return pre_core(ext_in, bd_in, taps_in, scale_in, offs_in, positions)

    (p_mat, u_mat, local_out, query_mix), core_back = jax.vjp(
        local_core, proj_ext, beta_decay, conv_taps, log_scale, offsets
    )
    state_in = jnp.zeros_like(u_mat)
    for turn in range(n_ctx - 1):
        leaving = jnp.einsum("shvk,shkl->shvl", state_in, p_mat, precision=exact_mode) + u_mat
        state_in = from_behind(leaving.astype(jnp.bfloat16), "ctx", 1).astype(leaving.dtype)
    mixed_f, post_back = jax.vjp(post_core, local_out, query_mix, state_in, gate, head_gain)
    mixed = mixed_f.astype(jnp.bfloat16)
    branch = jnp.einsum("spe,ed->spd", mixed, full_out, preferred_element_type=jnp.float32)
    resid = xfull + live_f * branch
    inv_two = lax.rsqrt(jnp.mean(resid * resid, -1, keepdims=True) + NORM_EPS)
    unit_two = resid * inv_two
    normed_two = (unit_two * mlp_gain).astype(jnp.bfloat16)
    hgate = jnp.einsum("spd,df->spf", normed_two, full_wg, preferred_element_type=jnp.float32)
    hup = jnp.einsum("spd,df->spf", normed_two, full_wu, preferred_element_type=jnp.float32)
    sigma = jax.nn.sigmoid(hgate)
    silu_gate = hgate * sigma
    hidden = (silu_gate * hup).astype(jnp.bfloat16)
    mlp_out = jnp.einsum("spf,fd->spd", hidden, full_wd, preferred_element_type=jnp.float32)
    block_out = (resid + live_f * mlp_out).astype(jnp.bfloat16)
    cot_f = cotangent.astype(jnp.float32)
    g_mlp = (cot_f * live_f).astype(jnp.bfloat16)
    d_hidden = jnp.einsum("spd,fd->spf", g_mlp, full_wd, preferred_element_type=jnp.float32)
    grad_wd = jnp.einsum("spf,spd->fd", hidden, g_mlp, preferred_element_type=jnp.float32)
    d_hgate = (d_hidden * hup * sigma * (1.0 + hgate * (1.0 - sigma))).astype(jnp.bfloat16)
    d_hup = (d_hidden * silu_gate).astype(jnp.bfloat16)
    grad_wg = jnp.einsum("spd,spf->df", normed_two, d_hgate, preferred_element_type=jnp.float32)
    grad_wu = jnp.einsum("spd,spf->df", normed_two, d_hup, preferred_element_type=jnp.float32)
    d_normed_two = jnp.einsum(
        "spf,df->spd", d_hgate, full_wg, preferred_element_type=jnp.float32
    ) + jnp.einsum("spf,df->spd", d_hup, full_wu, preferred_element_type=jnp.float32)
    d_gain_two = jnp.sum(d_normed_two * unit_two, axis=(0, 1))
    d_unit_two = d_normed_two * mlp_gain
    d_resid = cot_f + inv_two * (
        d_unit_two - unit_two * jnp.mean(d_unit_two * unit_two, -1, keepdims=True)
    )
    g_branch = (d_resid * live_f).astype(jnp.bfloat16)
    d_mixed = jnp.einsum("spd,ed->spe", g_branch, full_out, preferred_element_type=jnp.float32)
    grad_out = jnp.einsum("spe,spd->ed", mixed, g_branch, preferred_element_type=jnp.float32)
    d_local, d_query, d_state, d_gate, d_hgain = post_back(d_mixed)
    state_cot = jnp.zeros_like(d_state)
    for turn in range(n_ctx - 1):
        leaving_cot = d_state + jnp.einsum(
            "shvl,shkl->shvk", state_cot, p_mat, precision=exact_mode
        )
        state_cot = from_behind(leaving_cot.astype(jnp.bfloat16), "ctx", -1).astype(
            leaving_cot.dtype
        )
    d_pmat = jnp.einsum("shvk,shvl->shkl", state_in, state_cot, precision=exact_mode)
    d_ext, d_bd, d_taps, d_scale, d_offs = core_back((d_pmat, state_cot, d_local, d_query))
    rim_cot = from_behind(d_ext[:, : CONV - 1, :], "ctx", -1)
    d_conv_cols = d_ext[:, CONV - 1 :, :] + jnp.pad(
        rim_cot, ((0, 0), (length - (CONV - 1), 0), (0, 0))
    )
    d_proj = jnp.concatenate([d_conv_cols, d_gate], axis=-1).astype(jnp.bfloat16)
    d_bd_b = d_bd.astype(jnp.bfloat16)
    grad_in = jnp.einsum("spd,spc->dc", normed, d_proj, preferred_element_type=jnp.float32)
    grad_ab = jnp.einsum("spd,spc->dc", normed, d_bd_b, preferred_element_type=jnp.float32)
    d_normed = jnp.einsum(
        "spc,dc->spd", d_proj, full_in, preferred_element_type=jnp.float32
    ) + jnp.einsum("spc,dc->spd", d_bd_b, full_ab, preferred_element_type=jnp.float32)
    d_gain = jnp.sum(d_normed * unit, axis=(0, 1))
    d_unit = d_normed * norm_gain
    input_grad = (
        d_resid + inv_rms * (d_unit - unit * jnp.mean(d_unit * unit, -1, keepdims=True))
    ).astype(jnp.bfloat16)
    grad_vec = jnp.concatenate([d_gain, d_taps.reshape(-1), d_gain_two])
    grad_small = jnp.concatenate([d_hgain, d_scale, d_offs])
    owned_in, owned_ab, owned_out, owned_wg, owned_wu, owned_wd, owned_vec = (
        lax.psum_scatter(grad_in, ("dp", "ctx"), scatter_dimension=0, tiled=True),
        lax.psum_scatter(grad_ab, ("dp", "ctx"), scatter_dimension=0, tiled=True),
        lax.psum_scatter(grad_out, ("dp", "ctx"), scatter_dimension=1, tiled=True),
        lax.psum_scatter(grad_wg, ("dp", "ctx"), scatter_dimension=0, tiled=True),
        lax.psum_scatter(grad_wu, ("dp", "ctx"), scatter_dimension=0, tiled=True),
        lax.psum_scatter(grad_wd, ("dp", "ctx"), scatter_dimension=1, tiled=True),
        lax.psum_scatter(grad_vec, ("dp", "ctx"), scatter_dimension=0, tiled=True),
    )
    summed_small = lax.psum(grad_small, ("dp", "ctx"))
    n_in, nm_in, ns_in = adamw(inproj, mom_inproj, sqr_inproj, owned_in)
    n_ab, nm_ab, ns_ab = adamw(gateproj, mom_gateproj, sqr_gateproj, owned_ab)
    n_out, nm_out, ns_out = adamw(outproj, mom_outproj, sqr_outproj, owned_out)
    n_wg, nm_wg, ns_wg = adamw(mlp_gate, mom_mlp_gate, sqr_mlp_gate, owned_wg)
    n_wu, nm_wu, ns_wu = adamw(mlp_up, mom_mlp_up, sqr_mlp_up, owned_wu)
    n_wd, nm_wd, ns_wd = adamw(mlp_down, mom_mlp_down, sqr_mlp_down, owned_wd)
    n_vec, nm_vec, ns_vec = adamw(vectors, mom_vectors, sqr_vectors, owned_vec)
    n_small, nm_small, ns_small = adamw(headvec, mom_headvec, sqr_headvec, summed_small)
    return (
        block_out,
        input_grad,
        owned_in,
        owned_ab,
        owned_out,
        owned_wg,
        owned_wu,
        owned_wd,
        owned_vec,
        summed_small,
        n_in,
        nm_in,
        ns_in,
        n_ab,
        nm_ab,
        ns_ab,
        n_out,
        nm_out,
        ns_out,
        n_wg,
        nm_wg,
        ns_wg,
        n_wu,
        nm_wu,
        ns_wu,
        n_wd,
        nm_wd,
        ns_wd,
        n_vec,
        nm_vec,
        ns_vec,
        n_small,
        nm_small,
        ns_small,
    )


def solution(mesh):
    placed = (
        P("dp", "ctx", None),
        P("dp", "ctx", None),
        P("dp"),
        P("dp", None),
        P(("dp", "ctx"), None),
        P(("dp", "ctx"), None),
        P(("dp", "ctx"), None),
        P(("dp", "ctx"), None),
        P(("dp", "ctx"), None),
        P(("dp", "ctx"), None),
        P(None, ("dp", "ctx")),
        P(None, ("dp", "ctx")),
        P(None, ("dp", "ctx")),
        P(("dp", "ctx"), None),
        P(("dp", "ctx"), None),
        P(("dp", "ctx"), None),
        P(("dp", "ctx"), None),
        P(("dp", "ctx"), None),
        P(("dp", "ctx"), None),
        P(None, ("dp", "ctx")),
        P(None, ("dp", "ctx")),
        P(None, ("dp", "ctx")),
        P(("dp", "ctx")),
        P(("dp", "ctx")),
        P(("dp", "ctx")),
        P(),
        P(),
        P(),
    )
    return jax.shard_map(
        local,
        mesh=mesh,
        in_specs=placed,
        out_specs=(
            P("dp", "ctx", None),
            P("dp", "ctx", None),
            P(("dp", "ctx"), None),
            P(("dp", "ctx"), None),
            P(None, ("dp", "ctx")),
            P(("dp", "ctx"), None),
            P(("dp", "ctx"), None),
            P(None, ("dp", "ctx")),
            P(("dp", "ctx")),
            P(),
            P(("dp", "ctx"), None),
            P(("dp", "ctx"), None),
            P(("dp", "ctx"), None),
            P(("dp", "ctx"), None),
            P(("dp", "ctx"), None),
            P(("dp", "ctx"), None),
            P(None, ("dp", "ctx")),
            P(None, ("dp", "ctx")),
            P(None, ("dp", "ctx")),
            P(("dp", "ctx"), None),
            P(("dp", "ctx"), None),
            P(("dp", "ctx"), None),
            P(("dp", "ctx"), None),
            P(("dp", "ctx"), None),
            P(("dp", "ctx"), None),
            P(None, ("dp", "ctx")),
            P(None, ("dp", "ctx")),
            P(None, ("dp", "ctx")),
            P(("dp", "ctx")),
            P(("dp", "ctx")),
            P(("dp", "ctx")),
            P(),
            P(),
            P(),
        ),
        check_vma=False,
    )
```

profile of v0, /device:TPU:0, one launch (start us, length us, event | category | flops | bytes accessed | tf_op | source)
XLA Modules:
  0.0 1382.2 jit_solution(6939329282184733915)
XLA Ops:
  14.6 42.4 %all-reduce.34 = bf16[10240]{0:T(1024)(128)(2,1)S(1)} all-reduce(bf16[10240]{0:T(1024)(128)(2,1)S(1)} %dynamic-update-slice), channel_id=1, replica_groups=mesh['dp'=8,'ctx'=4] {'dp','ctx'}, use_global_device_ids=true, to_apply=%add.34 | all-reduce | flops 10240 | bytes 40960
  61.3 41.5 %all-gather = bf16[32,32,8]{1,2,0:T(8,128)(2,1)S(1)} all-gather(bf16[1,32,8]{1,2,0:T(8,128)(2,1)S(1)} %convert_bitcast_fusion), channel_id=1, replica_groups=mesh['dp'=8,'ctx'=4] {'dp','ctx'}, dimensions={0}, use_global_device_ids=true | all-gather | bytes 16896 | tf_op jit(solution)/shard_map/all_gather | solution.py:165
  108.1 3.9 convolution_bitcast_fusion
  118.3 19.7 %custom-call.10 = f32[4,1,64,64]{2,3,1,0:T(8,128)S(1)} custom-call(f32[4,1,64,64]{3,2,1,0:T(8,128)S(1)} %get-tuple-element.146), custom_call_target="InvertDiagBlocksLowerTriangular" | custom-call | tf_op jit(solution)/shard_map/jvp(jit(_solve_triangular))/vmap()/triangular_solve | solution.py:57
  138.7 19.7 %custom-call.11 = f32[4,1,64,64]{2,3,1,0:T(8,128)S(1)} custom-call(f32[4,1,64,64]{3,2,1,0:T(8,128)S(1)} %get-tuple-element.145), custom_call_target="InvertDiagBlocksLowerTriangular" | custom-call | tf_op jit(solution)/shard_map/jvp(jit(_solve_triangular))/vmap()/triangular_solve | solution.py:57
  170.9 6.6 collective-permute-start.2
  179.4 6.1 collective-permute-start.3
  194.7 18.0 %all-gather.11.cloned.1.call-done = bf16[1024,2816]{1,0:T(8,128)(2,1)} async-done(((bf16[32,2816]{1,0:T(8,128)(2,1)}), bf16[1024,2816]{1,0:T(8,128)(2,1)}) %all-gather.11.cloned.1.call-update) | async-done | bytes 5767184 | tf_op jit(solution)/shard_map/all_gather | solution.py:167
  212.8 4.7 fusion.415
  217.5 64.6 %all-gather.13.cloned.1.call-done = bf16[1024,2816]{1,0:T(8,128)(2,1)} async-done(((bf16[32,2816]{1,0:T(8,128)(2,1)}), bf16[1024,2816]{1,0:T(8,128)(2,1)}) %all-gather.13.cloned.1.call-update) | async-done | bytes 5767184 | tf_op jit(solution)/shard_map/all_gather | solution.py:168
  282.1 4.7 fusion.416
  286.7 64.6 %all-gather.15.cloned.1.call-done = bf16[2816,1024]{0,1:T(8,128)(2,1)} async-done(((bf16[2816,32]{0,1:T(8,128)(2,1)}), bf16[2816,1024]{0,1:T(8,128)(2,1)}) %all-gather.15.cloned.1.call-update) | async-done | bytes 5767184 | tf_op jit(solution)/shard_map/all_gather | solution.py:169
  351.3 5.8 multiply_convert_fusion
  357.1 5.1 fusion.417
  376.8 21.0 %custom-call.12 = f32[4,1,64,64]{2,3,1,0:T(8,128)} custom-call(f32[4,1,64,64]{3,2,1,0:T(8,128)} %get-tuple-element.144), custom_call_target="InvertDiagBlocksLowerTriangular" | custom-call | tf_op jit(solution)/shard_map/transpose(jvp(jit(_solve_triangular)))/vmap()/triangular_solve | solution.py:57
  397.8 20.3 %custom-call.13 = f32[4,1,64,64]{2,3,1,0:T(8,128)} custom-call(f32[4,1,64,64]{3,2,1,0:T(8,128)S(1)} %get-tuple-element.143), custom_call_target="InvertDiagBlocksLowerTriangular" | custom-call | tf_op jit(solution)/shard_map/transpose(jvp(jit(_solve_triangular)))/vmap()/triangular_solve | solution.py:57
  430.4 4.2 collective-permute-done.6
  464.6 3.9 fusion.244
  482.4 5.6 collective-permute-done.7
  488.1 6.4 fusion.99
  495.7 6.0 fusion.421
  502.8 6.0 fusion.420
  509.9 5.9 fusion.172
  515.9 5.3 fusion.20
  521.5 5.1 fusion.100
  527.2 41.8 %all-reduce.36 = (f32[10240]{0:T(1024)S(1)}, f32[264]{0:T(512)S(1)}) all-reduce(f32[10240]{0:T(1024)S(1)} %pad_maximum_fusion.5, f32[264]{0:T(512)S(1)} %pad_maximum_fusion.6), channel_id=8, replica_groups=mesh['dp'=8,'ctx'=4] {'dp','ctx'}, use_global_device_ids=true, to_apply=%region_44.47.clone | all-reduce | flops 10504 | bytes 84032
  571.3 32.0 %reduce-scatter.19.cloned.1.call-done = f32[32,8]{1,0:T(8,128)} async-done(((f32[1024,8]{1,0:T(8,128)}), f32[32,8]{1,0:T(8,128)}) %reduce-scatter.19.cloned.1.call-update) | async-done | bytes 1040
  604.8 139.7 %reduce-scatter.11.cloned.1.call-done = f32[1024,32]{0,1:T(8,128)} async-done(((f32[1024,1024]{0,1:T(8,128)}), f32[1024,32]{0,1:T(8,128)}) %reduce-scatter.11.cloned.1.call-update) | async-done | bytes 131088 | tf_op jit(solution)/shard_map/reduce_scatter | solution.py:271
  746.3 155.7 %reduce-scatter.9.cloned.1.call-done = f32[32,3072]{1,0:T(8,128)} async-done(((f32[1024,3072]{1,0:T(8,128)}), f32[32,3072]{1,0:T(8,128)}) %reduce-scatter.9.cloned.1.call-update) | async-done | bytes 393232 | tf_op jit(solution)/shard_map/reduce_scatter | solution.py:269
  904.1 155.0 %reduce-scatter.15.cloned.1.call-done = f32[32,2816]{1,0:T(8,128)} async-done(((f32[1024,2816]{1,0:T(8,128)}), f32[32,2816]{1,0:T(8,128)}) %reduce-scatter.15.cloned.1.call-update) | async-done | bytes 360464 | tf_op jit(solution)/shard_map/reduce_scatter | solution.py:273
  1061.2 155.2 %reduce-scatter.13.cloned.1.call-done = f32[32,2816]{1,0:T(8,128)} async-done(((f32[1024,2816]{1,0:T(8,128)}), f32[32,2816]{1,0:T(8,128)}) %reduce-scatter.13.cloned.1.call-update) | async-done | bytes 360464 | tf_op jit(solution)/shard_map/reduce_scatter | solution.py:272
  1218.7 154.6 %reduce-scatter.17.cloned.1.call-done = f32[2816,32]{0,1:T(8,128)} async-done(((f32[2816,1024]{0,1:T(8,128)}), f32[2816,32]{0,1:T(8,128)}) %reduce-scatter.17.cloned.1.call-update) | async-done | bytes 360464 | tf_op jit(solution)/shard_map/reduce_scatter | solution.py:274
  (649 shorter events, 133.1 us)
Async XLA Ops:
  7.3 100.8 %all-gather.7.cloned.1.call-start = ((), (), s32[]{:S(2)}) async-start(), calls=%async_computation.6 | async-start | bytes 6488064 | tf_op jit(solution)/shard_map/all_gather | solution.py:164
  9.1 181.7 %all-gather.9.cloned.1.call-start = ((), (), s32[]{:S(2)}) async-start(), calls=%async_computation.7 | async-start | bytes 2162688 | tf_op jit(solution)/shard_map/all_gather | solution.py:166
  10.7 202.0 %all-gather.11.cloned.1.call-start = ((), (), s32[]{:S(2)}) async-start(), calls=%async_computation.8 | async-start | bytes 5947392 | tf_op jit(solution)/shard_map/all_gather | solution.py:167
  12.5 269.6 %all-gather.13.cloned.1.call-start = ((), (), s32[]{:S(2)}) async-start(), calls=%async_computation.9 | async-start | bytes 5947392 | tf_op jit(solution)/shard_map/all_gather | solution.py:168
  14.2 337.1 %all-gather.15.cloned.1.call-start = ((), (), s32[]{:S(2)}) async-start(), calls=%async_computation.10 | async-start | bytes 5947392 | tf_op jit(solution)/shard_map/all_gather | solution.py:169
  57.9 54.4 %collective-permute-start = (bf16[1,3,1024]{2,1,0:T(4,128)(2,1)S(1)}, bf16[1,3,1024]{2,1,0:T(4,128)(2,1)S(1)}, u32[]{:S(2)}, u32[]{:S(2)}) collective-permute-start(bf16[1,3,1024]{2,1,0:T(4,128)(2,1)S(1)} %slice.195), channel_id=1, source_target_pairs={{0,1},{1,2},{2,3},{4,5},{5,6},{6,7},{8,9},{9,10},{10,11},{12,13},{... | collective-permute-start | bytes 18440 | tf_op jit(solution)/shard_map/ppermute | solution.py:28
  60.0 543.3 %reduce-scatter.19.cloned.1.call-start = ((), (), s32[]{:S(2)}) async-start(), calls=%async_computation.16 | async-start | bytes 540672
  166.8 3.7 collective-permute-start.1
  170.9 8.1 collective-permute-start.2
  179.4 7.3 collective-permute-start.3
  374.2 45.5 %collective-permute-start.4 = (bf16[1,4,256,128]{3,2,1,0:T(8,128)(2,1)}, bf16[1,4,256,128]{3,2,1,0:T(8,128)(2,1)S(1)}, u32[]{:S(2)}, u32[]{:S(2)}) collective-permute-start(bf16[1,4,256,128]{3,2,1,0:T(8,128)(2,1)} %fusion.33), channel_id=1, source_target_pairs={{1,0},{2,1},{3,2},{5,4},{6,5},{7,6},{9,8},{10,9},{11,10},{13,12},{... | collective-permute-start | bytes 786440 | tf_op jit(solution)/shard_map/ppermute | solution.py:28
  421.3 4.2 collective-permute-start.5
  426.8 7.7 collective-permute-start.6
  464.6 279.9 %reduce-scatter.11.cloned.1.call-start = ((), (), s32[]{:S(2)}) async-start(), calls=%async_computation.12 | async-start | bytes 4325376 | tf_op jit(solution)/shard_map/reduce_scatter | solution.py:271
  468.6 433.3 %reduce-scatter.9.cloned.1.call-start = ((), (), s32[]{:S(2)}) async-start(), calls=%async_computation.11 | async-start | bytes 12976128 | tf_op jit(solution)/shard_map/reduce_scatter | solution.py:269
  480.5 7.5 collective-permute-start.7
  494.6 564.5 %reduce-scatter.15.cloned.1.call-start = ((), (), s32[]{:S(2)}) async-start(), calls=%async_computation.14 | async-start | bytes 11894784 | tf_op jit(solution)/shard_map/reduce_scatter | solution.py:273
  501.7 714.7 %reduce-scatter.13.cloned.1.call-start = ((), (), s32[]{:S(2)}) async-start(), calls=%async_computation.13 | async-start | bytes 11894784 | tf_op jit(solution)/shard_map/reduce_scatter | solution.py:272
  508.8 864.5 %reduce-scatter.17.cloned.1.call-start = ((), (), s32[]{:S(2)}) async-start(), calls=%async_computation.15 | async-start | bytes 11894784 | tf_op jit(solution)/shard_map/reduce_scatter | solution.py:274
  526.7 217.8 %copy-start.95 = (f32[1024,32]{0,1:T(8,128)S(1)}, f32[1024,32]{0,1:T(8,128)}, u32[]{:S(2)}) copy-start(f32[1024,32]{0,1:T(8,128)} %param.44) | copy-start | bytes 393220
  526.7 375.2 %copy-start.78 = (f32[32,3072]{1,0:T(8,128)S(1)}, f32[32,3072]{1,0:T(8,128)}, u32[]{:S(2)}) copy-start(f32[32,3072]{1,0:T(8,128)} %param.38) | copy-start | bytes 1179652
  526.8 375.2 %copy-start.98 = (f32[32,3072]{1,0:T(8,128)S(1)}, f32[32,3072]{1,0:T(8,128)}, u32[]{:S(2)}) copy-start(f32[32,3072]{1,0:T(8,128)} %param.39) | copy-start | bytes 1179652
  526.8 375.2 %copy-start.99 = (f32[32,3072]{1,0:T(8,128)S(1)}, f32[32,3072]{1,0:T(8,128)}, u32[]{:S(2)}) copy-start(f32[32,3072]{1,0:T(8,128)} %param.40) | copy-start | bytes 1179652
  569.0 335.1 %copy-start.214 = (f32[264]{0:T(512)}, f32[264]{0:T(512)S(1)}, u32[]{:S(2)}) copy-start(f32[264]{0:T(512)S(1)} %get-tuple-element.79) | copy-start | bytes 3172
  571.3 487.8 %copy-start.81 = (f32[32,2816]{1,0:T(8,128)S(1)}, f32[32,2816]{1,0:T(8,128)}, u32[]{:S(2)}) copy-start(f32[32,2816]{1,0:T(8,128)} %param.50) | copy-start | bytes 1081348
  571.3 487.8 %copy-start.100 = (f32[32,2816]{1,0:T(8,128)S(1)}, f32[32,2816]{1,0:T(8,128)}, u32[]{:S(2)}) copy-start(f32[32,2816]{1,0:T(8,128)} %param.51) | copy-start | bytes 1081348
  571.3 487.8 %copy-start.101 = (f32[32,2816]{1,0:T(8,128)S(1)}, f32[32,2816]{1,0:T(8,128)}, u32[]{:S(2)}) copy-start(f32[32,2816]{1,0:T(8,128)} %param.52) | copy-start | bytes 1081348
  604.1 457.1 %copy-start.172 = (f32[32,8]{0,1:T(8,128)}, f32[32,8]{0,1:T(8,128)S(1)}, u32[]{:S(2)}) copy-start(f32[32,8]{0,1:T(8,128)S(1)} %copy.323) | copy-start | bytes 3076
  746.3 470.1 %copy-start.82 = (f32[32,2816]{1,0:T(8,128)S(1)}, f32[32,2816]{1,0:T(8,128)}, u32[]{:S(2)}) copy-start(f32[32,2816]{1,0:T(8,128)} %param.47) | copy-start | bytes 1081348
  904.1 469.2 %copy-start.84 = (f32[2816,32]{0,1:T(8,128)S(1)}, f32[2816,32]{0,1:T(8,128)}, u32[]{:S(2)}) copy-start(f32[2816,32]{0,1:T(8,128)} %param.53) | copy-start | bytes 1081348
  904.1 469.2 %copy-start.102 = (f32[2816,32]{0,1:T(8,128)S(1)}, f32[2816,32]{0,1:T(8,128)}, u32[]{:S(2)}) copy-start(f32[2816,32]{0,1:T(8,128)} %param.54) | copy-start | bytes 1081348
  904.1 469.2 %copy-start.103 = (f32[2816,32]{0,1:T(8,128)S(1)}, f32[2816,32]{0,1:T(8,128)}, u32[]{:S(2)}) copy-start(f32[2816,32]{0,1:T(8,128)} %param.55) | copy-start | bytes 1081348
  (205 other events, 2658.2 us)
Sparse Core Ops, SparseCore 0:
  11.6 72.4 all-gather.6
  87.5 55.5 all-gather.8
  146.5 66.2 all-gather.10
  216.1 65.9 all-gather.12
  285.4 65.9 all-gather.14
  464.7 138.5 reduce-scatter.18
  606.2 138.2 reduce-scatter.10
  751.1 150.7 reduce-scatter.8
  904.8 154.2 reduce-scatter.14
  1061.8 154.4 reduce-scatter.12
  1219.3 153.9 reduce-scatter.16
where the time goes:
time: 1400 us; the launch traced here: 1380 us
  waiting for transfers between devices  950 us (68%)
  blocking collectives  126 us (9%)
  matrix products  124 us (9%)
  other arithmetic  123 us (9%)
  starting transfers between devices  23 us (2%)
  between operations  18.1 us (1%)
  local copies, waits for them, and re-layouts  17.9 us (1%)
    reduce_scatter x1, waiting for transfers between devices, local(): lax.psum_scatter(grad_in, ('dp', 'ctx'), scatter_dimension=0, tiled=True)  156 us
    reduce_scatter x1, waiting for transfers between devices, local(): lax.psum_scatter(grad_wg, ('dp', 'ctx'), scatter_dimension=0, tiled=True)  155 us
    reduce_scatter x1, waiting for transfers between devices, local(): lax.psum_scatter(grad_wu, ('dp', 'ctx'), scatter_dimension=0, tiled=True)  155 us
    reduce_scatter x1, waiting for transfers between devices, local(): lax.psum_scatter(grad_wd, ('dp', 'ctx'), scatter_dimension=1, tiled=True)  155 us
    reduce_scatter x1, waiting for transfers between devices, local(): lax.psum_scatter(grad_out, ('dp', 'ctx'), scatter_dimension=1, tiled=True)  140 us
    unnamed x2, blocking collectives  84.2 us
    another operation x9, other arithmetic, group_step(): jax.scipy.linalg.solve_triangular(jnp.eye(width, dtype=jnp.float32) + low...  81.9 us
    all_gather x1, waiting for transfers between devices, local(): lax.all_gather(mlp_down.astype(jnp.bfloat16), ('dp', 'ctx'), axis=1, tile...  64.6 us
  transfers between devices with their start and end apart: 19, of which 12 were waited for; matrix products, arithmetic and copies ran while one was open for 14% of the time, Pallas kernels for 0%

commit v1 on v0

v1 whole, which is shorter than its diff:
```python
import jax
import jax.numpy as jnp
from jax import lax
from jax.experimental import pallas as pl
from jax.experimental.pallas import tpu as pltpu
from jax.sharding import PartitionSpec as P

D = 1024
H = 4
DK = 128
DV = 256
CONV = 4
GROUP = 64
STEP = 5
CONVC = 2048

NORM_EPS = 1e-06
beta_one = 0.9
beta_two = 0.999
learn_rate = 0.01
weight_decay = 0.1
adam_eps = 1e-08

F32 = jnp.float32
BF = jnp.bfloat16
EXACT = lax.Precision.HIGHEST

HEADQ = DK
HEADC = 2 * DK + DV
HEADG = HEADC + DV
EXTRA = 128


def mm(a, b, lhs=1, rhs=0):
    return lax.dot_general(
        a, b, (((lhs,), (rhs,)), ((), ())), precision=EXACT, preferred_element_type=F32
    )


def shift_rows(value, steps):
    return pltpu.roll(value, steps % value.shape[0], axis=0)


def pre_stage(px_ref, taps_ref, par_ref, pos_ref):
    rows = px_ref.shape[0]
    pos = pos_ref[...]
    x = px_ref[:, :HEADC]
    conv = x * taps_ref[CONV - 1 : CONV, :]
    for s in range(1, CONV):
        valid = (pos >= s).astype(F32)
        conv = conv + taps_ref[CONV - 1 - s : CONV - s, :] * (shift_rows(x, s) * valid)
    sig = jax.nn.sigmoid(conv)
    act = conv * sig
    qr = act[:, :DK]
    kr = act[:, DK : 2 * DK]
    v = act[:, 2 * DK :]
    rq = lax.rsqrt(jnp.sum(qr * qr, -1, keepdims=True) + NORM_EPS)
    rk = lax.rsqrt(jnp.sum(kr * kr, -1, keepdims=True) + NORM_EPS)
    q = qr * rq * DK ** (-0.5)
    k = kr * rk
    mix = px_ref[:, HEADG : HEADG + EXTRA]
    lane = lax.broadcasted_iota(jnp.int32, (rows, EXTRA), 1)
    b_raw = jnp.sum(jnp.where(lane == 0, mix, 0.0), -1, keepdims=True)
    a_raw = jnp.sum(jnp.where(lane == 1, mix, 0.0), -1, keepdims=True)
    beta = jax.nn.sigmoid(b_raw)
    scale = -jnp.exp(jnp.zeros((rows, 1), F32) + par_ref[0])
    shifted = a_raw + par_ref[1]
    soft = jnp.maximum(shifted, 0.0) + jnp.log1p(jnp.exp(-jnp.abs(shifted)))
    logd = scale * soft
    return pos, x, conv, sig, qr, kr, rq, rk, q, k, v, beta, scale, shifted, logd


def block_masks(width):
    row = lax.broadcasted_iota(jnp.int32, (width, width), 0)
    col = lax.broadcasted_iota(jnp.int32, (width, width), 1)
    same = (row // GROUP) == (col // GROUP)
    return row, col, same


def gates_of(pos, logd, width):
    row, col, same = block_masks(width)
    lower = ((row >= col) & same).astype(F32)
    lb = jnp.broadcast_to(logd, (width, width))
    cum_t = mm(lower, lb)
    cum_i = mm(lb, lower, 0, 1)
    keep = ((row >= col) & same & (pos >= row - col)).astype(F32)
    decays = jnp.exp(jnp.minimum(cum_t - cum_i, 0.0)) * keep
    at = lax.broadcasted_iota(jnp.int32, (width, 1), 0) % GROUP
    carried = jnp.exp(cum_t[:, :1]) * (pos >= at + 1).astype(F32)
    strict = (row > col).astype(F32)
    return decays, carried, lower, strict


def unit_inverse(low):
    width = low.shape[0]
    row, col, same = block_masks(width)
    size = 1
    out = None
    while size < GROUP:
        join = (
            ((row // (2 * size)) == (col // (2 * size)))
            & ((row // size) % 2 == 1)
            & ((col // size) % 2 == 0)
        )
        part = jnp.where(join, low, 0.0)
        if out is None:
            out = (row == col).astype(F32) - part
        else:
            out = out - mm(mm(out, part), out)
        size *= 2
    return out


def final_of(decays, width):
    row, col, same = block_masks(width)
    last = ((col % GROUP) == GROUP - 1) & same
    pick = jnp.where((row % GROUP) == GROUP - 1, decays, 0.0)
    ones = jnp.ones((width, DK), F32)
    return mm(pick, ones, 0, 0)


def core_fwd_kernel(
    px_ref, taps_ref, par_ref, pos_ref, hg_ref,
    mixed_ref, state_ref, inv_ref, wr_ref, y_ref, qt_ref, m_ref, o_ref,
    n_ref,
):
    rows = px_ref.shape[0]
    width = min(4 * GROUP, rows)
    pos, x, conv, sig, qr, kr, rq, rk, q, k, v, beta, scale, shifted, logd = pre_stage(
        px_ref, taps_ref, par_ref, pos_ref
    )
    spans = [slice(i, i + width) for i in range(0, rows, width)]
    eye = (
        lax.broadcasted_iota(jnp.int32, (DK, DK), 0) == lax.broadcasted_iota(jnp.int32, (DK, DK), 1)
    ).astype(F32)
    us, pus = [], []
    for at in spans:
        decays, carried, lower, strict = gates_of(pos[at], logd[at], width)
        key_dots = mm(k[at], k[at], 1, 1)
        inv = unit_inverse(beta[at] * decays * key_dots * strict)
        inv_ref[at, :] = inv
        u = mm(inv, beta[at] * v[at])
        y = mm(inv, (beta[at] * carried) * k[at])
        p = decays * mm(q[at], k[at], 1, 1)
        qt = carried * q[at] - mm(p, y)
        pus.append(mm(p, u))
        us.append(u)
        y_ref[at, :] = y
        qt_ref[at, :] = qt
        kf = final_of(decays, width) * k[at]
        for j in range(width // GROUP):
            g = slice(j * GROUP, (j + 1) * GROUP)
            index = at.start // GROUP + j
            end = carried[(j + 1) * GROUP - 1 : (j + 1) * GROUP, :]
            m_ref[index] = end * eye - mm(kf[g], y[g], 0, 0)
            n_ref[index] = mm(kf[g], u[g], 0, 0)
    state = jnp.zeros((DK, DV), F32)
    for index in range(rows // GROUP):
        state_ref[index] = state
        if index + 1 < rows // GROUP:
            state = mm(m_ref[index], state) + n_ref[index]
    for index in range(rows // GROUP):
        g = slice(index * GROUP, (index + 1) * GROUP)
        inner = slice((index * GROUP) % width, (index * GROUP) % width + GROUP)
        state = state_ref[index]
        wr_ref[g, :] = us[index * GROUP // width][inner] - mm(y_ref[g, :], state)
        o_ref[g, :] = mm(qt_ref[g, :], state) + pus[index * GROUP // width][inner]
    out = o_ref[...]
    ro = lax.rsqrt(jnp.mean(out * out, -1, keepdims=True) + NORM_EPS)
    gate = px_ref[:, HEADC:HEADG]
    mixed_ref[...] = (out * ro * hg_ref[...] * (gate * jax.nn.sigmoid(gate))).astype(BF)


def core_bwd_kernel(
    px_ref, taps_ref, par_ref, pos_ref, hg_ref, dm_ref,
    state_ref, inv_ref, wr_ref, y_ref, qt_ref, m_ref, o_ref,
    dpx_ref, dtaps_ref, dhg_ref, dpar_ref,
    dst_ref, do_ref, dq_ref, dk_ref, dv_ref, db_ref, dg_ref,
):
    rows = px_ref.shape[0]
    width = min(4 * GROUP, rows)
    groups = rows // GROUP
    out = o_ref[...]
    ro = lax.rsqrt(jnp.mean(out * out, -1, keepdims=True) + NORM_EPS)
    on = out * ro
    gate = px_ref[:, HEADC:HEADG]
    sg = jax.nn.sigmoid(gate)
    dm = dm_ref[...]
    dpx_ref[:, HEADC:HEADG] = (dm * on * hg_ref[...] * (sg * (1.0 + gate * (1.0 - sg)))).astype(BF)
    dgained = dm * (gate * sg)
    dhg_ref[...] = jnp.sum(dgained * on, 0, keepdims=True)
    don = dgained * hg_ref[...]
    do_ref[...] = ro * (don - on * jnp.mean(don * on, -1, keepdims=True))

    pos, x, conv, sig, qr, kr, rq, rk, q, k, v, beta, scale, shifted, logd = pre_stage(
        px_ref, taps_ref, par_ref, pos_ref
    )
    back = jnp.zeros((DK, DV), F32)
    for index in reversed(range(groups)):
        g = slice(index * GROUP, (index + 1) * GROUP)
        dst_ref[index] = back
        if index:
            back = mm(m_ref[index], back, 0, 0) + mm(qt_ref[g, :], do_ref[g, :], 0, 0)
    for start in range(0, rows, width):
        at = slice(start, start + width)
        decays, carried, lower, strict = gates_of(pos[at], logd[at], width)
        qs, ks, vs, bs = q[at], k[at], v[at], beta[at]
        key_dots = mm(ks, ks, 1, 1)
        query_dots = mm(qs, ks, 1, 1)
        final = final_of(decays, width)
        kf = final * ks
        do = do_ref[at, :]
        w = wr_ref[at, :]
        inv = inv_ref[at, :]
        parts_w, parts_os, parts_kf, lasts = [], [], [], []
        for j in range(width // GROUP):
            g = slice(j * GROUP, (j + 1) * GROUP)
            index = start // GROUP + j
            parts_w.append(mm(kf[g], dst_ref[index]))
            parts_os.append(mm(do[g], state_ref[index], 1, 1))
            parts_kf.append(mm(w[g], dst_ref[index], 1, 1))
            lasts.append(
                jnp.sum(jnp.sum(dst_ref[index] * state_ref[index], -1, keepdims=True), 0, keepdims=True)
            )
        dw = mm(decays * query_dots, do, 0, 0) + jnp.concatenate(parts_w, 0)
        dtar = mm(inv, dw, 0, 0)
        dts = jnp.concatenate(
            [
                mm(dtar[j * GROUP : (j + 1) * GROUP], state_ref[start // GROUP + j], 1, 1)
                for j in range(width // GROUP)
            ],
            0,
        )
        dos = jnp.concatenate(parts_os, 0)
        dkf = jnp.concatenate(parts_kf, 0)
        dp = mm(do, w, 1, 1)
        dlow = -mm(dtar, w, 1, 1) * strict
        dqk = decays * dp
        low_dots = decays * key_dots * dlow
        dkk = bs * decays * dlow
        dq_ref[at, :] = mm(dqk, ks) + carried * dos
        k_dts = jnp.sum(ks * dts, -1, keepdims=True)
        dk_ref[at, :] = (
            mm(dqk, qs, 0, 0)
            + mm(dkk, ks)
            + mm(dkk, ks, 0, 0)
            - (bs * carried) * dts
            + final * dkf
        )
        dv_ref[at, :] = bs * dtar
        db_ref[at, :] = (
            jnp.sum(dtar * vs, -1, keepdims=True)
            - carried * k_dts
            + jnp.sum(low_dots, -1, keepdims=True)
        )
        dfinal = jnp.sum(dkf * ks, -1, keepdims=True)
        dcar = jnp.sum(qs * dos, -1, keepdims=True) - bs * k_dts
        pair = query_dots * dqk + bs * low_dots
        ones = jnp.ones((width, DK), F32)
        row_at = lax.broadcasted_iota(jnp.int32, (width, 1), 0)
        fin = dfinal * final[:, :1]
        dcum = (
            jnp.broadcast_to(jnp.sum(pair, -1, keepdims=True) + dcar * carried - fin, (width, DK))
            - mm(pair, ones, 0, 0)
        )
        for j in range(width // GROUP):
            g = slice(j * GROUP, (j + 1) * GROUP)
            e = (j + 1) * GROUP - 1
            gain = lasts[j] * carried[e : e + 1, :] + jnp.sum(fin[g], 0, keepdims=True)
            dcum = dcum + jnp.where(row_at == e, gain, 0.0)
        dg_ref[at, :] = mm(lower, dcum, 0, 0)[:, :1]

    dqn = dq_ref[...] * DK ** (-0.5)
    dkn = dk_ref[...]
    dqr = rq * (dqn - qr * (rq * rq) * jnp.sum(dqn * qr, -1, keepdims=True))
    dkr = rk * (dkn - kr * (rk * rk) * jnp.sum(dkn * kr, -1, keepdims=True))
    dact = jnp.concatenate([dqr, dkr, dv_ref[...]], -1)
    dconv = dact * (sig * (1.0 + conv * (1.0 - sig)))
    dx = dconv * taps_ref[CONV - 1 : CONV, :]
    dtaps_ref[CONV - 1 : CONV, :] = jnp.sum(dconv * x, 0, keepdims=True)
    for s in range(1, CONV):
        used = dconv * (pos >= s).astype(F32)
        dx = dx + taps_ref[CONV - 1 - s : CONV - s, :] * shift_rows(used, -s)
        dtaps_ref[CONV - 1 - s : CONV - s, :] = jnp.sum(used * shift_rows(x, s), 0, keepdims=True)
    dpx_ref[:, :HEADC] = dx.astype(BF)
    db = db_ref[...] * beta * (1.0 - beta)
    dg = dg_ref[...]
    da = dg * scale * jax.nn.sigmoid(shifted)
    lane = lax.broadcasted_iota(jnp.int32, (rows, EXTRA), 1)
    dpx_ref[:, HEADG:] = jnp.where(lane == 0, db, jnp.where(lane == 1, da, 0.0)).astype(BF)
    one = lax.broadcasted_iota(jnp.int32, (1, EXTRA), 1)
    dpar_ref[...] = jnp.where(
        one == 0,
        jnp.sum(dg * logd, 0, keepdims=True),
        jnp.where(one == 1, jnp.sum(da, 0, keepdims=True), 0.0),
    )


def vspec():
    return pl.BlockSpec(memory_space=pltpu.VMEM)


def core_fwd(px, taps, par, pos, gain):
    rows = px.shape[0]
    groups = rows // GROUP
    width = min(4 * GROUP, rows)
    shape = jax.ShapeDtypeStruct
    return pl.pallas_call(
        core_fwd_kernel,
        name="core_fwd",
        out_shape=(
            shape((rows, DV), BF),
            shape((groups, DK, DV), F32),
            shape((rows, width), F32),
            shape((rows, DV), F32),
            shape((rows, DK), F32),
            shape((rows, DK), F32),
            shape((groups, DK, DK), F32),
            shape((rows, DV), F32),
        ),
        in_specs=[vspec(), vspec(), pl.BlockSpec(memory_space=pltpu.SMEM), vspec(), vspec()],
        out_specs=tuple(vspec() for _ in range(8)),
        scratch_shapes=[pltpu.VMEM((groups, DK, DV), F32)],
        compiler_params=pltpu.CompilerParams(vmem_limit_bytes=48 << 20),
    )(px, taps, par, pos, gain)


def core_bwd(px, taps, par, pos, gain, dm, saved):
    rows = px.shape[0]
    groups = rows // GROUP
    shape = jax.ShapeDtypeStruct
    return pl.pallas_call(
        core_bwd_kernel,
        name="core_bwd",
        out_shape=(
            shape((rows, HEADG + EXTRA), BF),
            shape((CONV, HEADC), F32),
            shape((1, DV), F32),
            shape((1, EXTRA), F32),
        ),
        in_specs=[vspec(), vspec(), pl.BlockSpec(memory_space=pltpu.SMEM)]
        + [vspec() for _ in range(3 + len(saved))],
        out_specs=tuple(vspec() for _ in range(4)),
        scratch_shapes=[
            pltpu.VMEM((groups, DK, DV), F32),
            pltpu.VMEM((rows, DV), F32),
            pltpu.VMEM((rows, DK), F32),
            pltpu.VMEM((rows, DK), F32),
            pltpu.VMEM((rows, DV), F32),
            pltpu.VMEM((rows, 1), F32),
            pltpu.VMEM((rows, 1), F32),
        ],
        compiler_params=pltpu.CompilerParams(vmem_limit_bytes=48 << 20),
    )(px, taps, par, pos, gain, dm, *saved)


def swap(value, axis, mask):
    count = lax.axis_size(axis)
    return lax.ppermute(value, axis, [(i, i ^ mask) for i in range(count)])


def put(buffer, piece, index, axis):
    return lax.dynamic_update_slice_in_dim(buffer, jnp.expand_dims(piece, axis), index, axis)


def take(buffer, index, axis):
    return lax.dynamic_index_in_dim(buffer, index, axis, keepdims=False)


def bits_of(axis):
    count = lax.axis_size(axis)
    assert count & (count - 1) == 0
    masks = []
    mask = count // 2
    while mask:
        masks.append(mask)
        mask //= 2
    return masks


def near_pieces(value, axis):
    pieces = {0: value}
    for mask in bits_of(axis):
        for m in list(pieces):
            pieces[m ^ mask] = swap(pieces[m], axis, mask)
    return [pieces[m] for m in range(lax.axis_size(axis))]


def ordered(pieces, axis):
    me = lax.axis_index(axis)
    out = jnp.zeros((len(pieces),) + pieces[0].shape, pieces[0].dtype)
    for m, piece in enumerate(pieces):
        out = put(out, piece, me ^ m, 0)
    return out


def gather_rows(value, axis):
    out = ordered(near_pieces(value, axis), axis)
    return out.reshape((-1,) + value.shape[1:])


def reduce_rows(value, axis):
    me = lax.axis_index(axis)
    count = value.shape[0]
    part = value
    for mask in bits_of(axis):
        halves = part.reshape((2, -1) + value.shape[1:])
        bit = (me // mask) % 2
        away = swap(take(halves, 1 - bit, 0).astype(BF), axis, mask)
        part = take(halves, bit, 0).astype(F32) + away.astype(F32)
    return part[0]


def trade(value, axis):
    me = lax.axis_index(axis)
    pieces = [take(value, me, 0)]
    for m in range(1, value.shape[0]):
        pieces.append(swap(take(value, me ^ m, 0), axis, m))
    return ordered(pieces, axis)


def gather_far(value, axis):
    count = lax.axis_size(axis)
    k, r, w = value.shape
    if count > 8 or count < 4 or r % 32:
        return lax.all_gather(value, axis, axis=1, tiled=True)
    me = lax.axis_index(axis)
    far, near = me // 2, me % 2
    half = r // 2
    first, second = value[:, :half], value[:, half:]
    out = jnp.zeros((k, count // 2, 2, 2, half, w), value.dtype)

    def place(out, piece, f, n, h):
        piece = piece.reshape((k, piece.size // (k * half * w), 1, 1, half, w)) if piece.ndim == 4 else piece[:, None, None, None]
        return lax.dynamic_update_slice(out, piece, (0, f, n, h, 0, 0))

    column = jnp.zeros((k, count // 2, half, w), value.dtype)
    column = put(column, first, far, 1)
    other = swap(second, axis, 1)
    pair = put(put(jnp.zeros((k, 2, half, w), value.dtype), second, near, 1), other, 1 - near, 1)
    for m in range(1, count // 2):
        column = put(column, swap(first, axis, 2 * m), far ^ m, 1)
    beside = swap(column, axis, 1)
    zero = jnp.zeros_like(far)
    out = lax.dynamic_update_slice(out, column[:, :, None, None], (zero, zero, near, zero, zero, zero))
    out = lax.dynamic_update_slice(out, beside[:, :, None, None], (zero, zero, 1 - near, zero, zero, zero))
    one = zero + 1
    out = lax.dynamic_update_slice(out, pair[:, None, :, None], (zero, far, zero, one, zero, zero))
    for m in range(1, count // 2):
        got = swap(pair, axis, 2 * m)
        out = lax.dynamic_update_slice(out, got[:, None, :, None], (zero, far ^ m, zero, one, zero, zero))
    return out.reshape(k, count * r, w)


def reduce_far(value, axis):
    count = lax.axis_size(axis)
    k, rows, w = value.shape
    r = rows // count
    if count > 8 or count < 4 or r % 32:
        return lax.psum_scatter(value, axis, scatter_dimension=1, tiled=True).astype(F32)
    me = lax.axis_index(axis)
    far, near = me // 2, me % 2
    half = r // 2
    blocks = value.reshape(k, count // 2, 2, 2, half, w)
    first, second = blocks[:, :, :, 0], blocks[:, :, :, 1]
    got = swap(take(first, 1 - near, 2), axis, 1)
    column = take(first, near, 2).astype(F32) + got.astype(F32)
    pair = take(second, far, 1).astype(F32)
    for m in range(1, count // 2):
        pair = pair + swap(take(second, far ^ m, 1), axis, 2 * m).astype(F32)
    sent = column.astype(BF)
    total_a = take(column, far, 1)
    for m in range(1, count // 2):
        total_a = total_a + swap(take(sent, far ^ m, 1), axis, 2 * m).astype(F32)
    back = swap(take(pair, 1 - near, 1).astype(BF), axis, 1)
    total_b = take(pair, near, 1) + back.astype(F32)
    return jnp.concatenate([total_a, total_b], axis=1)


def sum_everywhere(value, axes):
    for axis in axes:
        count = lax.axis_size(axis)
        if count & (count - 1):
            value = lax.psum(value, axis)
            continue
        for mask in bits_of(axis):
            value = value + swap(value, axis, mask)
    return value


def doc_positions(lengths, count):
    ends = jnp.cumsum(lengths, axis=-1)
    starts = ends - lengths
    places = jnp.arange(count, dtype=jnp.int32)
    owner = jnp.max(jnp.where(starts[None, :] <= places[:, None], starts[None, :], 0), axis=-1)
    return places - owner


def adamw(weights, moment, square, grads):
    new_moment = beta_one * moment + (1.0 - beta_one) * grads
    new_square = beta_two * square + (1.0 - beta_two) * grads * grads
    corrected = new_moment / (1.0 - beta_one**STEP)
    scaled = new_square / (1.0 - beta_two**STEP)
    new_weights = weights - learn_rate * (
        corrected / (jnp.sqrt(scaled) + adam_eps) + weight_decay * weights
    )
    return (new_weights, new_moment, new_square)


def dot(a, b, lhs=1, rhs=0):
    return lax.dot_general(a, b, (((lhs,), (rhs,)), ((), ())), preferred_element_type=F32)


def local(
    activations, cotangent, live_slots, doc_lengths,
    inproj, mom_inproj, sqr_inproj,
    gateproj, mom_gateproj, sqr_gateproj,
    outproj, mom_outproj, sqr_outproj,
    mlp_gate, mom_mlp_gate, sqr_mlp_gate,
    mlp_up, mom_mlp_up, sqr_mlp_up,
    mlp_down, mom_mlp_down, sqr_mlp_down,
    vectors, mom_vectors, sqr_vectors,
    headvec, mom_headvec, sqr_headvec,
):
    n_ctx = lax.axis_size("ctx")
    me = lax.axis_index("ctx")
    assert n_ctx == H and activations.shape[0] == 1
    length = activations.shape[1]
    rows = inproj.shape[0]
    ff = mlp_gate.shape[1] // n_ctx
    per_row = vectors.shape[0] // rows
    vec_at = 2
    assert per_row * rows == vectors.shape[0] and vec_at + per_row <= EXTRA
    live = live_slots[0].astype(F32)
    act_own, cot_own = activations[0], cotangent[0]

    in_b = inproj.astype(BF)
    gp_b = gateproj.astype(BF)
    vec_b = vectors.astype(BF).reshape(rows, per_row)
    pad_b = jnp.zeros((rows, EXTRA - vec_at - per_row), BF)
    kq, vq, gq = H * DK, 2 * H * DK, 2 * H * DK + H * DV

    def in_slice(c):
        return jnp.concatenate(
            [
                in_b[:, c * DK : (c + 1) * DK],
                in_b[:, kq + c * DK : kq + (c + 1) * DK],
                in_b[:, vq + c * DV : vq + (c + 1) * DV],
                in_b[:, gq + c * DV : gq + (c + 1) * DV],
                gp_b[:, c : c + 1],
                gp_b[:, H + c : H + c + 1],
                vec_b,
                pad_b,
            ],
            axis=1,
        )

    w_in = trade(jnp.stack([in_slice(c) for c in range(n_ctx)]), "ctx").reshape(1, n_ctx * rows, -1)
    full_in = gather_far(w_in, "dp")[0]
    x_full = gather_rows(act_own, "ctx")
    out_t = outproj.T.astype(BF)
    w_out = trade(jnp.stack([out_t[:, c * DV : (c + 1) * DV] for c in range(n_ctx)]), "ctx")
    full_out = gather_far(w_out.reshape(1, n_ctx * rows, DV), "dp")[0]
    down_t = mlp_down.T
    w_mlp = jnp.stack(
        [
            jnp.stack([w[:, c * ff : (c + 1) * ff].astype(BF) for w in (mlp_gate, mlp_up, down_t)])
            for c in range(n_ctx)
        ]
    )
    w_mlp = jnp.swapaxes(trade(w_mlp, "ctx"), 0, 1).reshape(3, n_ctx * rows, ff)
    full_mlp = gather_far(w_mlp, "dp")
    full_wg, full_wu, full_wd = full_mlp[0], full_mlp[1], full_mlp[2]
    outs_near = near_pieces(full_out, "ctx")
    cot_full = gather_rows(cot_own, "ctx")

    vec_float = full_in[:, HEADG + vec_at : HEADG + vec_at + per_row].astype(F32).reshape(-1)
    norm_gain = vec_float[:D]
    taps_all = vec_float[D : D + CONV * CONVC].reshape(CONV, CONVC)
    mlp_gain = vec_float[D + CONV * CONVC :]
    head_gain = headvec[:DV]

    def my_taps(first, size):
        return lax.dynamic_slice_in_dim(taps_all, first + me * size, size, 1)

    taps = jnp.concatenate([my_taps(0, DK), my_taps(kq, DK), my_taps(vq, DV)], axis=1)
    par = jnp.stack(
        [
            lax.dynamic_index_in_dim(headvec, DV + me, 0, keepdims=False),
            lax.dynamic_index_in_dim(headvec, DV + H + me, 0, keepdims=False),
        ]
    )
    total = n_ctx * length
    pos = doc_positions(doc_lengths[0], total)[:, None]

    xf = x_full.astype(F32)
    inv_rms = lax.rsqrt(jnp.mean(xf * xf, -1, keepdims=True) + NORM_EPS)
    unit = xf * inv_rms
    normed = (unit * norm_gain).astype(BF)
    px = dot(normed, full_in)
    mixed, *saved = core_fwd(px, taps, par, pos, head_gain[None, :])
    branch = 0.0
    for piece, weight in zip(near_pieces(mixed, "ctx"), outs_near):
        branch = branch + dot(piece, weight, 1, 1)
    resid = xf + live * branch
    inv_two = lax.rsqrt(jnp.mean(resid * resid, -1, keepdims=True) + NORM_EPS)
    unit_two = resid * inv_two
    normed_two = (unit_two * mlp_gain).astype(BF)

    hgate = dot(normed_two, full_wg)
    hup = dot(normed_two, full_wu)
    sigma = jax.nn.sigmoid(hgate)
    silu_gate = hgate * sigma
    hidden = (silu_gate * hup).astype(BF)
    g_mlp = (cot_full.astype(F32) * live).astype(BF)
    d_hidden = dot(g_mlp, full_wd)
    d_hgate = (d_hidden * hup * sigma * (1.0 + hgate * (1.0 - sigma))).astype(BF)
    d_hup = (d_hidden * silu_gate).astype(BF)
    d_two = dot(d_hgate, full_wg, 1, 1) + dot(d_hup, full_wu, 1, 1)
    d_gain_two = jnp.sum(d_two * unit_two, axis=0)
    d_two_own = reduce_rows(d_two.astype(BF).reshape(n_ctx, length, D), "ctx")

    def own_rows(value):
        return lax.dynamic_slice_in_dim(value, me * length, length, 0)

    x_own = act_own.astype(F32)
    resid_own = own_rows(resid)
    inv_own = lax.rsqrt(jnp.mean(resid_own * resid_own, -1, keepdims=True) + NORM_EPS)
    unit_own = resid_own * inv_own
    d_unit_two = d_two_own * mlp_gain
    d_resid = cot_own.astype(F32) + inv_own * (
        d_unit_two - unit_own * jnp.mean(d_unit_two * unit_own, -1, keepdims=True)
    )
    g_own = (d_resid * live).astype(BF)
    g_branch = gather_rows(g_own, "ctx")

    mlp_part = dot(hidden, full_wd, 1, 1).astype(BF)
    mlp_own = reduce_rows(mlp_part.reshape(n_ctx, length, D), "ctx")
    block_out = (resid_own + live * mlp_own).astype(BF)

    grad_mlp = jnp.stack(
        [
            dot(normed_two, d_hgate, 0, 0).astype(BF),
            dot(normed_two, d_hup, 0, 0).astype(BF),
            dot(g_mlp, hidden, 0, 0).astype(BF),
        ]
    )

    d_mixed = dot(g_branch, full_out)
    grad_out = dot(g_branch, mixed, 0, 0).astype(BF)
    d_px, d_taps, d_hgain, d_par = core_bwd(px, taps, par, pos, head_gain[None, :], d_mixed, saved)
    d_normed = dot(d_px, full_in, 1, 1)
    d_gain = jnp.sum(d_normed * unit, axis=0)
    d_taps_all = jnp.zeros((CONV, CONVC), F32)
    for piece, first, size in (
        (d_taps[:, :DK], 0, DK),
        (d_taps[:, DK : 2 * DK], kq, DK),
        (d_taps[:, 2 * DK :], vq, DV),
    ):
        d_taps_all = lax.dynamic_update_slice(d_taps_all, piece, (0, first + me * size))
    grad_vec = jnp.concatenate([d_gain, d_taps_all.reshape(-1), d_gain_two]).reshape(-1, per_row)
    grad_in = dot(normed, d_px, 0, 0)
    grad_in = jnp.concatenate(
        [
            grad_in[:, : HEADG + vec_at],
            grad_vec,
            jnp.zeros((grad_in.shape[0], EXTRA - vec_at - per_row), F32),
        ],
        axis=1,
    ).astype(BF)

    def to_owner(value):
        part = reduce_far(value, "dp")
        k, _, w = part.shape
        part = jnp.swapaxes(part.reshape(k, n_ctx, rows, w), 0, 1).astype(BF)
        return trade(part, "ctx").astype(F32)

    own_mlp = to_owner(grad_mlp)
    own_out = to_owner(grad_out[None])[:, 0]
    own_in = to_owner(grad_in[None])[:, 0]

    def beside(value, first, size):
        return [value[c, :, first : first + size] for c in range(n_ctx)]

    owned_in = jnp.concatenate(
        beside(own_in, 0, DK) + beside(own_in, DK, DK) + beside(own_in, 2 * DK, DV) + beside(own_in, HEADC, DV),
        axis=1,
    )
    owned_ab = jnp.concatenate(beside(own_in, HEADG, 1) + beside(own_in, HEADG + 1, 1), axis=1)
    owned_vec = jnp.sum(own_in[:, :, HEADG + vec_at : HEADG + vec_at + per_row], axis=0).reshape(-1)
    owned_out = jnp.concatenate(beside(own_out, 0, DV), axis=1).T
    owned_wg, owned_wu, owned_wd_t = (
        jnp.concatenate([own_mlp[c, k] for c in range(n_ctx)], axis=1) for k in range(3)
    )
    owned_wd = owned_wd_t.T
    at_head = jnp.arange(H) == me
    grad_small = jnp.concatenate(
        [d_hgain[0], jnp.where(at_head, d_par[0, 0], 0.0), jnp.where(at_head, d_par[0, 1], 0.0)]
    )
    summed_small = sum_everywhere(grad_small, ("ctx", "dp"))

    d_normed_own = reduce_rows(d_normed.astype(BF).reshape(n_ctx, length, D), "ctx")
    inv_x = lax.rsqrt(jnp.mean(x_own * x_own, -1, keepdims=True) + NORM_EPS)
    unit_x = x_own * inv_x
    d_unit = d_normed_own * norm_gain
    input_grad = (
        d_resid + inv_x * (d_unit - unit_x * jnp.mean(d_unit * unit_x, -1, keepdims=True))
    ).astype(BF)

    n_in, nm_in, ns_in = adamw(inproj, mom_inproj, sqr_inproj, owned_in)
    n_ab, nm_ab, ns_ab = adamw(gateproj, mom_gateproj, sqr_gateproj, owned_ab)
    n_out, nm_out, ns_out = adamw(outproj, mom_outproj, sqr_outproj, owned_out)
    n_wg, nm_wg, ns_wg = adamw(mlp_gate, mom_mlp_gate, sqr_mlp_gate, owned_wg)
    n_wu, nm_wu, ns_wu = adamw(mlp_up, mom_mlp_up, sqr_mlp_up, owned_wu)
    n_wd, nm_wd, ns_wd = adamw(mlp_down, mom_mlp_down, sqr_mlp_down, owned_wd)
    n_vec, nm_vec, ns_vec = adamw(vectors, mom_vectors, sqr_vectors, owned_vec)
    n_small, nm_small, ns_small = adamw(headvec, mom_headvec, sqr_headvec, summed_small)
    return (
        block_out[None], input_grad[None],
        owned_in, owned_ab, owned_out, owned_wg, owned_wu, owned_wd, owned_vec, summed_small,
        n_in, nm_in, ns_in,
        n_ab, nm_ab, ns_ab,
        n_out, nm_out, ns_out,
        n_wg, nm_wg, ns_wg,
        n_wu, nm_wu, ns_wu,
        n_wd, nm_wd, ns_wd,
        n_vec, nm_vec, ns_vec,
        n_small, nm_small, ns_small,
    )


def solution(mesh):
    rows = P(("dp", "ctx"), None)
    cols = P(None, ("dp", "ctx"))
    flat = P(("dp", "ctx"))
    tokens = P("dp", "ctx", None)
    params = (rows,) * 6 + (cols,) * 3 + (rows,) * 6 + (cols,) * 3 + (flat,) * 3 + (P(),) * 3
    grads = (rows, rows, cols, rows, rows, cols, flat, P())
    return jax.shard_map(
        local,
        mesh=mesh,
        in_specs=(tokens, tokens, P("dp"), P("dp", None)) + params,
        out_specs=(tokens, tokens) + grads + params,
        check_vma=False,
    )
```

time: 1400 us -> 503 us (0.36)
  waiting for transfers between devices: 950 us -> 206 us
  blocking collectives: 126 us -> 0 us
  matrix products: 124 us -> 25.7 us
  starting transfers between devices: 23 us -> 117 us
  other arithmetic: 123 us -> 36.1 us
  local copies, waits for them, and re-layouts: 17.9 us -> 66.4 us
  Pallas kernels: 0 us -> 38.1 us
  between operations: 18.1 us -> 3.88 us
    reduce_scatter x5 -> x0, waiting for transfers between devices: 760 us -> none  [the longest x1 156 us: local(): lax.psum_scatter(grad_in, ('dp', 'ctx'), scatter_dimension=0, tiled=True)]
    ppermute x8 -> x92, waiting for transfers between devices: 10.7 us -> 206 us  [swap(): return lax.ppermute(value, axis, [(i, i ^ mask) for i in range(count)])]
    all_gather x5 -> x0, waiting for transfers between devices: 147 us -> none  [the longest x1 64.6 us: local(): lax.all_gather(mlp_down.astype(jnp.bfloat16), ('dp', 'ctx'), axis=1, tile...]
    ppermute x8 -> x92, starting transfers between devices: 22.4 us -> 117 us  [swap(): return lax.ppermute(value, axis, [(i, i ^ mask) for i in range(count)])]
    dot_general x64 -> x18, matrix products: 115 us -> 25.7 us  [dot(): lax.dot_general(a, b, (((lhs,), (rhs,)), ((), ())), preferred_element_typ...]
    unnamed x2 -> x0, blocking collectives: 84.2 us -> none
    another operation x16 -> x19, other arithmetic: 86.3 us -> 7.95 us  [the longest x9 81.9 us: group_step(): jax.scipy.linalg.solve_triangular(jnp.eye(width, dtype=jnp.float32) + low...]
    all_gather x1 -> x0, blocking collectives: 41.5 us -> none  [local(): lax.all_gather(gateproj.astype(jnp.bfloat16), ('dp', 'ctx'), axis=0, tile...]
  transfers between devices with their start and end apart: 19 -> 92, of which waited for: 12 -> 48; matrix products, arithmetic and copies ran while one was open for 14% -> 21% of each run, Pallas kernels for 0% -> 8%
where the time goes in v1:
time: 503 us; the launch traced here: 493 us
  waiting for transfers between devices  206 us (41%)
  starting transfers between devices  117 us (23%)
  local copies, waits for them, and re-layouts  66.4 us (13%)
  Pallas kernels  38.1 us (8%)
  other arithmetic  36.1 us (7%)
  matrix products  25.7 us (5%)
    ppermute x92, waiting for transfers between devices, swap(): return lax.ppermute(value, axis, [(i, i ^ mask) for i in range(count)])  206 us
    ppermute x92, starting transfers between devices, swap(): return lax.ppermute(value, axis, [(i, i ^ mask) for i in range(count)])  117 us
    dot_general x18, matrix products, dot(): lax.dot_general(a, b, (((lhs,), (rhs,)), ((), ())), preferred_element_typ...  25.7 us
    pallas_call x1, Pallas kernels, core_fwd(): pl.pallas_call(core_fwd_kernel, name='core_fwd', out_shape=(shape((rows,...  21.5 us
    pallas_call x1, Pallas kernels, core_bwd(): pl.pallas_call(core_bwd_kernel, name='core_bwd', out_shape=(shape((rows,...  16.7 us
  transfers between devices with their start and end apart: 92, of which 48 were waited for; matrix products, arithmetic and copies ran while one was open for 21% of the time, Pallas kernels for 8%

profile of v1, /device:TPU:0, one launch (start us, length us, event | category | flops | bytes accessed | tf_op | source)
XLA Modules:
  0.0 493.3 jit_solution(15155859231820728860)
XLA Ops:
  34.1 4.2 collective-permute-start.19
  50.3 3.7 collective-permute-done.5
  56.6 4.8 collective-permute-done.32
  61.6 5.8 %collective-permute-done.33 = bf16[3,32,704]{2,1,0:T(8,128)(2,1)S(1)} collective-permute-done((bf16[3,32,704]{2,1,0:T(8,128)(2,1)S(1)}, bf16[3,32,704]{2,1,0:T(8,128)(2,1)S(1)}, u32[]{:S(2)}, u32[]{:S(2)}) %collective-permute-start.33) | collective-permute-done | bytes 135200 | tf_op jit(solution)/shard_map/ppermute | solution.py:359
  75.1 5.2 %collective-permute-done.7 = bf16[1,64,896]{2,1,0:T(8,128)(2,1)S(1)} collective-permute-done((bf16[1,64,896]{2,1,0:T(8,128)(2,1)S(1)}, bf16[1,64,896]{2,1,0:T(8,128)(2,1)S(1)}, u32[]{:S(2)}, u32[]{:S(2)}) %collective-permute-start.7) | collective-permute-done | bytes 114720 | tf_op jit(solution)/shard_map/ppermute | solution.py:359
  80.3 3.5 collective-permute-start.8
  93.3 3.5 collective-permute-done.20
  106.9 3.9 collective-permute-start.24
  114.3 4.5 collective-permute-start.35
  125.0 4.5 collective-permute-done.34
  130.3 8.9 %collective-permute-done.35 = bf16[3,64,704]{2,1,0:T(8,128)(2,1)S(1)} collective-permute-done((bf16[3,64,704]{2,1,0:T(8,128)(2,1)S(1)}, bf16[3,64,704]{2,1,0:T(8,128)(2,1)S(1)}, u32[]{:S(2)}, u32[]{:S(2)}) %collective-permute-start.35) | collective-permute-done | bytes 270368 | tf_op jit(solution)/shard_map/ppermute | solution.py:359
  151.0 3.4 collective-permute-start.28
  157.4 8.9 %collective-permute-start.39 = (bf16[3,2,64,704]{3,2,1,0:T(8,128)(2,1)}, bf16[3,2,64,704]{3,2,1,0:T(8,128)(2,1)}, u32[]{:S(2)}, u32[]{:S(2)}) collective-permute-start(bf16[3,2,64,704]{3,2,1,0:T(8,128)(2,1)} %bitcast_dynamic-update-slice_fusion.8), channel_id=1, source_target_pairs={{0,8},{4,12},{8,0},{12,4},{16,24},{20,28},{24,16},{28,20},{1,9},{5... | collective-permute-start | bytes 1622024 | tf_op jit(solution)/shard_map/ppermute | solution.py:359
  170.9 21.5 %core_fwd.1 = (bf16[512,256]{1,0:T(8,128)(2,1)S(1)}, f32[8,128,256]{2,1,0:T(8,128)S(1)}, f32[512,256]{1,0:T(8,128)S(1)}, f32[512,256]{1,0:T(8,128)S(1)}, f32[512...) custom-call(f32[512,896]{1,0:T(8,128)S(1)} %fusion.83.px_ref, ...), custom_call_target="tpu_custom_call" | custom-call | tf_op jit(solution)/shard_map/core_fwd/pallas_call | solution.py:308
  194.8 5.8 %collective-permute-done.27 = bf16[512,256]{1,0:T(8,128)(2,1)S(1)} collective-permute-done((bf16[512,256]{1,0:T(8,128)(2,1)S(1)}, bf16[512,256]{1,0:T(8,128)(2,1)S(1)}, u32[]{:S(2)}, u32[]{:S(2)}) %collective-permute-start.27) | collective-permute-done | bytes 262176 | tf_op jit(solution)/shard_map/ppermute | solution.py:359
  214.5 29.6 %collective-permute-done.40 = bf16[3,2,64,704]{3,2,1,0:T(8,128)(2,1)S(1)} collective-permute-done((bf16[3,2,64,704]{3,2,1,0:T(8,128)(2,1)}, bf16[3,2,64,704]{3,2,1,0:T(8,128)(2,1)S(1)}, u32[]{:S(2)}, u32[]{:S(2)}) %collective-permute-start.40) | collective-permute-done | bytes 540704 | tf_op jit(solution)/shard_map/ppermute | solution.py:359
  277.2 12.3 %collective-permute-start.81 = (bf16[3,2,64,704]{3,2,1,0:T(8,128)(2,1)S(1)}, bf16[3,2,64,704]{3,2,1,0:T(8,128)(2,1)S(1)}, u32[]{:S(2)}, u32[]{:S(2)}) collective-permute-start(bf16[3,2,64,704]{3,2,1,0:T(8,128)(2,1)S(1)} %get-tuple-element.111), channel_id=1, source_target_pairs={{0,16},{4,20},{8,24},{12,28},{16,0},{20,4},{24,8},{28,12},{1,17},{... | collective-permute-start | bytes 1622024 | tf_op jit(solution)/shard_map/ppermute | solution.py:359
  293.7 36.4 %collective-permute-done.81 = bf16[3,2,64,704]{3,2,1,0:T(8,128)(2,1)S(1)} collective-permute-done((bf16[3,2,64,704]{3,2,1,0:T(8,128)(2,1)S(1)}, bf16[3,2,64,704]{3,2,1,0:T(8,128)(2,1)S(1)}, u32[]{:S(2)}, u32[]{:S(2)}) %collective-permute-start.81) | collective-permute-done | bytes 540704 | tf_op jit(solution)/shard_map/ppermute | solution.py:359
  333.6 5.8 %collective-permute-done.83 = bf16[3,64,704]{2,1,0:T(8,128)(2,1)S(1)} collective-permute-done((bf16[3,64,704]{2,1,0:T(8,128)(2,1)S(1)}, bf16[3,64,704]{2,1,0:T(8,128)(2,1)S(1)}, u32[]{:S(2)}, u32[]{:S(2)}) %collective-permute-start.83) | collective-permute-done | bytes 270368 | tf_op jit(solution)/shard_map/ppermute | solution.py:359
  352.2 16.7 %core_bwd.1 = (bf16[512,896]{1,0:T(8,128)(2,1)S(1)}, f32[4,512]{1,0:T(4,128)S(1)}, f32[1,256]{1,0:T(1,128)S(1)}, f32[1,128]{1,0:T(1,128)S(1)}) custom-call(f32[512,896]{1,0:T(8,128)} %copy-done, f32[4,512]{1,0:T(4,128)S(1)} %pad_maximum_fusion.8.taps_ref, f32[2]{0:T(128)S(1)} %pad_maximum_fusion.10.par_ref, s32[512,1]{1,0:T(8,128)S(1)} %iota_subtract_fusion.pos_ref, ...), custom_call_target="tpu_custom_call" | custom-call | tf_op jit(solution)/shard_map/core_bwd/pallas_call | solution.py:332
  381.3 3.6 collective-permute-done.87
  387.4 3.4 collective-permute-done.89
  391.0 3.3 collective-permute-done.90
  408.7 4.0 collective-permute-done.70
  415.9 3.2 collective-permute-start.67
  420.2 4.0 collective-permute-start.59
  426.1 5.6 %collective-permute-done.85 = bf16[3,32,704]{2,1,0:T(8,128)(2,1)S(1)} collective-permute-done((bf16[3,32,704]{2,1,0:T(8,128)(2,1)S(1)}, bf16[3,32,704]{2,1,0:T(8,128)(2,1)S(1)}, u32[]{:S(2)}, u32[]{:S(2)}) %collective-permute-start.85) | collective-permute-done | bytes 135200 | tf_op jit(solution)/shard_map/ppermute | solution.py:359
  431.7 5.7 %collective-permute-done.86 = bf16[3,32,704]{2,1,0:T(8,128)(2,1)S(1)} collective-permute-done((bf16[3,32,704]{2,1,0:T(8,128)(2,1)S(1)}, bf16[3,32,704]{2,1,0:T(8,128)(2,1)S(1)}, u32[]{:S(2)}, u32[]{:S(2)}) %collective-permute-start.86) | collective-permute-done | bytes 135200 | tf_op jit(solution)/shard_map/ppermute | solution.py:359
  442.6 3.3 multiply_subtract_fusion.2
  447.7 3.2 collective-permute-done.74
  458.3 9.9 %collective-permute-done.61 = bf16[1,64,896]{2,1,0:T(8,128)(2,1)S(1)} collective-permute-done((bf16[1,64,896]{2,1,0:T(8,128)(2,1)S(1)}, bf16[1,64,896]{2,1,0:T(8,128)(2,1)S(1)}, u32[]{:S(2)}, u32[]{:S(2)}) %collective-permute-start.61) | collective-permute-done | bytes 114720 | tf_op jit(solution)/shard_map/ppermute | solution.py:359
  476.4 4.6 collective-permute-done.56
  (579 shorter events, 243.0 us)
Async XLA Ops:
  0.7 113.6 %collective-permute-start = (bf16[128,1024]{1,0:T(8,128)(2,1)}, bf16[128,1024]{1,0:T(8,128)(2,1)}, u32[]{:S(2)}, u32[]{:S(2)}) collective-permute-start(bf16[128,1024]{1,0:T(8,128)(2,1)} %bitcast.607), channel_id=1, source_target_pairs={{0,1},{1,0},{2,3},{3,2},{4,5},{5,4},{6,7},{7,6},{8,9},{9,8},{10,11... | collective-permute-start | bytes 786440 | tf_op jit(solution)/shard_map/ppermute | solution.py:359
  1.3 118.5 %collective-permute-start.1 = (bf16[128,1024]{1,0:T(8,128)(2,1)}, bf16[128,1024]{1,0:T(8,128)(2,1)}, u32[]{:S(2)}, u32[]{:S(2)}) collective-permute-start(bf16[128,1024]{1,0:T(8,128)(2,1)} %bitcast.608), channel_id=1, source_target_pairs={{0,2},{1,3},{2,0},{3,1},{4,6},{5,7},{6,4},{7,5},{8,10},{9,11},{10,... | collective-permute-start | bytes 786440 | tf_op jit(solution)/shard_map/ppermute | solution.py:359
  3.9 117.0 %collective-permute-start.44 = (bf16[128,1024]{1,0:T(8,128)(2,1)}, bf16[128,1024]{1,0:T(8,128)(2,1)}, u32[]{:S(2)}, u32[]{:S(2)}) collective-permute-start(bf16[128,1024]{1,0:T(8,128)(2,1)} %bitcast.629), channel_id=1, source_target_pairs={{0,1},{1,0},{2,3},{3,2},{4,5},{5,4},{6,7},{7,6},{8,9},{9,8},{10,11... | collective-permute-start | bytes 786440 | tf_op jit(solution)/shard_map/ppermute | solution.py:359
  4.0 119.4 %collective-permute-start.45 = (bf16[128,1024]{1,0:T(8,128)(2,1)}, bf16[128,1024]{1,0:T(8,128)(2,1)}, u32[]{:S(2)}, u32[]{:S(2)}) collective-permute-start(bf16[128,1024]{1,0:T(8,128)(2,1)} %bitcast.630), channel_id=1, source_target_pairs={{0,2},{1,3},{2,0},{3,1},{4,6},{5,7},{6,4},{7,5},{8,10},{9,11},{10,... | collective-permute-start | bytes 786440 | tf_op jit(solution)/shard_map/ppermute | solution.py:359
  114.3 24.8 %collective-permute-start.35 = (bf16[3,64,704]{2,1,0:T(8,128)(2,1)S(1)}, bf16[3,64,704]{2,1,0:T(8,128)(2,1)S(1)}, u32[]{:S(2)}, u32[]{:S(2)}) collective-permute-start(bf16[3,64,704]{2,1,0:T(8,128)(2,1)S(1)} %get-tuple-element.143), channel_id=1, source_target_pairs={{0,16},{4,20},{8,24},{12,28},{16,0},{20,4},{24,8},{28,12},{1,17},{... | collective-permute-start | bytes 811016 | tf_op jit(solution)/shard_map/ppermute | solution.py:359
  119.8 20.1 %collective-permute-start.36 = (bf16[3,64,704]{2,1,0:T(8,128)(2,1)S(1)}, bf16[3,64,704]{2,1,0:T(8,128)(2,1)S(1)}, u32[]{:S(2)}, u32[]{:S(2)}) collective-permute-start(bf16[3,64,704]{2,1,0:T(8,128)(2,1)S(1)} %get-tuple-element.143), channel_id=1, source_target_pairs={{0,24},{4,28},{8,16},{12,20},{16,8},{20,12},{24,0},{28,4},{1,25},{... | collective-permute-start | bytes 811016 | tf_op jit(solution)/shard_map/ppermute | solution.py:359
  120.9 22.4 %collective-permute-start.38 = (bf16[3,64,704]{2,1,0:T(8,128)(2,1)S(1)}, bf16[3,64,704]{2,1,0:T(8,128)(2,1)S(1)}, u32[]{:S(2)}, u32[]{:S(2)}) collective-permute-start(bf16[3,64,704]{2,1,0:T(8,128)(2,1)S(1)} %get-tuple-element.142), channel_id=1, source_target_pairs={{0,4},{4,0},{8,12},{12,8},{16,20},{20,16},{24,28},{28,24},{1,5},{5... | collective-permute-start | bytes 811016 | tf_op jit(solution)/shard_map/ppermute | solution.py:359
  123.4 32.2 %collective-permute-start.9 = (bf16[1,4,64,896]{3,2,1,0:T(8,128)(2,1)S(1)}, bf16[1,4,64,896]{3,2,1,0:T(8,128)(2,1)S(1)}, u32[]{:S(2)}, u32[]{:S(2)}) collective-permute-start(bf16[1,4,64,896]{3,2,1,0:T(8,128)(2,1)S(1)} %bitcast_dynamic-update-slice_fusion.39), channel_id=1, source_target_pairs={{0,4},{4,0},{8,12},{12,8},{16,20},{20,16},{24,28},{28,24},{1,5},{5... | collective-permute-start | bytes 1376264 | tf_op jit(solution)/shard_map/ppermute | solution.py:359
  129.5 26.3 %collective-permute-start.11 = (bf16[1,2,64,896]{3,2,1,0:T(8,128)(2,1)S(1)}, bf16[1,2,64,896]{3,2,1,0:T(8,128)(2,1)S(1)}, u32[]{:S(2)}, u32[]{:S(2)}) collective-permute-start(bf16[1,2,64,896]{3,2,1,0:T(8,128)(2,1)S(1)} %bitcast_dynamic-update-slice_fusion.37), channel_id=1, source_target_pairs={{0,8},{4,12},{8,0},{12,4},{16,24},{20,28},{24,16},{28,20},{1,9},{5... | collective-permute-start | bytes 688136 | tf_op jit(solution)/shard_map/ppermute | solution.py:359
  139.2 18.2 %collective-permute-start.12 = (bf16[1,2,64,896]{3,2,1,0:T(8,128)(2,1)S(1)}, bf16[1,2,64,896]{3,2,1,0:T(8,128)(2,1)S(1)}, u32[]{:S(2)}, u32[]{:S(2)}) collective-permute-start(bf16[1,2,64,896]{3,2,1,0:T(8,128)(2,1)S(1)} %bitcast_dynamic-update-slice_fusion.37), channel_id=1, source_target_pairs={{0,16},{4,20},{8,24},{12,28},{16,0},{20,4},{24,8},{28,12},{1,17},{... | collective-permute-start | bytes 688136 | tf_op jit(solution)/shard_map/ppermute | solution.py:359
  139.9 26.4 %collective-permute-start.13 = (bf16[1,2,64,896]{3,2,1,0:T(8,128)(2,1)S(1)}, bf16[1,2,64,896]{3,2,1,0:T(8,128)(2,1)S(1)}, u32[]{:S(2)}, u32[]{:S(2)}) collective-permute-start(bf16[1,2,64,896]{3,2,1,0:T(8,128)(2,1)S(1)} %bitcast_dynamic-update-slice_fusion.37), channel_id=1, source_target_pairs={{0,24},{4,28},{8,16},{12,20},{16,8},{20,12},{24,0},{28,4},{1,25},{... | collective-permute-start | bytes 688136 | tf_op jit(solution)/shard_map/ppermute | solution.py:359
  151.0 43.7 %collective-permute-start.28 = (bf16[1024,256]{1,0:T(8,128)(2,1)}, bf16[1024,256]{1,0:T(8,128)(2,1)}, u32[]{:S(2)}, u32[]{:S(2)}) collective-permute-start(bf16[1024,256]{1,0:T(8,128)(2,1)} %bitcast.66), channel_id=1, source_target_pairs={{0,2},{1,3},{2,0},{3,1},{4,6},{5,7},{6,4},{7,5},{8,10},{9,11},{10,... | collective-permute-start | bytes 1572872 | tf_op jit(solution)/shard_map/ppermute | solution.py:359
  155.6 46.5 %collective-permute-start.26 = (bf16[1024,256]{1,0:T(8,128)(2,1)}, bf16[1024,256]{1,0:T(8,128)(2,1)}, u32[]{:S(2)}, u32[]{:S(2)}) collective-permute-start(bf16[1024,256]{1,0:T(8,128)(2,1)} %bitcast.66), channel_id=1, source_target_pairs={{0,1},{1,0},{2,3},{3,2},{4,5},{5,4},{6,7},{7,6},{8,9},{9,8},{10,11... | collective-permute-start | bytes 1572872 | tf_op jit(solution)/shard_map/ppermute | solution.py:359
  155.8 52.1 %collective-permute-start.37 = (bf16[3,4,64,704]{3,2,1,0:T(8,128)(2,1)}, bf16[3,4,64,704]{3,2,1,0:T(8,128)(2,1)}, u32[]{:S(2)}, u32[]{:S(2)}) collective-permute-start(bf16[3,4,64,704]{3,2,1,0:T(8,128)(2,1)} %bitcast_dynamic-update-slice_fusion.10), channel_id=1, source_target_pairs={{0,4},{4,0},{8,12},{12,8},{16,20},{20,16},{24,28},{28,24},{1,5},{5... | collective-permute-start | bytes 3244040 | tf_op jit(solution)/shard_map/ppermute | solution.py:359
  157.4 55.2 %collective-permute-start.39 = (bf16[3,2,64,704]{3,2,1,0:T(8,128)(2,1)}, bf16[3,2,64,704]{3,2,1,0:T(8,128)(2,1)}, u32[]{:S(2)}, u32[]{:S(2)}) collective-permute-start(bf16[3,2,64,704]{3,2,1,0:T(8,128)(2,1)} %bitcast_dynamic-update-slice_fusion.8), channel_id=1, source_target_pairs={{0,8},{4,12},{8,0},{12,4},{16,24},{20,28},{24,16},{28,20},{1,9},{5... | collective-permute-start | bytes 1622024 | tf_op jit(solution)/shard_map/ppermute | solution.py:359
  202.2 42.0 %collective-permute-start.40 = (bf16[3,2,64,704]{3,2,1,0:T(8,128)(2,1)}, bf16[3,2,64,704]{3,2,1,0:T(8,128)(2,1)S(1)}, u32[]{:S(2)}, u32[]{:S(2)}) collective-permute-start(bf16[3,2,64,704]{3,2,1,0:T(8,128)(2,1)} %bitcast_dynamic-update-slice_fusion.8), channel_id=1, source_target_pairs={{0,16},{4,20},{8,24},{12,28},{16,0},{20,4},{24,8},{28,12},{1,17},{... | collective-permute-start | bytes 1622024 | tf_op jit(solution)/shard_map/ppermute | solution.py:359
  204.3 40.7 %collective-permute-start.41 = (bf16[3,2,64,704]{3,2,1,0:T(8,128)(2,1)}, bf16[3,2,64,704]{3,2,1,0:T(8,128)(2,1)S(1)}, u32[]{:S(2)}, u32[]{:S(2)}) collective-permute-start(bf16[3,2,64,704]{3,2,1,0:T(8,128)(2,1)} %bitcast_dynamic-update-slice_fusion.8), channel_id=1, source_target_pairs={{0,24},{4,28},{8,16},{12,20},{16,8},{20,12},{24,0},{28,4},{1,25},{... | collective-permute-start | bytes 1622024 | tf_op jit(solution)/shard_map/ppermute | solution.py:359
  263.1 26.5 %collective-permute-start.47 = (bf16[2,128,1024]{2,1,0:T(8,128)(2,1)}, bf16[2,128,1024]{2,1,0:T(8,128)(2,1)}, u32[]{:S(2)}, u32[]{:S(2)}) collective-permute-start(bf16[2,128,1024]{2,1,0:T(8,128)(2,1)} %dynamic-slice_bitcast_fusion.5), channel_id=1, source_target_pairs={{0,2},{1,3},{2,0},{3,1},{4,6},{5,7},{6,4},{7,5},{8,10},{9,11},{10,... | collective-permute-start | bytes 1572872 | tf_op jit(solution)/shard_map/ppermute | solution.py:359
  264.2 27.2 %collective-permute-start.42 = (bf16[2,128,1024]{2,1,0:T(8,128)(2,1)}, bf16[2,128,1024]{2,1,0:T(8,128)(2,1)}, u32[]{:S(2)}, u32[]{:S(2)}) collective-permute-start(bf16[2,128,1024]{2,1,0:T(8,128)(2,1)} %dynamic-slice_bitcast_fusion.6), channel_id=1, source_target_pairs={{0,2},{1,3},{2,0},{3,1},{4,6},{5,7},{6,4},{7,5},{8,10},{9,11},{10,... | collective-permute-start | bytes 1572872 | tf_op jit(solution)/shard_map/ppermute | solution.py:359
  275.6 18.1 %collective-permute-start.82 = (bf16[3,2,64,704]{3,2,1,0:T(8,128)(2,1)S(1)}, bf16[3,2,64,704]{3,2,1,0:T(8,128)(2,1)S(1)}, u32[]{:S(2)}, u32[]{:S(2)}) collective-permute-start(bf16[3,2,64,704]{3,2,1,0:T(8,128)(2,1)S(1)} %get-tuple-element.110), channel_id=1, source_target_pairs={{0,24},{4,28},{8,16},{12,20},{16,8},{20,12},{24,0},{28,4},{1,25},{... | collective-permute-start | bytes 1622024 | tf_op jit(solution)/shard_map/ppermute | solution.py:359
  277.2 52.9 %collective-permute-start.81 = (bf16[3,2,64,704]{3,2,1,0:T(8,128)(2,1)S(1)}, bf16[3,2,64,704]{3,2,1,0:T(8,128)(2,1)S(1)}, u32[]{:S(2)}, u32[]{:S(2)}) collective-permute-start(bf16[3,2,64,704]{3,2,1,0:T(8,128)(2,1)S(1)} %get-tuple-element.111), channel_id=1, source_target_pairs={{0,16},{4,20},{8,24},{12,28},{16,0},{20,4},{24,8},{28,12},{1,17},{... | collective-permute-start | bytes 1622024 | tf_op jit(solution)/shard_map/ppermute | solution.py:359
  289.4 40.7 %collective-permute-start.80 = (bf16[3,2,64,704]{3,2,1,0:T(8,128)(2,1)S(1)}, bf16[3,2,64,704]{3,2,1,0:T(8,128)(2,1)S(1)}, u32[]{:S(2)}, u32[]{:S(2)}) collective-permute-start(bf16[3,2,64,704]{3,2,1,0:T(8,128)(2,1)S(1)} %get-tuple-element.109), channel_id=1, source_target_pairs={{0,8},{4,12},{8,0},{12,4},{16,24},{20,28},{24,16},{28,20},{1,9},{5... | collective-permute-start | bytes 1622024 | tf_op jit(solution)/shard_map/ppermute | solution.py:359
  289.6 52.5 %collective-permute-start.76 = (bf16[3,4,64,704]{3,2,1,0:T(8,128)(2,1)S(1)}, bf16[3,4,64,704]{3,2,1,0:T(8,128)(2,1)S(1)}, u32[]{:S(2)}, u32[]{:S(2)}) collective-permute-start(bf16[3,4,64,704]{3,2,1,0:T(8,128)(2,1)S(1)} %dynamic-slice_bitcast_fusion), channel_id=1, source_target_pairs={{0,4},{4,0},{8,12},{12,8},{16,20},{20,16},{24,28},{28,24},{1,5},{5... | collective-permute-start | bytes 3244040 | tf_op jit(solution)/shard_map/ppermute | solution.py:359
  291.5 39.6 %collective-permute-start.48 = (bf16[1,128,1024]{2,1,0:T(8,128)(2,1)S(1)}, bf16[1,128,1024]{2,1,0:T(8,128)(2,1)S(1)}, u32[]{:S(2)}, u32[]{:S(2)}) collective-permute-start(bf16[1,128,1024]{2,1,0:T(8,128)(2,1)S(1)} %dynamic-slice_convert_fusion.2), channel_id=1, source_target_pairs={{0,1},{1,0},{2,3},{3,2},{4,5},{5,4},{6,7},{7,6},{8,9},{9,8},{10,11... | collective-permute-start | bytes 786440 | tf_op jit(solution)/shard_map/ppermute | solution.py:359
  293.7 37.4 %collective-permute-start.43 = (bf16[1,128,1024]{2,1,0:T(8,128)(2,1)S(1)}, bf16[1,128,1024]{2,1,0:T(8,128)(2,1)S(1)}, u32[]{:S(2)}, u32[]{:S(2)}) collective-permute-start(bf16[1,128,1024]{2,1,0:T(8,128)(2,1)S(1)} %dynamic-slice_convert_fusion.3), channel_id=1, source_target_pairs={{0,1},{1,0},{2,3},{3,2},{4,5},{5,4},{6,7},{7,6},{8,9},{9,8},{10,11... | collective-permute-start | bytes 786440 | tf_op jit(solution)/shard_map/ppermute | solution.py:359
  344.8 55.2 %collective-permute-start.79 = (bf16[3,64,704]{2,1,0:T(8,128)(2,1)}, bf16[3,64,704]{2,1,0:T(8,128)(2,1)}, u32[]{:S(2)}, u32[]{:S(2)}) collective-permute-start(bf16[3,64,704]{2,1,0:T(8,128)(2,1)} %get-tuple-element.133), channel_id=1, source_target_pairs={{0,24},{4,28},{8,16},{12,20},{16,8},{20,12},{24,0},{28,4},{1,25},{... | collective-permute-start | bytes 811016 | tf_op jit(solution)/shard_map/ppermute | solution.py:359
  346.2 56.1 %collective-permute-start.78 = (bf16[3,64,704]{2,1,0:T(8,128)(2,1)}, bf16[3,64,704]{2,1,0:T(8,128)(2,1)}, u32[]{:S(2)}, u32[]{:S(2)}) collective-permute-start(bf16[3,64,704]{2,1,0:T(8,128)(2,1)} %get-tuple-element.134), channel_id=1, source_target_pairs={{0,16},{4,20},{8,24},{12,28},{16,0},{20,4},{24,8},{28,12},{1,17},{... | collective-permute-start | bytes 811016 | tf_op jit(solution)/shard_map/ppermute | solution.py:359
  346.2 56.1 %collective-permute-start.77 = (bf16[3,64,704]{2,1,0:T(8,128)(2,1)}, bf16[3,64,704]{2,1,0:T(8,128)(2,1)}, u32[]{:S(2)}, u32[]{:S(2)}) collective-permute-start(bf16[3,64,704]{2,1,0:T(8,128)(2,1)} %get-tuple-element.132), channel_id=1, source_target_pairs={{0,8},{4,12},{8,0},{12,4},{16,24},{20,28},{24,16},{28,20},{1,9},{5... | collective-permute-start | bytes 811016 | tf_op jit(solution)/shard_map/ppermute | solution.py:359
  371.1 101.8 %collective-permute-start.52 = (bf16[2,128,1024]{2,1,0:T(8,128)(2,1)}, bf16[2,128,1024]{2,1,0:T(8,128)(2,1)}, u32[]{:S(2)}, u32[]{:S(2)}) collective-permute-start(bf16[2,128,1024]{2,1,0:T(8,128)(2,1)} %dynamic-slice_bitcast_fusion.4), channel_id=1, source_target_pairs={{0,2},{1,3},{2,0},{3,1},{4,6},{5,7},{6,4},{7,5},{8,10},{9,11},{10,... | collective-permute-start | bytes 1572872 | tf_op jit(solution)/shard_map/ppermute | solution.py:359
  397.9 57.6 %collective-permute-start.60 = (bf16[1,2,64,896]{3,2,1,0:T(8,128)(2,1)}, bf16[1,2,64,896]{3,2,1,0:T(8,128)(2,1)}, u32[]{:S(2)}, u32[]{:S(2)}) collective-permute-start(bf16[1,2,64,896]{3,2,1,0:T(8,128)(2,1)} %get-tuple-element.137), channel_id=1, source_target_pairs={{0,24},{4,28},{8,16},{12,20},{16,8},{20,12},{24,0},{28,4},{1,25},{... | collective-permute-start | bytes 688136 | tf_op jit(solution)/shard_map/ppermute | solution.py:359
  420.2 35.3 %collective-permute-start.59 = (bf16[1,2,64,896]{3,2,1,0:T(8,128)(2,1)}, bf16[1,2,64,896]{3,2,1,0:T(8,128)(2,1)}, u32[]{:S(2)}, u32[]{:S(2)}) collective-permute-start(bf16[1,2,64,896]{3,2,1,0:T(8,128)(2,1)} %get-tuple-element.138), channel_id=1, source_target_pairs={{0,16},{4,20},{8,24},{12,28},{16,0},{20,4},{24,8},{28,12},{1,17},{... | collective-permute-start | bytes 688136 | tf_op jit(solution)/shard_map/ppermute | solution.py:359
  424.4 31.1 %collective-permute-start.58 = (bf16[1,2,64,896]{3,2,1,0:T(8,128)(2,1)}, bf16[1,2,64,896]{3,2,1,0:T(8,128)(2,1)}, u32[]{:S(2)}, u32[]{:S(2)}) collective-permute-start(bf16[1,2,64,896]{3,2,1,0:T(8,128)(2,1)} %get-tuple-element.136), channel_id=1, source_target_pairs={{0,8},{4,12},{8,0},{12,4},{16,24},{20,28},{24,16},{28,20},{1,9},{5... | collective-permute-start | bytes 688136 | tf_op jit(solution)/shard_map/ppermute | solution.py:359
  (139 other events, 1072.9 us)

commit v2 on v1

--- a/solution.py
+++ b/solution.py
@@ -354,6 +354,95 @@
     )(px, taps, par, pos, gain, dm, *saved)
 
 
+TILE = 256
+
+
+def mlp_grad_kernel(two_ref, cot_ref, dg_ref, du_ref, hid_ref, out_ref, turned_ref):
+    step = pl.program_id(0)
+    third = pl.num_programs(0) // 3
+
+    @pl.when(step == 0)
+    def _():
+        turned_ref[...] = two_ref[...].T
+
+    @pl.when(step == 2 * third)
+    def _():
+        turned_ref[...] = cot_ref[...].T
+
+    right = jnp.where(step < third, dg_ref[...], jnp.where(step < 2 * third, du_ref[...], hid_ref[...]))
+    out_ref[...] = lax.dot_general(
+        turned_ref[...], right, (((1,), (0,)), ((), ())), preferred_element_type=F32
+    ).astype(BF)
+
+
+def mlp_grad(two, cot, dg, du, hid):
+    rows, width = dg.shape
+    depth = two.shape[1]
+    third = width // TILE
+    whole = pl.BlockSpec((rows, depth), lambda i: (0, 0))
+
+    def tile(first):
+        return pl.BlockSpec((rows, TILE), lambda i: (0, jnp.clip(i - first, 0, third - 1)))
+
+    return pl.pallas_call(
+        mlp_grad_kernel,
+        name="mlp_grad",
+        grid=(3 * third,),
+        out_shape=jax.ShapeDtypeStruct((depth, 3 * width), BF),
+        in_specs=[whole, whole, tile(0), tile(third), tile(2 * third)],
+        out_specs=pl.BlockSpec((depth, TILE), lambda i: (0, i)),
+        scratch_shapes=[pltpu.VMEM((depth, rows), BF)],
+        compiler_params=pltpu.CompilerParams(vmem_limit_bytes=32 << 20),
+    )(two, cot, dg, du, hid)
+
+
+def mix_grad_kernel(norm_ref, dpx_ref, branch_ref, mixed_ref, vec_ref, out_ref, turned_ref):
+    step = pl.program_id(0)
+    first = (HEADG + EXTRA) // EXTRA
+
+    @pl.when(step == 0)
+    def _():
+        turned_ref[...] = norm_ref[...].T
+
+    @pl.when(step == first)
+    def _():
+        turned_ref[...] = branch_ref[...].T
+
+    right = jnp.where(step < first, dpx_ref[...], mixed_ref[...])
+    got = lax.dot_general(
+        turned_ref[...], right, (((1,), (0,)), ((), ())), preferred_element_type=F32
+    )
+    out_ref[...] = got.astype(BF)
+
+    @pl.when(step == first - 1)
+    def _():
+        lane = lax.broadcasted_iota(jnp.int32, got.shape, 1)
+        out_ref[...] = jnp.where(lane < EXTRA // 2, got, vec_ref[...]).astype(BF)
+
+
+def mix_grad(normed, dpx, branch, mixed, vec):
+    rows, depth = normed.shape
+    first = dpx.shape[1] // EXTRA
+    steps = first + mixed.shape[1] // EXTRA
+    whole = pl.BlockSpec((rows, depth), lambda i: (0, 0))
+    return pl.pallas_call(
+        mix_grad_kernel,
+        name="mix_grad",
+        grid=(steps,),
+        out_shape=jax.ShapeDtypeStruct((depth, steps * EXTRA), BF),
+        in_specs=[
+            whole,
+            pl.BlockSpec((rows, EXTRA), lambda i: (0, jnp.minimum(i, first - 1))),
+            whole,
+            pl.BlockSpec((rows, EXTRA), lambda i: (0, jnp.maximum(i - first, 0))),
+            pl.BlockSpec((depth, EXTRA), lambda i: (0, 0)),
+        ],
+        out_specs=pl.BlockSpec((depth, EXTRA), lambda i: (0, i)),
+        scratch_shapes=[pltpu.VMEM((depth, rows), BF)],
+        compiler_params=pltpu.CompilerParams(vmem_limit_bytes=32 << 20),
+    )(normed, dpx, branch, mixed, vec)
+
+
 def swap(value, axis, mask):
     count = lax.axis_size(axis)
     return lax.ppermute(value, axis, [(i, i ^ mask) for i in range(count)])
@@ -379,11 +468,12 @@
 
 
 def near_pieces(value, axis):
-    pieces = {0: value}
+    stack = value[None]
+    order = [0]
     for mask in bits_of(axis):
-        for m in list(pieces):
-            pieces[m ^ mask] = swap(pieces[m], axis, mask)
-    return [pieces[m] for m in range(lax.axis_size(axis))]
+        stack = jnp.concatenate([stack, swap(stack, axis, mask)], 0)
+        order = order + [m ^ mask for m in order]
+    return [stack[order.index(m)] for m in range(lax.axis_size(axis))]
 
 
 def ordered(pieces, axis):
@@ -401,22 +491,34 @@
 
 def reduce_rows(value, axis):
     me = lax.axis_index(axis)
-    count = value.shape[0]
     part = value
-    for mask in bits_of(axis):
-        halves = part.reshape((2, -1) + value.shape[1:])
+    for mask in reversed(bits_of(axis)):
+        pairs = part.reshape((-1, 2) + value.shape[1:])
         bit = (me // mask) % 2
-        away = swap(take(halves, 1 - bit, 0).astype(BF), axis, mask)
-        part = take(halves, bit, 0).astype(F32) + away.astype(F32)
+        away = swap(take(pairs, 1 - bit, 1).astype(BF), axis, mask)
+        part = take(pairs, bit, 1).astype(F32) + away.astype(F32)
     return part[0]
 
 
 def trade(value, axis):
     me = lax.axis_index(axis)
-    pieces = [take(value, me, 0)]
-    for m in range(1, value.shape[0]):
-        pieces.append(swap(take(value, me ^ m, 0), axis, m))
-    return ordered(pieces, axis)
+    count = value.shape[0]
+    held = value[:, None]
+    for mask in bits_of(axis):
+        halves = held.reshape((2, held.shape[0] // 2) + held.shape[1:])
+        bit = (me // mask) % 2
+        mine, away = take(halves, bit, 0), take(halves, 1 - bit, 0)
+        got = swap(away, axis, mask)
+        held = jnp.concatenate([mine, got], 1)
+    held = held[0]
+    out = jnp.zeros_like(held)
+    masks = bits_of(axis)
+    order = [0]
+    for mask in masks:
+        order = order + [m ^ mask for m in order]
+    for at, m in enumerate(order):
+        out = put(out, held[at], me ^ m, 0)
+    return out
 
 
 def gather_far(value, axis):
@@ -511,6 +613,22 @@
     return lax.dot_general(a, b, (((lhs,), (rhs,)), ((), ())), preferred_element_type=F32)
 
 
+def lines_of(flat, rows, half):
+    size = flat.shape[-1]
+    lead = flat.shape[:-1]
+    per = half if size <= rows * half and size % half == 0 else size // rows
+    assert size % per == 0 and size // per <= rows and per <= half
+    out = flat.reshape(lead + (size // per, per))
+    edge = [(0, 0)] * len(lead) + [(0, rows - size // per), (0, half - per)]
+    return jnp.pad(out, edge)
+
+
+def flat_of(block, size):
+    rows, half = block.shape[-2:]
+    per = half if size <= rows * half and size % half == 0 else size // rows
+    return block[:, : size // per, :per].reshape(-1)
+
+
 def local(
     activations, cotangent, live_slots, doc_lengths,
     inproj, mom_inproj, sqr_inproj,
@@ -528,16 +646,14 @@
     length = activations.shape[1]
     rows = inproj.shape[0]
     ff = mlp_gate.shape[1] // n_ctx
-    per_row = vectors.shape[0] // rows
-    vec_at = 2
-    assert per_row * rows == vectors.shape[0] and vec_at + per_row <= EXTRA
+    half = EXTRA // 2
     live = live_slots[0].astype(F32)
     act_own, cot_own = activations[0], cotangent[0]
 
     in_b = inproj.astype(BF)
     gp_b = gateproj.astype(BF)
-    vec_b = vectors.astype(BF).reshape(rows, per_row)
-    pad_b = jnp.zeros((rows, EXTRA - vec_at - per_row), BF)
+    vec_b = lines_of(vectors, rows, half).astype(BF)
+    pad_b = jnp.zeros((rows, half - 2), BF)
     kq, vq, gq = H * DK, 2 * H * DK, 2 * H * DK + H * DV
 
     def in_slice(c):
@@ -549,32 +665,41 @@
                 in_b[:, gq + c * DV : gq + (c + 1) * DV],
                 gp_b[:, c : c + 1],
                 gp_b[:, H + c : H + c + 1],
+                pad_b,
                 vec_b,
-                pad_b,
             ],
             axis=1,
         )
 
-    w_in = trade(jnp.stack([in_slice(c) for c in range(n_ctx)]), "ctx").reshape(1, n_ctx * rows, -1)
-    full_in = gather_far(w_in, "dp")[0]
-    x_full = gather_rows(act_own, "ctx")
     out_t = outproj.T.astype(BF)
-    w_out = trade(jnp.stack([out_t[:, c * DV : (c + 1) * DV] for c in range(n_ctx)]), "ctx")
-    full_out = gather_far(w_out.reshape(1, n_ctx * rows, DV), "dp")[0]
+    w_one = jnp.stack(
+        [jnp.concatenate([in_slice(c), out_t[:, c * DV : (c + 1) * DV]], axis=1) for c in range(n_ctx)]
+    )
+    w_one = trade(w_one, "ctx").reshape(1, n_ctx * rows, -1)
+    full_one = gather_far(w_one, "dp")[0]
+    full_in, full_out = full_one[:, : HEADG + EXTRA], full_one[:, HEADG + EXTRA :]
+    tokens = jnp.concatenate([act_own, cot_own], axis=1)
+    tokens = gather_rows(tokens, "ctx")
+    x_full, cot_full = tokens[:, :D], tokens[:, D:]
+    ff_pad = -(-ff // 256) * 256
+    fill = jnp.zeros((rows, ff_pad - ff), BF)
     down_t = mlp_down.T
     w_mlp = jnp.stack(
         [
-            jnp.stack([w[:, c * ff : (c + 1) * ff].astype(BF) for w in (mlp_gate, mlp_up, down_t)])
+            jnp.concatenate(
+                sum(([w[:, c * ff : (c + 1) * ff].astype(BF), fill] for w in (mlp_gate, mlp_up, down_t)), []),
+                axis=1,
+            )
             for c in range(n_ctx)
         ]
     )
-    w_mlp = jnp.swapaxes(trade(w_mlp, "ctx"), 0, 1).reshape(3, n_ctx * rows, ff)
-    full_mlp = gather_far(w_mlp, "dp")
-    full_wg, full_wu, full_wd = full_mlp[0], full_mlp[1], full_mlp[2]
+    w_mlp = trade(w_mlp, "ctx").reshape(n_ctx * rows, 3 * ff_pad)
+    full_mlp = lax.all_gather(w_mlp, "dp", axis=0, tiled=True)
+    full_wg, full_wu, full_wd = (full_mlp[:, k * ff_pad : (k + 1) * ff_pad] for k in range(3))
     outs_near = near_pieces(full_out, "ctx")
-    cot_full = gather_rows(cot_own, "ctx")
-
-    vec_float = full_in[:, HEADG + vec_at : HEADG + vec_at + per_row].astype(F32).reshape(-1)
+
+    share = vectors.shape[0]
+    vec_float = flat_of(full_in[:, HEADG + half :].astype(F32).reshape(-1, rows, half), share)
     norm_gain = vec_float[:D]
     taps_all = vec_float[D : D + CONV * CONVC].reshape(CONV, CONVC)
     mlp_gain = vec_float[D + CONV * CONVC :]
@@ -618,36 +743,35 @@
     d_hup = (d_hidden * silu_gate).astype(BF)
     d_two = dot(d_hgate, full_wg, 1, 1) + dot(d_hup, full_wu, 1, 1)
     d_gain_two = jnp.sum(d_two * unit_two, axis=0)
-    d_two_own = reduce_rows(d_two.astype(BF).reshape(n_ctx, length, D), "ctx")
-
-    def own_rows(value):
-        return lax.dynamic_slice_in_dim(value, me * length, length, 0)
-
+    low, high = me % 2, me // 2
+    grid = (2, 2, length, D)
+    pairs = d_two.astype(BF).reshape(grid)
+    got = swap(take(pairs, 1 - low, 1), "ctx", 1)
+    column = take(pairs, low, 1).astype(F32) + got.astype(F32)
+    d_two_col = column + swap(column.astype(BF), "ctx", 2).astype(F32)
+    resid_col = take(resid.reshape(grid), low, 1)
+    cot_col = take(cot_full.reshape(grid), low, 1).astype(F32)
+    inv_col = lax.rsqrt(jnp.mean(resid_col * resid_col, -1, keepdims=True) + NORM_EPS)
+    unit_col = resid_col * inv_col
+    d_unit_two = d_two_col * mlp_gain
+    d_resid_col = cot_col + inv_col * (
+        d_unit_two - unit_col * jnp.mean(d_unit_two * unit_col, -1, keepdims=True)
+    )
+    g_col = (d_resid_col * live).astype(BF)
+    g_other = swap(g_col, "ctx", 1)
+    g_branch = put(put(jnp.zeros(grid, BF), g_col, low, 1), g_other, 1 - low, 1)
+    g_branch = g_branch.reshape(-1, D)
+    d_resid = take(d_resid_col, high, 0)
+    resid_own = take(resid_col, high, 0)
     x_own = act_own.astype(F32)
-    resid_own = own_rows(resid)
-    inv_own = lax.rsqrt(jnp.mean(resid_own * resid_own, -1, keepdims=True) + NORM_EPS)
-    unit_own = resid_own * inv_own
-    d_unit_two = d_two_own * mlp_gain
-    d_resid = cot_own.astype(F32) + inv_own * (
-        d_unit_two - unit_own * jnp.mean(d_unit_two * unit_own, -1, keepdims=True)
-    )
-    g_own = (d_resid * live).astype(BF)
-    g_branch = gather_rows(g_own, "ctx")
-
+
+    grad_mlp = mlp_grad(normed_two, g_mlp, d_hgate, d_hup, hidden)
     mlp_part = dot(hidden, full_wd, 1, 1).astype(BF)
+    mlp_part, g_branch = lax.optimization_barrier((mlp_part, g_branch))
     mlp_own = reduce_rows(mlp_part.reshape(n_ctx, length, D), "ctx")
     block_out = (resid_own + live * mlp_own).astype(BF)
 
-    grad_mlp = jnp.stack(
-        [
-            dot(normed_two, d_hgate, 0, 0).astype(BF),
-            dot(normed_two, d_hup, 0, 0).astype(BF),
-            dot(g_mlp, hidden, 0, 0).astype(BF),
-        ]
-    )
-
     d_mixed = dot(g_branch, full_out)
-    grad_out = dot(g_branch, mixed, 0, 0).astype(BF)
     d_px, d_taps, d_hgain, d_par = core_bwd(px, taps, par, pos, head_gain[None, :], d_mixed, saved)
     d_normed = dot(d_px, full_in, 1, 1)
     d_gain = jnp.sum(d_normed * unit, axis=0)
@@ -658,26 +782,16 @@
         (d_taps[:, 2 * DK :], vq, DV),
     ):
         d_taps_all = lax.dynamic_update_slice(d_taps_all, piece, (0, first + me * size))
-    grad_vec = jnp.concatenate([d_gain, d_taps_all.reshape(-1), d_gain_two]).reshape(-1, per_row)
-    grad_in = dot(normed, d_px, 0, 0)
-    grad_in = jnp.concatenate(
-        [
-            grad_in[:, : HEADG + vec_at],
-            grad_vec,
-            jnp.zeros((grad_in.shape[0], EXTRA - vec_at - per_row), F32),
-        ],
-        axis=1,
-    ).astype(BF)
-
-    def to_owner(value):
-        part = reduce_far(value, "dp")
-        k, _, w = part.shape
-        part = jnp.swapaxes(part.reshape(k, n_ctx, rows, w), 0, 1).astype(BF)
-        return trade(part, "ctx").astype(F32)
-
-    own_mlp = to_owner(grad_mlp)
-    own_out = to_owner(grad_out[None])[:, 0]
-    own_in = to_owner(grad_in[None])[:, 0]
+    grad_vec = jnp.concatenate([d_gain, d_taps_all.reshape(-1), d_gain_two]).reshape(-1, share)
+    grad_vec = jnp.pad(lines_of(grad_vec, rows, half), ((0, 0), (0, 0), (half, 0)))
+    grad_one = mix_grad(normed, d_px, g_branch, mixed, grad_vec.reshape(-1, EXTRA))
+
+    def to_owner(part):
+        return trade(part.reshape(n_ctx, rows, -1).astype(BF), "ctx").astype(F32)
+
+    own_mlp = to_owner(lax.psum_scatter(grad_mlp, "dp", scatter_dimension=0, tiled=True))
+    own_one = to_owner(reduce_far(grad_one[None], "dp")[0])
+    own_in, own_out = own_one[:, :, : HEADG + EXTRA], own_one[:, :, HEADG + EXTRA :]
 
     def beside(value, first, size):
         return [value[c, :, first : first + size] for c in range(n_ctx)]
@@ -687,10 +801,10 @@
         axis=1,
     )
     owned_ab = jnp.concatenate(beside(own_in, HEADG, 1) + beside(own_in, HEADG + 1, 1), axis=1)
-    owned_vec = jnp.sum(own_in[:, :, HEADG + vec_at : HEADG + vec_at + per_row], axis=0).reshape(-1)
+    owned_vec = flat_of(jnp.sum(own_in[:, :, HEADG + half :], axis=0)[None], share)
     owned_out = jnp.concatenate(beside(own_out, 0, DV), axis=1).T
     owned_wg, owned_wu, owned_wd_t = (
-        jnp.concatenate([own_mlp[c, k] for c in range(n_ctx)], axis=1) for k in range(3)
+        jnp.concatenate(beside(own_mlp, k * ff_pad, ff), axis=1) for k in range(3)
     )
     owned_wd = owned_wd_t.T
     at_head = jnp.arange(H) == me

time: 503 us -> 358 us (0.71)
  waiting for transfers between devices: 206 us -> 131 us
  starting transfers between devices: 117 us -> 54.9 us
  local copies, waits for them, and re-layouts: 66.4 us -> 44.5 us
  between operations: 3.88 us -> 16.9 us
  Pallas kernels: 38.1 us -> 48.6 us
    ppermute x92 -> x42, waiting for transfers between devices: 206 us -> 123 us  [swap(): return lax.ppermute(value, axis, [(i, i ^ mask) for i in range(count)])]
    ppermute x92 -> x42, starting transfers between devices: 117 us -> 54.6 us  [swap(): return lax.ppermute(value, axis, [(i, i ^ mask) for i in range(count)])]
    pallas_call x0 -> x2, Pallas kernels: none -> 10.9 us  [the longest x1 5.54 us: mix_grad(): pl.pallas_call(mix_grad_kernel, name='mix_grad', grid=(steps,), out_shape...]
    unnamed x175 -> x171, local copies, waits for them, and re-layouts: 3.32 us -> 11.9 us
    all_gather x0 -> x1, waiting for transfers between devices: none -> 8.09 us  [local(): full_mlp = lax.all_gather(w_mlp, 'dp', axis=0, tiled=True)]
    convert_element_type x6 -> x2, local copies, waits for them, and re-layouts: 7.66 us -> 0.08 us  [reduce_rows(): away = swap(take(pairs, 1 - bit, 1).astype(BF), axis, mask)]
    another operation x18 -> x9, other arithmetic: 6.59 us -> 1.15 us
    dot_general x18 -> x13, matrix products: 25.7 us -> 25 us  [dot(): lax.dot_general(a, b, (((lhs,), (rhs,)), ((), ())), preferred_element_typ...]
  transfers between devices with their start and end apart: 92 -> 44, of which waited for: 48 -> 21; matrix products, arithmetic and copies ran while one was open for 21% -> 19% of each run, Pallas kernels for 8% -> 14%
where the time goes in v2:
time: 358 us; the launch traced here: 353 us
  waiting for transfers between devices  131 us (37%)
  starting transfers between devices  54.9 us (15%)
  Pallas kernels  48.6 us (14%)
  local copies, waits for them, and re-layouts  44.5 us (12%)
  other arithmetic  32.1 us (9%)
  matrix products  25 us (7%)
  between operations  16.9 us (5%)
    ppermute x42, waiting for transfers between devices, swap(): return lax.ppermute(value, axis, [(i, i ^ mask) for i in range(count)])  123 us
    ppermute x42, starting transfers between devices, swap(): return lax.ppermute(value, axis, [(i, i ^ mask) for i in range(count)])  54.6 us
    dot_general x13, matrix products, dot(): lax.dot_general(a, b, (((lhs,), (rhs,)), ((), ())), preferred_element_typ...  25 us
    pallas_call x1, Pallas kernels, core_fwd(): pl.pallas_call(core_fwd_kernel, name='core_fwd', out_shape=(shape((rows,...  21.2 us
    pallas_call x1, Pallas kernels, core_bwd(): pl.pallas_call(core_bwd_kernel, name='core_bwd', out_shape=(shape((rows,...  16.5 us
    unnamed x171, local copies, waits for them, and re-layouts  11.9 us
    all_gather x1, waiting for transfers between devices, local(): full_mlp = lax.all_gather(w_mlp, 'dp', axis=0, tiled=True)  8.09 us
    sub x7, other arithmetic, adamw(): weights - learn_rate * (corrected / (jnp.sqrt(scaled) + adam_eps) + weigh...  7.97 us
  transfers between devices with their start and end apart: 44, of which 21 were waited for; matrix products, arithmetic and copies ran while one was open for 19% of the time, Pallas kernels for 14%

profile of v2, /device:TPU:0, one launch (start us, length us, event | category | flops | bytes accessed | tf_op | source)
XLA Modules:
  0.0 353.1 jit_solution(6013554511913999098)
XLA Ops:
  12.3 3.0 collective-permute-start.2
  26.6 2.6 collective-permute-start.5
  29.4 7.6 %collective-permute-done.16 = bf16[2,1,32,2304]{3,2,1,0:T(8,128)(2,1)} collective-permute-done((bf16[2,1,32,2304]{3,2,1,0:T(8,128)(2,1)}, bf16[2,1,32,2304]{3,2,1,0:T(8,128)(2,1)}, u32[]{:S(2)}, u32[]{:S(2)}) %collective-permute-start.16) | collective-permute-done | bytes 294944 | tf_op jit(solution)/shard_map/ppermute | solution.py:448
  44.6 2.7 collective-permute-start.10
  53.0 2.3 pad_maximum_fusion
  55.3 7.4 %collective-permute-done.7 = bf16[1,4,64,1152]{3,2,1,0:T(8,128)(2,1)} collective-permute-done((bf16[1,4,64,1152]{3,2,1,0:T(8,128)(2,1)S(1)}, bf16[1,4,64,1152]{3,2,1,0:T(8,128)(2,1)}, u32[]{:S(2)}, u32[]{:S(2)}) %collective-permute-start.7) | collective-permute-done | bytes 589856 | tf_op jit(solution)/shard_map/ppermute | solution.py:448
  68.0 3.8 %collective-permute-done.10 = bf16[1,2,64,1152]{3,2,1,0:T(8,128)(2,1)} collective-permute-done((bf16[1,2,64,1152]{3,2,1,0:T(8,128)(2,1)}, bf16[1,2,64,1152]{3,2,1,0:T(8,128)(2,1)}, u32[]{:S(2)}, u32[]{:S(2)}) %collective-permute-start.10) | collective-permute-done | bytes 294944 | tf_op jit(solution)/shard_map/ppermute | solution.py:448
  81.3 5.4 %collective-permute-done.14 = bf16[1,1024,256]{2,1,0:T(8,128)(2,1)S(1)} collective-permute-done((bf16[1,1024,256]{2,1,0:T(8,128)(2,1)S(1)}, bf16[1,1024,256]{2,1,0:T(8,128)(2,1)S(1)}, u32[]{:S(2)}, u32[]{:S(2)}) %collective-permute-start.14) | collective-permute-done | bytes 524320 | tf_op jit(solution)/shard_map/ppermute | solution.py:448
  93.6 3.1 fusion.7.px_ref
  96.7 21.2 %core_fwd.1 = (bf16[512,256]{1,0:T(8,128)(2,1)S(1)}, f32[8,128,256]{2,1,0:T(8,128)S(1)}, f32[512,256]{1,0:T(8,128)S(1)}, f32[512,256]{1,0:T(8,128)S(1)}, f32[512...) custom-call(f32[512,896]{1,0:T(8,128)S(1)} %fusion.7.px_ref, ...), custom_call_target="tpu_custom_call" | custom-call | tf_op jit(solution)/shard_map/core_fwd/pallas_call | solution.py:308
  119.6 7.2 %collective-permute-done.12 = bf16[1,512,256]{2,1,0:T(8,128)(2,1)S(1)} collective-permute-done((bf16[1,512,256]{2,1,0:T(8,128)(2,1)S(1)}, bf16[1,512,256]{2,1,0:T(8,128)(2,1)S(1)}, u32[]{:S(2)}, u32[]{:S(2)}) %collective-permute-start.12) | collective-permute-done | bytes 262176 | tf_op jit(solution)/shard_map/ppermute | solution.py:448
  134.2 8.1 %all-gather.2.cloned.1.call-done = bf16[1024,2304]{1,0:T(8,128)(2,1)} async-done(((bf16[128,2304]{1,0:T(8,128)(2,1)}), bf16[1024,2304]{1,0:T(8,128)(2,1)}) %all-gather.2.cloned.1.call-update) | async-done | bytes 4718608 | tf_op jit(solution)/shard_map/all_gather | solution.py:697
  142.3 2.5 fusion.18
  146.1 2.4 multiply_convert_fusion.2
  158.7 10.1 %collective-permute-done.19 = bf16[2,128,1024]{2,1,0:T(8,128)(2,1)} collective-permute-done((bf16[2,128,1024]{2,1,0:T(8,128)(2,1)}, bf16[2,128,1024]{2,1,0:T(8,128)(2,1)}, u32[]{:S(2)}, u32[]{:S(2)}) %collective-permute-start.19) | collective-permute-done | bytes 524320 | tf_op jit(solution)/shard_map/ppermute | solution.py:448
  170.6 2.9 bitcast_dynamic-update-slice_fusion.3
  174.5 5.4 %mlp_grad.1 = bf16[1024,2304]{1,0:T(8,128)(2,1)S(1)} custom-call(bf16[512,1024]{1,0:T(8,128)(2,1)S(1)} %multiply_convert_fusion.1.two_ref, bf16[512,1024]{1,0:T(8,128)(2,1)S(1)} %get-tuple-element.110.cot_ref, bf16[512,768]{1,0:T(8,128)(2,1)S(1)} %copy-done.13, bf16[512,768]{1,0:T(8,128)(2,1)S(1)} %get-tuple-element.101.du_ref, bf16[512,768]{1,0:T(8,128)(2,1)S(1)} %copy-done.10), custom_call_target="tpu_custom_call" | custom-call | tf_op jit(solution)/shard_map/mlp_grad/pallas_call | solution.py:387
  183.2 2.5 convolution_convert_fusion
  189.7 16.5 %core_bwd.1 = (bf16[512,896]{1,0:T(8,128)(2,1)S(1)}, f32[4,512]{1,0:T(4,128)S(1)}, f32[1,256]{1,0:T(1,128)S(1)}, f32[1,128]{1,0:T(1,128)S(1)}) custom-call(f32[512,896]{1,0:T(8,128)} %copy-done.1, f32[4,512]{1,0:T(4,128)S(1)} %pad_maximum_fusion.7.taps_ref, f32[2]{0:T(128)S(1)} %pad_maximum_fusion.9.par_ref, s32[512,1]{1,0:T(8,128)S(1)} %iota_subtract_fusion.pos_ref, ...), custom_call_target="tpu_custom_call" | custom-call | tf_op jit(solution)/shard_map/core_bwd/pallas_call | solution.py:332
  206.3 4.2 %fusion.3 = (f32[1024]{0:T(1024)S(1)}, bf16[512,1024]{1,0:T(8,128)(2,1)}) fusion(f32[512]{0:T(512)S(1)} %add_rsqrt_fusion.1, bf16[512,2048]{1,0:T(8,128)(2,1)S(1)} %bitcast.424, bf16[512,896]{1,0:T(8,128)(2,1)S(1)} %get-tuple-element.58.dpx_ref, bf16[1024,1152]{1,0:T(8,128)(2,1)} %bitcast.36), kind=kOutput, calls=%fused_computation.6 | convolution fusion | flops 942144512 | bytes 4855808 | tf_op jit(solution)/shard_map/dot_general | solution.py:613
  211.9 5.5 %mix_grad.1 = bf16[1024,1152]{1,0:T(8,128)(2,1)S(1)} custom-call(bf16[512,1024]{1,0:T(8,128)(2,1)S(1)} %copy-done.3, bf16[512,896]{1,0:T(8,128)(2,1)S(1)} %copy-done.9, bf16[512,1024]{1,0:T(8,128)(2,1)S(1)} %bitcast.408, bf16[512,256]{1,0:T(8,128)(2,1)S(1)} %get-tuple-element.48.mixed_ref, f32[1024,128]{1,0:T(8,128)S(1)} %bitcast.411), custom_call_target="tpu_custom_call" | custom-call | tf_op jit(solution)/shard_map/mix_grad/pallas_call | solution.py:428
  224.9 12.4 %collective-permute-start.30 = (bf16[1,2,64,1152]{3,2,1,0:T(8,128)(2,1)S(1)}, bf16[1,2,64,1152]{3,2,1,0:T(8,128)(2,1)S(1)}, u32[]{:S(2)}, u32[]{:S(2)}) collective-permute-start(bf16[1,2,64,1152]{3,2,1,0:T(8,128)(2,1)S(1)} %get-tuple-element.126), channel_id=1, source_target_pairs={{0,16},{4,20},{8,24},{12,28},{16,0},{20,4},{24,8},{28,12},{1,17},{... | collective-permute-start | bytes 884744 | tf_op jit(solution)/shard_map/ppermute | solution.py:448
  237.9 2.9 collective-permute-start.39
  240.9 26.3 %collective-permute-done.39 = f32[264]{0:T(512)S(1)} collective-permute-done((f32[264]{0:T(512)S(1)}, f32[264]{0:T(512)S(1)}, u32[]{:S(2)}, u32[]{:S(2)}) %collective-permute-start.39) | collective-permute-done | bytes 1088 | tf_op jit(solution)/shard_map/ppermute | solution.py:448
  267.2 3.5 collective-permute-done.40
  274.6 14.3 %collective-permute-done.41 = f32[264]{0:T(512)S(1)} collective-permute-done((f32[264]{0:T(512)S(1)}, f32[264]{0:T(512)S(1)}, u32[]{:S(2)}, u32[]{:S(2)}) %collective-permute-start.41) | collective-permute-done | bytes 1088 | tf_op jit(solution)/shard_map/ppermute | solution.py:448
  289.5 5.2 %collective-permute-done.32 = bf16[1,64,1152]{2,1,0:T(8,128)(2,1)S(1)} collective-permute-done((bf16[1,64,1152]{2,1,0:T(8,128)(2,1)S(1)}, bf16[1,64,1152]{2,1,0:T(8,128)(2,1)S(1)}, u32[]{:S(2)}, u32[]{:S(2)}) %collective-permute-start.32) | collective-permute-done | bytes 147488 | tf_op jit(solution)/shard_map/ppermute | solution.py:448
  296.8 4.3 %collective-permute-start.26 = (bf16[1,64,1152]{2,1,0:T(8,128)(2,1)S(1)}, bf16[1,64,1152]{2,1,0:T(8,128)(2,1)S(1)}, u32[]{:S(2)}, u32[]{:S(2)}) collective-permute-start(bf16[1,64,1152]{2,1,0:T(8,128)(2,1)S(1)} %get-tuple-element.135), channel_id=1, source_target_pairs={{0,8},{4,12},{8,0},{12,4},{16,24},{20,28},{24,16},{28,20},{1,9},{5... | collective-permute-start | bytes 442376 | tf_op jit(solution)/shard_map/ppermute | solution.py:448
  302.1 6.3 %collective-permute-done.28 = bf16[1,64,1152]{2,1,0:T(8,128)(2,1)S(1)} collective-permute-done((bf16[1,64,1152]{2,1,0:T(8,128)(2,1)S(1)}, bf16[1,64,1152]{2,1,0:T(8,128)(2,1)S(1)}, u32[]{:S(2)}, u32[]{:S(2)}) %collective-permute-start.28) | collective-permute-done | bytes 147488 | tf_op jit(solution)/shard_map/ppermute | solution.py:448
  308.3 9.9 %collective-permute-done.27 = bf16[1,64,1152]{2,1,0:T(8,128)(2,1)S(1)} collective-permute-done((bf16[1,64,1152]{2,1,0:T(8,128)(2,1)S(1)}, bf16[1,64,1152]{2,1,0:T(8,128)(2,1)S(1)}, u32[]{:S(2)}, u32[]{:S(2)}) %collective-permute-start.27) | collective-permute-done | bytes 147488 | tf_op jit(solution)/shard_map/ppermute | solution.py:448
  332.0 6.3 %collective-permute-done.35 = bf16[2,1,32,2304]{3,2,1,0:T(8,128)(2,1)S(1)} collective-permute-done((bf16[2,1,32,2304]{3,2,1,0:T(8,128)(2,1)S(1)}, bf16[2,1,32,2304]{3,2,1,0:T(8,128)(2,1)S(1)}, u32[]{:S(2)}, u32[]{:S(2)}) %collective-permute-start.35) | collective-permute-done | bytes 294944 | tf_op jit(solution)/shard_map/ppermute | solution.py:448
  343.0 3.0 multiply_subtract_fusion.2
  (414 shorter events, 115.4 us)
Async XLA Ops:
  7.2 135.1 %all-gather.2.cloned.1.call-start = ((), (), s32[]{:S(2)}) async-start(), calls=%async_computation.1 | async-start | bytes 5308416 | tf_op jit(solution)/shard_map/all_gather | solution.py:697
  12.3 11.1 %collective-permute-start.2 = (bf16[2,1,32,1152]{3,2,1,0:T(8,128)(2,1)}, bf16[2,1,32,1152]{3,2,1,0:T(8,128)(2,1)S(1)}, u32[]{:S(2)}, u32[]{:S(2)}) collective-permute-start(bf16[2,1,32,1152]{3,2,1,0:T(8,128)(2,1)} %get-tuple-element.152), channel_id=1, source_target_pairs={{0,2},{1,3},{2,0},{3,1},{4,6},{5,7},{6,4},{7,5},{8,10},{9,11},{10,... | collective-permute-start | bytes 442376 | tf_op jit(solution)/shard_map/ppermute | solution.py:448
  16.1 36.9 %collective-permute-start = (bf16[1,128,2048]{2,1,0:T(8,128)(2,1)}, bf16[1,128,2048]{2,1,0:T(8,128)(2,1)}, u32[]{:S(2)}, u32[]{:S(2)}) collective-permute-start(bf16[1,128,2048]{2,1,0:T(8,128)(2,1)} %maximum_bitcast_fusion), channel_id=1, source_target_pairs={{0,2},{1,3},{2,0},{3,1},{4,6},{5,7},{6,4},{7,5},{8,10},{9,11},{10,... | collective-permute-start | bytes 1572872 | tf_op jit(solution)/shard_map/ppermute | solution.py:448
  17.8 19.2 %collective-permute-start.16 = (bf16[2,1,32,2304]{3,2,1,0:T(8,128)(2,1)}, bf16[2,1,32,2304]{3,2,1,0:T(8,128)(2,1)}, u32[]{:S(2)}, u32[]{:S(2)}) collective-permute-start(bf16[2,1,32,2304]{3,2,1,0:T(8,128)(2,1)} %get-tuple-element.140), channel_id=1, source_target_pairs={{0,2},{1,3},{2,0},{3,1},{4,6},{5,7},{6,4},{7,5},{8,10},{9,11},{10,... | collective-permute-start | bytes 884744 | tf_op jit(solution)/shard_map/ppermute | solution.py:448
  24.9 17.9 %collective-permute-start.4 = (bf16[1,64,1152]{2,1,0:T(8,128)(2,1)S(1)}, bf16[1,64,1152]{2,1,0:T(8,128)(2,1)S(1)}, u32[]{:S(2)}, u32[]{:S(2)}) collective-permute-start(bf16[1,64,1152]{2,1,0:T(8,128)(2,1)S(1)} %get-tuple-element.147), channel_id=1, source_target_pairs={{0,8},{4,12},{8,0},{12,4},{16,24},{20,28},{24,16},{28,20},{1,9},{5... | collective-permute-start | bytes 442376 | tf_op jit(solution)/shard_map/ppermute | solution.py:448
  26.6 18.1 %collective-permute-start.5 = (bf16[1,64,1152]{2,1,0:T(8,128)(2,1)S(1)}, bf16[1,64,1152]{2,1,0:T(8,128)(2,1)S(1)}, u32[]{:S(2)}, u32[]{:S(2)}) collective-permute-start(bf16[1,64,1152]{2,1,0:T(8,128)(2,1)S(1)} %get-tuple-element.147), channel_id=1, source_target_pairs={{0,16},{4,20},{8,24},{12,28},{16,0},{20,4},{24,8},{28,12},{1,17},{... | collective-permute-start | bytes 442376 | tf_op jit(solution)/shard_map/ppermute | solution.py:448
  29.2 18.2 %collective-permute-start.6 = (bf16[1,64,1152]{2,1,0:T(8,128)(2,1)S(1)}, bf16[1,64,1152]{2,1,0:T(8,128)(2,1)S(1)}, u32[]{:S(2)}, u32[]{:S(2)}) collective-permute-start(bf16[1,64,1152]{2,1,0:T(8,128)(2,1)S(1)} %get-tuple-element.147), channel_id=1, source_target_pairs={{0,24},{4,28},{8,16},{12,20},{16,8},{20,12},{24,0},{28,4},{1,25},{... | collective-permute-start | bytes 442376 | tf_op jit(solution)/shard_map/ppermute | solution.py:448
  42.1 9.5 %collective-permute-start.17 = (bf16[1,2,32,2304]{3,2,1,0:T(8,128)(2,1)S(1)}, bf16[1,2,32,2304]{3,2,1,0:T(8,128)(2,1)S(1)}, u32[]{:S(2)}, u32[]{:S(2)}) collective-permute-start(bf16[1,2,32,2304]{3,2,1,0:T(8,128)(2,1)S(1)} %get-tuple-element.138), channel_id=1, source_target_pairs={{0,1},{1,0},{2,3},{3,2},{4,5},{5,4},{6,7},{7,6},{8,9},{9,8},{10,11... | collective-permute-start | bytes 884744 | tf_op jit(solution)/shard_map/ppermute | solution.py:448
  42.8 23.5 %collective-permute-start.9 = (bf16[1,2,64,1152]{3,2,1,0:T(8,128)(2,1)}, bf16[1,2,64,1152]{3,2,1,0:T(8,128)(2,1)}, u32[]{:S(2)}, u32[]{:S(2)}) collective-permute-start(bf16[1,2,64,1152]{3,2,1,0:T(8,128)(2,1)} %bitcast_dynamic-update-slice_fusion.8), channel_id=1, source_target_pairs={{0,8},{4,12},{8,0},{12,4},{16,24},{20,28},{24,16},{28,20},{1,9},{5... | collective-permute-start | bytes 884744 | tf_op jit(solution)/shard_map/ppermute | solution.py:448
  44.6 27.2 %collective-permute-start.10 = (bf16[1,2,64,1152]{3,2,1,0:T(8,128)(2,1)}, bf16[1,2,64,1152]{3,2,1,0:T(8,128)(2,1)}, u32[]{:S(2)}, u32[]{:S(2)}) collective-permute-start(bf16[1,2,64,1152]{3,2,1,0:T(8,128)(2,1)} %bitcast_dynamic-update-slice_fusion.8), channel_id=1, source_target_pairs={{0,16},{4,20},{8,24},{12,28},{16,0},{20,4},{24,8},{28,12},{1,17},{... | collective-permute-start | bytes 884744 | tf_op jit(solution)/shard_map/ppermute | solution.py:448
  47.4 15.3 %collective-permute-start.7 = (bf16[1,4,64,1152]{3,2,1,0:T(8,128)(2,1)S(1)}, bf16[1,4,64,1152]{3,2,1,0:T(8,128)(2,1)}, u32[]{:S(2)}, u32[]{:S(2)}) collective-permute-start(bf16[1,4,64,1152]{3,2,1,0:T(8,128)(2,1)S(1)} %bitcast_dynamic-update-slice_fusion.10), channel_id=1, source_target_pairs={{0,4},{4,0},{8,12},{12,8},{16,20},{20,16},{24,28},{28,24},{1,5},{5... | collective-permute-start | bytes 1769480 | tf_op jit(solution)/shard_map/ppermute | solution.py:448
  51.6 22.0 %collective-permute-start.11 = (bf16[1,2,64,1152]{3,2,1,0:T(8,128)(2,1)}, bf16[1,2,64,1152]{3,2,1,0:T(8,128)(2,1)}, u32[]{:S(2)}, u32[]{:S(2)}) collective-permute-start(bf16[1,2,64,1152]{3,2,1,0:T(8,128)(2,1)} %bitcast_dynamic-update-slice_fusion.8), channel_id=1, source_target_pairs={{0,24},{4,28},{8,16},{12,20},{16,8},{20,12},{24,0},{28,4},{1,25},{... | collective-permute-start | bytes 884744 | tf_op jit(solution)/shard_map/ppermute | solution.py:448
  52.8 275.3 %reduce-scatter.2.cloned.1.call-start = ((), (), s32[]{:S(2)}) async-start(), calls=%async_computation.2 | async-start | bytes 5308416 | tf_op jit(solution)/shard_map/reduce_scatter | solution.py:792
  55.3 31.6 %collective-permute-start.1 = (bf16[2,128,2048]{2,1,0:T(8,128)(2,1)}, bf16[2,128,2048]{2,1,0:T(8,128)(2,1)}, u32[]{:S(2)}, u32[]{:S(2)}) collective-permute-start(bf16[2,128,2048]{2,1,0:T(8,128)(2,1)} %pad_maximum_fusion), channel_id=1, source_target_pairs={{0,1},{1,0},{2,3},{3,2},{4,5},{5,4},{6,7},{7,6},{8,9},{9,8},{10,11... | collective-permute-start | bytes 3145736 | tf_op jit(solution)/shard_map/ppermute | solution.py:448
  86.8 42.2 %collective-permute-start.15 = (bf16[2,1024,256]{2,1,0:T(8,128)(2,1)S(1)}, bf16[2,1024,256]{2,1,0:T(8,128)(2,1)}, u32[]{:S(2)}, u32[]{:S(2)}) collective-permute-start(bf16[2,1024,256]{2,1,0:T(8,128)(2,1)S(1)} %pad_maximum_fusion.1), channel_id=1, source_target_pairs={{0,1},{1,0},{2,3},{3,2},{4,5},{5,4},{6,7},{7,6},{8,9},{9,8},{10,11... | collective-permute-start | bytes 3145736 | tf_op jit(solution)/shard_map/ppermute | solution.py:448
  154.5 14.3 %collective-permute-start.19 = (bf16[2,128,1024]{2,1,0:T(8,128)(2,1)}, bf16[2,128,1024]{2,1,0:T(8,128)(2,1)}, u32[]{:S(2)}, u32[]{:S(2)}) collective-permute-start(bf16[2,128,1024]{2,1,0:T(8,128)(2,1)} %fusion.21), channel_id=1, source_target_pairs={{0,2},{1,3},{2,0},{3,1},{4,6},{5,7},{6,4},{7,5},{8,10},{9,11},{10,... | collective-permute-start | bytes 1572872 | tf_op jit(solution)/shard_map/ppermute | solution.py:448
  173.5 12.3 %collective-permute-start.20 = (bf16[2,128,1024]{2,1,0:T(8,128)(2,1)}, bf16[2,128,1024]{2,1,0:T(8,128)(2,1)}, u32[]{:S(2)}, u32[]{:S(2)}) collective-permute-start(bf16[2,128,1024]{2,1,0:T(8,128)(2,1)} %get-tuple-element.99), channel_id=1, source_target_pairs={{0,1},{1,0},{2,3},{3,2},{4,5},{5,4},{6,7},{7,6},{8,9},{9,8},{10,11... | collective-permute-start | bytes 1572872 | tf_op jit(solution)/shard_map/ppermute | solution.py:448
  188.1 106.6 %collective-permute-start.21 = (bf16[2,128,1024]{2,1,0:T(8,128)(2,1)}, bf16[2,128,1024]{2,1,0:T(8,128)(2,1)S(1)}, u32[]{:S(2)}, u32[]{:S(2)}) collective-permute-start(bf16[2,128,1024]{2,1,0:T(8,128)(2,1)} %dynamic-slice_bitcast_fusion.2), channel_id=1, source_target_pairs={{0,1},{1,0},{2,3},{3,2},{4,5},{5,4},{6,7},{7,6},{8,9},{9,8},{10,11... | collective-permute-start | bytes 1572872 | tf_op jit(solution)/shard_map/ppermute | solution.py:448
  223.1 14.8 %collective-permute-start.38 = (f32[264]{0:T(512)S(1)}, f32[264]{0:T(512)S(1)}, u32[]{:S(2)}, u32[]{:S(2)}) collective-permute-start(f32[264]{0:T(512)S(1)} %fusion.74), channel_id=1, source_target_pairs={{0,1},{1,0},{2,3},{3,2},{4,5},{5,4},{6,7},{7,6},{8,9},{9,8},{10,11... | collective-permute-start | bytes 3176 | tf_op jit(solution)/shard_map/ppermute | solution.py:448
  223.2 47.6 %collective-permute-start.31 = (bf16[1,2,64,1152]{3,2,1,0:T(8,128)(2,1)S(1)}, bf16[1,2,64,1152]{3,2,1,0:T(8,128)(2,1)S(1)}, u32[]{:S(2)}, u32[]{:S(2)}) collective-permute-start(bf16[1,2,64,1152]{3,2,1,0:T(8,128)(2,1)S(1)} %get-tuple-element.125), channel_id=1, source_target_pairs={{0,24},{4,28},{8,16},{12,20},{16,8},{20,12},{24,0},{28,4},{1,25},{... | collective-permute-start | bytes 884744 | tf_op jit(solution)/shard_map/ppermute | solution.py:448
  224.9 47.4 %collective-permute-start.30 = (bf16[1,2,64,1152]{3,2,1,0:T(8,128)(2,1)S(1)}, bf16[1,2,64,1152]{3,2,1,0:T(8,128)(2,1)S(1)}, u32[]{:S(2)}, u32[]{:S(2)}) collective-permute-start(bf16[1,2,64,1152]{3,2,1,0:T(8,128)(2,1)S(1)} %get-tuple-element.126), channel_id=1, source_target_pairs={{0,16},{4,20},{8,24},{12,28},{16,0},{20,4},{24,8},{28,12},{1,17},{... | collective-permute-start | bytes 884744 | tf_op jit(solution)/shard_map/ppermute | solution.py:448
  237.4 35.5 %collective-permute-start.29 = (bf16[1,2,64,1152]{3,2,1,0:T(8,128)(2,1)S(1)}, bf16[1,2,64,1152]{3,2,1,0:T(8,128)(2,1)S(1)}, u32[]{:S(2)}, u32[]{:S(2)}) collective-permute-start(bf16[1,2,64,1152]{3,2,1,0:T(8,128)(2,1)S(1)} %get-tuple-element.124), channel_id=1, source_target_pairs={{0,8},{4,12},{8,0},{12,4},{16,24},{20,28},{24,16},{28,20},{1,9},{5... | collective-permute-start | bytes 884744 | tf_op jit(solution)/shard_map/ppermute | solution.py:448
  237.9 29.3 %collective-permute-start.39 = (f32[264]{0:T(512)S(1)}, f32[264]{0:T(512)S(1)}, u32[]{:S(2)}, u32[]{:S(2)}) collective-permute-start(f32[264]{0:T(512)S(1)} %add.496), channel_id=1, source_target_pairs={{0,16},{4,20},{8,24},{12,28},{16,0},{20,4},{24,8},{28,12},{1,17},{... | collective-permute-start | bytes 3176 | tf_op jit(solution)/shard_map/ppermute | solution.py:448
  270.7 30.3 %collective-permute-start.23 = (bf16[2,128,1024]{2,1,0:T(8,128)(2,1)S(1)}, bf16[2,128,1024]{2,1,0:T(8,128)(2,1)S(1)}, u32[]{:S(2)}, u32[]{:S(2)}) collective-permute-start(bf16[2,128,1024]{2,1,0:T(8,128)(2,1)S(1)} %dynamic-slice_bitcast_fusion.1), channel_id=1, source_target_pairs={{0,1},{1,0},{2,3},{3,2},{4,5},{5,4},{6,7},{7,6},{8,9},{9,8},{10,11... | collective-permute-start | bytes 1572872 | tf_op jit(solution)/shard_map/ppermute | solution.py:448
  270.7 25.6 %collective-permute-start.25 = (bf16[1,4,64,1152]{3,2,1,0:T(8,128)(2,1)S(1)}, bf16[1,4,64,1152]{3,2,1,0:T(8,128)(2,1)S(1)}, u32[]{:S(2)}, u32[]{:S(2)}) collective-permute-start(bf16[1,4,64,1152]{3,2,1,0:T(8,128)(2,1)S(1)} %dynamic-slice_bitcast_fusion), channel_id=1, source_target_pairs={{0,4},{4,0},{8,12},{12,8},{16,20},{20,16},{24,28},{28,24},{1,5},{5... | collective-permute-start | bytes 1769480 | tf_op jit(solution)/shard_map/ppermute | solution.py:448
  272.3 16.6 %collective-permute-start.41 = (f32[264]{0:T(512)S(1)}, f32[264]{0:T(512)S(1)}, u32[]{:S(2)}, u32[]{:S(2)}) collective-permute-start(f32[264]{0:T(512)S(1)} %add.498), channel_id=1, source_target_pairs={{0,4},{4,0},{8,12},{12,8},{16,20},{20,16},{24,28},{28,24},{1,5},{5... | collective-permute-start | bytes 3176 | tf_op jit(solution)/shard_map/ppermute | solution.py:448
  273.0 21.7 %collective-permute-start.32 = (bf16[1,64,1152]{2,1,0:T(8,128)(2,1)S(1)}, bf16[1,64,1152]{2,1,0:T(8,128)(2,1)S(1)}, u32[]{:S(2)}, u32[]{:S(2)}) collective-permute-start(bf16[1,64,1152]{2,1,0:T(8,128)(2,1)S(1)} %fusion.49), channel_id=1, source_target_pairs={{0,4},{4,0},{8,12},{12,8},{16,20},{20,16},{24,28},{28,24},{1,5},{5... | collective-permute-start | bytes 442376 | tf_op jit(solution)/shard_map/ppermute | solution.py:448
  295.0 26.1 %collective-permute-start.22 = (bf16[1,128,1024]{2,1,0:T(8,128)(2,1)S(1)}, bf16[1,128,1024]{2,1,0:T(8,128)(2,1)S(1)}, u32[]{:S(2)}, u32[]{:S(2)}) collective-permute-start(bf16[1,128,1024]{2,1,0:T(8,128)(2,1)S(1)} %dynamic-slice_convert_fusion.1), channel_id=1, source_target_pairs={{0,2},{1,3},{2,0},{3,1},{4,6},{5,7},{6,4},{7,5},{8,10},{9,11},{10,... | collective-permute-start | bytes 786440 | tf_op jit(solution)/shard_map/ppermute | solution.py:448
  296.6 11.7 %collective-permute-start.28 = (bf16[1,64,1152]{2,1,0:T(8,128)(2,1)S(1)}, bf16[1,64,1152]{2,1,0:T(8,128)(2,1)S(1)}, u32[]{:S(2)}, u32[]{:S(2)}) collective-permute-start(bf16[1,64,1152]{2,1,0:T(8,128)(2,1)S(1)} %get-tuple-element.136), channel_id=1, source_target_pairs={{0,24},{4,28},{8,16},{12,20},{16,8},{20,12},{24,0},{28,4},{1,25},{... | collective-permute-start | bytes 442376 | tf_op jit(solution)/shard_map/ppermute | solution.py:448
  296.7 21.6 %collective-permute-start.27 = (bf16[1,64,1152]{2,1,0:T(8,128)(2,1)S(1)}, bf16[1,64,1152]{2,1,0:T(8,128)(2,1)S(1)}, u32[]{:S(2)}, u32[]{:S(2)}) collective-permute-start(bf16[1,64,1152]{2,1,0:T(8,128)(2,1)S(1)} %get-tuple-element.137), channel_id=1, source_target_pairs={{0,16},{4,20},{8,24},{12,28},{16,0},{20,4},{24,8},{28,12},{1,17},{... | collective-permute-start | bytes 442376 | tf_op jit(solution)/shard_map/ppermute | solution.py:448
  296.8 21.5 %collective-permute-start.26 = (bf16[1,64,1152]{2,1,0:T(8,128)(2,1)S(1)}, bf16[1,64,1152]{2,1,0:T(8,128)(2,1)S(1)}, u32[]{:S(2)}, u32[]{:S(2)}) collective-permute-start(bf16[1,64,1152]{2,1,0:T(8,128)(2,1)S(1)} %get-tuple-element.135), channel_id=1, source_target_pairs={{0,8},{4,12},{8,0},{12,4},{16,24},{20,28},{24,16},{28,20},{1,9},{5... | collective-permute-start | bytes 442376 | tf_op jit(solution)/shard_map/ppermute | solution.py:448
  301.3 18.6 %collective-permute-start.24 = (bf16[1,128,1024]{2,1,0:T(8,128)(2,1)S(1)}, bf16[1,128,1024]{2,1,0:T(8,128)(2,1)S(1)}, u32[]{:S(2)}, u32[]{:S(2)}) collective-permute-start(bf16[1,128,1024]{2,1,0:T(8,128)(2,1)S(1)} %dynamic-slice_convert_fusion), channel_id=1, source_target_pairs={{0,2},{1,3},{2,0},{3,1},{4,6},{5,7},{6,4},{7,5},{8,10},{9,11},{10,... | collective-permute-start | bytes 786440 | tf_op jit(solution)/shard_map/ppermute | solution.py:448
  (89 other events, 686.3 us)
Sparse Core Ops, SparseCore 0:
  52.9 89.3 all-gather.1
  182.2 135.4 reduce-scatter.1

commit v3 on v2

--- a/solution.py
+++ b/solution.py
@@ -676,11 +676,6 @@
         [jnp.concatenate([in_slice(c), out_t[:, c * DV : (c + 1) * DV]], axis=1) for c in range(n_ctx)]
     )
     w_one = trade(w_one, "ctx").reshape(1, n_ctx * rows, -1)
-    full_one = gather_far(w_one, "dp")[0]
-    full_in, full_out = full_one[:, : HEADG + EXTRA], full_one[:, HEADG + EXTRA :]
-    tokens = jnp.concatenate([act_own, cot_own], axis=1)
-    tokens = gather_rows(tokens, "ctx")
-    x_full, cot_full = tokens[:, :D], tokens[:, D:]
     ff_pad = -(-ff // 256) * 256
     fill = jnp.zeros((rows, ff_pad - ff), BF)
     down_t = mlp_down.T
@@ -694,9 +689,14 @@
         ]
     )
     w_mlp = trade(w_mlp, "ctx").reshape(n_ctx * rows, 3 * ff_pad)
+    tokens = jnp.concatenate([act_own, cot_own], axis=1)
+    w_mlp, w_one, tokens = lax.optimization_barrier((w_mlp, w_one, tokens))
+    tokens = gather_rows(tokens, "ctx")
+    x_full, cot_full = tokens[:, :D], tokens[:, D:]
     full_mlp = lax.all_gather(w_mlp, "dp", axis=0, tiled=True)
+    full_one = gather_far(w_one, "dp")[0]
+    full_in, full_out = full_one[:, : HEADG + EXTRA], full_one[:, HEADG + EXTRA :]
     full_wg, full_wu, full_wd = (full_mlp[:, k * ff_pad : (k + 1) * ff_pad] for k in range(3))
-    outs_near = near_pieces(full_out, "ctx")
 
     share = vectors.shape[0]
     vec_float = flat_of(full_in[:, HEADG + half :].astype(F32).reshape(-1, rows, half), share)
@@ -723,6 +723,8 @@
     unit = xf * inv_rms
     normed = (unit * norm_gain).astype(BF)
     px = dot(normed, full_in)
+    px, out_away = lax.optimization_barrier((px, full_out))
+    outs_near = near_pieces(out_away, "ctx")
     mixed, *saved = core_fwd(px, taps, par, pos, head_gain[None, :])
     branch = 0.0
     for piece, weight in zip(near_pieces(mixed, "ctx"), outs_near):
@@ -748,7 +750,9 @@
     pairs = d_two.astype(BF).reshape(grid)
     got = swap(take(pairs, 1 - low, 1), "ctx", 1)
     column = take(pairs, low, 1).astype(F32) + got.astype(F32)
-    d_two_col = column + swap(column.astype(BF), "ctx", 2).astype(F32)
+    grad_mlp = mlp_grad(normed_two, g_mlp, d_hgate, d_hup, hidden)
+    met, _ = lax.optimization_barrier((swap(column.astype(BF), "ctx", 2), grad_mlp))
+    d_two_col = column + met.astype(F32)
     resid_col = take(resid.reshape(grid), low, 1)
     cot_col = take(cot_full.reshape(grid), low, 1).astype(F32)
     inv_col = lax.rsqrt(jnp.mean(resid_col * resid_col, -1, keepdims=True) + NORM_EPS)
@@ -765,7 +769,6 @@
     resid_own = take(resid_col, high, 0)
     x_own = act_own.astype(F32)
 
-    grad_mlp = mlp_grad(normed_two, g_mlp, d_hgate, d_hup, hidden)
     mlp_part = dot(hidden, full_wd, 1, 1).astype(BF)
     mlp_part, g_branch = lax.optimization_barrier((mlp_part, g_branch))
     mlp_own = reduce_rows(mlp_part.reshape(n_ctx, length, D), "ctx")
@@ -790,8 +793,19 @@
         return trade(part.reshape(n_ctx, rows, -1).astype(BF), "ctx").astype(F32)
 
     own_mlp = to_owner(lax.psum_scatter(grad_mlp, "dp", scatter_dimension=0, tiled=True))
-    own_one = to_owner(reduce_far(grad_one[None], "dp")[0])
+    far_one, d_normed_b = lax.optimization_barrier(
+        (reduce_far(grad_one[None], "dp")[0], d_normed.astype(BF))
+    )
+    own_one = to_owner(far_one)
     own_in, own_out = own_one[:, :, : HEADG + EXTRA], own_one[:, :, HEADG + EXTRA :]
+    at_head = jnp.arange(H) == me
+    grad_small = jnp.concatenate(
+        [d_hgain[0], jnp.where(at_head, d_par[0, 0], 0.0), jnp.where(at_head, d_par[0, 1], 0.0)]
+    )
+    grad_small, own_one = lax.optimization_barrier((grad_small, own_one))
+    own_in, own_out = own_one[:, :, : HEADG + EXTRA], own_one[:, :, HEADG + EXTRA :]
+    summed_small = sum_everywhere(grad_small, ("ctx", "dp"))
+
 
     def beside(value, first, size):
         return [value[c, :, first : first + size] for c in range(n_ctx)]
@@ -807,13 +821,7 @@
         jnp.concatenate(beside(own_mlp, k * ff_pad, ff), axis=1) for k in range(3)
     )
     owned_wd = owned_wd_t.T
-    at_head = jnp.arange(H) == me
-    grad_small = jnp.concatenate(
-        [d_hgain[0], jnp.where(at_head, d_par[0, 0], 0.0), jnp.where(at_head, d_par[0, 1], 0.0)]
-    )
-    summed_small = sum_everywhere(grad_small, ("ctx", "dp"))
-
-    d_normed_own = reduce_rows(d_normed.astype(BF).reshape(n_ctx, length, D), "ctx")
+    d_normed_own = reduce_rows(d_normed_b.reshape(n_ctx, length, D), "ctx")
     inv_x = lax.rsqrt(jnp.mean(x_own * x_own, -1, keepdims=True) + NORM_EPS)
     unit_x = x_own * inv_x
     d_unit = d_normed_own * norm_gain

time: 358 us -> 336 us (0.939)
  local copies, waits for them, and re-layouts: 44.5 us -> 31.7 us
  waiting for transfers between devices: 131 us -> 124 us
  matrix products: 25 us -> 19.1 us
    all_gather x1, waiting for transfers between devices: 8.09 us -> 0.02 us  [local(): full_mlp = lax.all_gather(w_mlp, 'dp', axis=0, tiled=True)]
    dot_general x13, matrix products: 25 us -> 19.1 us  [dot(): lax.dot_general(a, b, (((lhs,), (rhs,)), ((), ())), preferred_element_typ...]
    dynamic_update_slice x3, local copies, waits for them, and re-layouts: 5.14 us -> 0.11 us  [gather_far(): lax.dynamic_update_slice(out, got[:, None, :, None], (zero, far ^ m, zero...]
  transfers between devices with their start and end apart: 44 -> 44, of which waited for: 21 -> 23; matrix products, arithmetic and copies ran while one was open for 19% -> 15% of each run, Pallas kernels for 14% -> 15%
where the time goes in v3:
time: 336 us; the launch traced here: 332 us
  waiting for transfers between devices  124 us (37%)
  starting transfers between devices  56.8 us (17%)
  Pallas kernels  48.9 us (15%)
  other arithmetic  34.8 us (10%)
  local copies, waits for them, and re-layouts  31.7 us (9%)
  matrix products  19.1 us (6%)
  between operations  16.8 us (5%)
    ppermute x42, waiting for transfers between devices, swap(): return lax.ppermute(value, axis, [(i, i ^ mask) for i in range(count)])  124 us
    ppermute x42, starting transfers between devices, swap(): return lax.ppermute(value, axis, [(i, i ^ mask) for i in range(count)])  56.5 us
    pallas_call x1, Pallas kernels, core_fwd(): pl.pallas_call(core_fwd_kernel, name='core_fwd', out_shape=(shape((rows,...  21.2 us
    dot_general x13, matrix products, dot(): lax.dot_general(a, b, (((lhs,), (rhs,)), ((), ())), preferred_element_typ...  19.1 us
    pallas_call x1, Pallas kernels, core_bwd(): pl.pallas_call(core_bwd_kernel, name='core_bwd', out_shape=(shape((rows,...  16.5 us
    unnamed x171, local copies, waits for them, and re-layouts  13.2 us
    sub x7, other arithmetic, adamw(): weights - learn_rate * (corrected / (jnp.sqrt(scaled) + adam_eps) + weigh...  7.97 us
  transfers between devices with their start and end apart: 44, of which 23 were waited for; matrix products, arithmetic and copies ran while one was open for 15% of the time, Pallas kernels for 15%

profile of v3, /device:TPU:0, one launch (start us, length us, event | category | flops | bytes accessed | tf_op | source)
XLA Modules:
  0.0 332.1 jit_solution(9085601542019474788)
XLA Ops:
  10.4 3.1 collective-permute-start
  17.0 6.6 %collective-permute-done.2 = bf16[2,1,32,1152]{3,2,1,0:T(8,128)(2,1)S(1)} collective-permute-done((bf16[2,1,32,1152]{3,2,1,0:T(8,128)(2,1)S(1)}, bf16[2,1,32,1152]{3,2,1,0:T(8,128)(2,1)S(1)}, u32[]{:S(2)}, u32[]{:S(2)}) %collective-permute-start.2) | collective-permute-done | bytes 147488 | tf_op jit(solution)/shard_map/ppermute | solution.py:448
  28.4 2.6 collective-permute-start.7
  35.0 3.6 %collective-permute-done.10 = bf16[1,64,1152]{2,1,0:T(8,128)(2,1)} collective-permute-done((bf16[1,64,1152]{2,1,0:T(8,128)(2,1)}, bf16[1,64,1152]{2,1,0:T(8,128)(2,1)}, u32[]{:S(2)}, u32[]{:S(2)}) %collective-permute-start.10) | collective-permute-done | bytes 147488 | tf_op jit(solution)/shard_map/ppermute | solution.py:448
  40.2 3.5 %collective-permute-start.12 = (bf16[1,2,64,1152]{3,2,1,0:T(8,128)(2,1)S(1)}, bf16[1,2,64,1152]{3,2,1,0:T(8,128)(2,1)S(1)}, u32[]{:S(2)}, u32[]{:S(2)}) collective-permute-start(bf16[1,2,64,1152]{3,2,1,0:T(8,128)(2,1)S(1)} %bitcast_dynamic-update-slice_fusion.8), channel_id=1, source_target_pairs={{0,16},{4,20},{8,24},{12,28},{16,0},{20,4},{24,8},{28,12},{1,17},{... | collective-permute-start | bytes 884744 | tf_op jit(solution)/shard_map/ppermute | solution.py:448
  51.1 12.7 %collective-permute-done.9 = bf16[1,4,64,1152]{3,2,1,0:T(8,128)(2,1)S(1)} collective-permute-done((bf16[1,4,64,1152]{3,2,1,0:T(8,128)(2,1)S(1)}, bf16[1,4,64,1152]{3,2,1,0:T(8,128)(2,1)S(1)}, u32[]{:S(2)}, u32[]{:S(2)}) %collective-permute-start.9) | collective-permute-done | bytes 589856 | tf_op jit(solution)/shard_map/ppermute | solution.py:448
  64.0 14.3 %collective-permute-done.12 = bf16[1,2,64,1152]{3,2,1,0:T(8,128)(2,1)S(1)} collective-permute-done((bf16[1,2,64,1152]{3,2,1,0:T(8,128)(2,1)S(1)}, bf16[1,2,64,1152]{3,2,1,0:T(8,128)(2,1)S(1)}, u32[]{:S(2)}, u32[]{:S(2)}) %collective-permute-start.12) | collective-permute-done | bytes 294944 | tf_op jit(solution)/shard_map/ppermute | solution.py:448
  90.4 7.0 %collective-permute-done.16 = bf16[1,1024,256]{2,1,0:T(8,128)(2,1)} collective-permute-done((bf16[1,1024,256]{2,1,0:T(8,128)(2,1)}, bf16[1,1024,256]{2,1,0:T(8,128)(2,1)}, u32[]{:S(2)}, u32[]{:S(2)}) %collective-permute-start.16) | collective-permute-done | bytes 524320 | tf_op jit(solution)/shard_map/ppermute | solution.py:448
  98.7 21.2 %core_fwd.1 = (bf16[512,256]{1,0:T(8,128)(2,1)S(1)}, f32[8,128,256]{2,1,0:T(8,128)S(1)}, f32[512,256]{1,0:T(8,128)S(1)}, f32[512,256]{1,0:T(8,128)S(1)}, f32[512...) custom-call(f32[512,896]{1,0:T(8,128)S(1)} %fusion.7.px_ref, ...), custom_call_target="tpu_custom_call" | custom-call | tf_op jit(solution)/shard_map/core_fwd/pallas_call | solution.py:308
  121.9 7.0 %collective-permute-done.14 = bf16[1,512,256]{2,1,0:T(8,128)(2,1)S(1)} collective-permute-done((bf16[1,512,256]{2,1,0:T(8,128)(2,1)S(1)}, bf16[1,512,256]{2,1,0:T(8,128)(2,1)S(1)}, u32[]{:S(2)}, u32[]{:S(2)}) %collective-permute-start.14) | collective-permute-done | bytes 262176 | tf_op jit(solution)/shard_map/ppermute | solution.py:448
  136.1 2.5 fusion.18
  139.9 2.5 multiply_convert_fusion.2
  151.5 2.3 slice.694
  155.2 5.4 %mlp_grad.1 = bf16[1024,2304]{1,0:T(8,128)(2,1)S(1)} custom-call(bf16[512,1024]{1,0:T(8,128)(2,1)S(1)} %multiply_convert_fusion.1.two_ref, bf16[512,1024]{1,0:T(8,128)(2,1)S(1)} %get-tuple-element.130.cot_ref, bf16[512,768]{1,0:T(8,128)(2,1)S(1)} %copy-done.11, bf16[512,768]{1,0:T(8,128)(2,1)S(1)} %get-tuple-element.121.du_ref, bf16[512,768]{1,0:T(8,128)(2,1)S(1)} %copy-done.8), custom_call_target="tpu_custom_call" | custom-call | tf_op jit(solution)/shard_map/mlp_grad/pallas_call | solution.py:387
  160.6 2.2 copy-done
  165.5 3.2 bitcast_dynamic-update-slice_fusion.3
  169.8 2.6 convolution_convert_fusion
  175.0 16.5 %core_bwd.1 = (bf16[512,896]{1,0:T(8,128)(2,1)S(1)}, f32[4,512]{1,0:T(4,128)S(1)}, f32[1,256]{1,0:T(1,128)S(1)}, f32[1,128]{1,0:T(1,128)S(1)}) custom-call(f32[512,896]{1,0:T(8,128)} %copy-done.1, f32[4,512]{1,0:T(4,128)S(1)} %pad_maximum_fusion.7.taps_ref, f32[2]{0:T(128)S(1)} %pad_maximum_fusion.9.par_ref, s32[512,1]{1,0:T(8,128)S(1)} %iota_subtract_fusion.pos_ref, ...), custom_call_target="tpu_custom_call" | custom-call | tf_op jit(solution)/shard_map/core_bwd/pallas_call | solution.py:332
  191.6 2.3 fusion.80
  195.3 5.8 %mix_grad.1 = bf16[1024,1152]{1,0:T(8,128)(2,1)S(1)} custom-call(bf16[512,1024]{1,0:T(8,128)(2,1)S(1)} %copy-done.3, bf16[512,896]{1,0:T(8,128)(2,1)S(1)} %copy-done.7, bf16[512,1024]{1,0:T(8,128)(2,1)S(1)} %bitcast.372, bf16[512,256]{1,0:T(8,128)(2,1)S(1)} %get-tuple-element.61.mixed_ref, f32[1024,128]{1,0:T(8,128)S(1)} %bitcast.375), custom_call_target="tpu_custom_call" | custom-call | tf_op jit(solution)/shard_map/mix_grad/pallas_call | solution.py:428
  201.4 4.5 %collective-permute-start.29 = (bf16[1,2,64,1152]{3,2,1,0:T(8,128)(2,1)S(1)}, bf16[1,2,64,1152]{3,2,1,0:T(8,128)(2,1)S(1)}, u32[]{:S(2)}, u32[]{:S(2)}) collective-permute-start(bf16[1,2,64,1152]{3,2,1,0:T(8,128)(2,1)S(1)} %get-tuple-element.145), channel_id=1, source_target_pairs={{0,24},{4,28},{8,16},{12,20},{16,8},{20,12},{24,0},{28,4},{1,25},{... | collective-permute-start | bytes 884744 | tf_op jit(solution)/shard_map/ppermute | solution.py:448
  205.9 11.5 %collective-permute-start.28 = (bf16[1,2,64,1152]{3,2,1,0:T(8,128)(2,1)S(1)}, bf16[1,2,64,1152]{3,2,1,0:T(8,128)(2,1)S(1)}, u32[]{:S(2)}, u32[]{:S(2)}) collective-permute-start(bf16[1,2,64,1152]{3,2,1,0:T(8,128)(2,1)S(1)} %get-tuple-element.146), channel_id=1, source_target_pairs={{0,16},{4,20},{8,24},{12,28},{16,0},{20,4},{24,8},{28,12},{1,17},{... | collective-permute-start | bytes 884744 | tf_op jit(solution)/shard_map/ppermute | solution.py:448
  220.1 35.2 %collective-permute-done.28 = bf16[1,2,64,1152]{3,2,1,0:T(8,128)(2,1)S(1)} collective-permute-done((bf16[1,2,64,1152]{3,2,1,0:T(8,128)(2,1)S(1)}, bf16[1,2,64,1152]{3,2,1,0:T(8,128)(2,1)S(1)}, u32[]{:S(2)}, u32[]{:S(2)}) %collective-permute-start.28) | collective-permute-done | bytes 294944 | tf_op jit(solution)/shard_map/ppermute | solution.py:448
  258.5 5.4 %collective-permute-done.30 = bf16[1,64,1152]{2,1,0:T(8,128)(2,1)S(1)} collective-permute-done((bf16[1,64,1152]{2,1,0:T(8,128)(2,1)S(1)}, bf16[1,64,1152]{2,1,0:T(8,128)(2,1)S(1)}, u32[]{:S(2)}, u32[]{:S(2)}) %collective-permute-start.30) | collective-permute-done | bytes 147488 | tf_op jit(solution)/shard_map/ppermute | solution.py:448
  265.6 3.0 collective-permute-start.24
  272.6 3.5 %collective-permute-done.25 = bf16[1,64,1152]{2,1,0:T(8,128)(2,1)S(1)} collective-permute-done((bf16[1,64,1152]{2,1,0:T(8,128)(2,1)S(1)}, bf16[1,64,1152]{2,1,0:T(8,128)(2,1)S(1)}, u32[]{:S(2)}, u32[]{:S(2)}) %collective-permute-start.25) | collective-permute-done | bytes 147488 | tf_op jit(solution)/shard_map/ppermute | solution.py:448
  281.0 2.6 collective-permute-done.33
  291.9 4.3 %collective-permute-done.39 = f32[264]{0:T(512)S(1)} collective-permute-done((f32[264]{0:T(512)S(1)}, f32[264]{0:T(512)S(1)}, u32[]{:S(2)}, u32[]{:S(2)}) %collective-permute-start.39) | collective-permute-done | bytes 1088 | tf_op jit(solution)/shard_map/ppermute | solution.py:448
  296.3 3.4 %collective-permute-done.40 = f32[264]{0:T(512)S(1)} collective-permute-done((f32[264]{0:T(512)S(1)}, f32[264]{0:T(512)S(1)}, u32[]{:S(2)}, u32[]{:S(2)}) %collective-permute-start.40) | collective-permute-done | bytes 1088 | tf_op jit(solution)/shard_map/ppermute | solution.py:448
  304.2 5.0 %collective-permute-done.32 = bf16[1,128,1024]{2,1,0:T(8,128)(2,1)S(1)} collective-permute-done((bf16[1,128,1024]{2,1,0:T(8,128)(2,1)S(1)}, bf16[1,128,1024]{2,1,0:T(8,128)(2,1)S(1)}, u32[]{:S(2)}, u32[]{:S(2)}) %collective-permute-start.32) | collective-permute-done | bytes 262176 | tf_op jit(solution)/shard_map/ppermute | solution.py:448
  312.4 4.9 %collective-permute-done.35 = bf16[2,1,32,2304]{3,2,1,0:T(8,128)(2,1)S(1)} collective-permute-done((bf16[2,1,32,2304]{3,2,1,0:T(8,128)(2,1)S(1)}, bf16[2,1,32,2304]{3,2,1,0:T(8,128)(2,1)S(1)}, u32[]{:S(2)}, u32[]{:S(2)}) %collective-permute-start.35) | collective-permute-done | bytes 294944 | tf_op jit(solution)/shard_map/ppermute | solution.py:448
  322.0 3.0 multiply_subtract_fusion.2
  (414 shorter events, 102.0 us)
Async XLA Ops:
  7.2 128.8 %all-gather.2.cloned.1.call-start = ((), (), s32[]{:S(2)}) async-start(), calls=%async_computation.1 | async-start | bytes 5308416 | tf_op jit(solution)/shard_map/all_gather | solution.py:696
  10.4 13.4 %collective-permute-start = (bf16[2,1,32,2304]{3,2,1,0:T(8,128)(2,1)S(1)}, bf16[2,1,32,2304]{3,2,1,0:T(8,128)(2,1)S(1)}, u32[]{:S(2)}, u32[]{:S(2)}) collective-permute-start(bf16[2,1,32,2304]{3,2,1,0:T(8,128)(2,1)S(1)} %get-tuple-element.160), channel_id=1, source_target_pairs={{0,2},{1,3},{2,0},{3,1},{4,6},{5,7},{6,4},{7,5},{8,10},{9,11},{10,... | collective-permute-start | bytes 884744 | tf_op jit(solution)/shard_map/ppermute | solution.py:448
  14.3 9.3 %collective-permute-start.2 = (bf16[2,1,32,1152]{3,2,1,0:T(8,128)(2,1)S(1)}, bf16[2,1,32,1152]{3,2,1,0:T(8,128)(2,1)S(1)}, u32[]{:S(2)}, u32[]{:S(2)}) collective-permute-start(bf16[2,1,32,1152]{3,2,1,0:T(8,128)(2,1)S(1)} %get-tuple-element.172), channel_id=1, source_target_pairs={{0,2},{1,3},{2,0},{3,1},{4,6},{5,7},{6,4},{7,5},{8,10},{9,11},{10,... | collective-permute-start | bytes 442376 | tf_op jit(solution)/shard_map/ppermute | solution.py:448
  26.6 13.6 %collective-permute-start.6 = (bf16[1,64,1152]{2,1,0:T(8,128)(2,1)}, bf16[1,64,1152]{2,1,0:T(8,128)(2,1)}, u32[]{:S(2)}, u32[]{:S(2)}) collective-permute-start(bf16[1,64,1152]{2,1,0:T(8,128)(2,1)} %get-tuple-element.167), channel_id=1, source_target_pairs={{0,8},{4,12},{8,0},{12,4},{16,24},{20,28},{24,16},{28,20},{1,9},{5... | collective-permute-start | bytes 442376 | tf_op jit(solution)/shard_map/ppermute | solution.py:448
  28.4 16.3 %collective-permute-start.7 = (bf16[1,64,1152]{2,1,0:T(8,128)(2,1)}, bf16[1,64,1152]{2,1,0:T(8,128)(2,1)}, u32[]{:S(2)}, u32[]{:S(2)}) collective-permute-start(bf16[1,64,1152]{2,1,0:T(8,128)(2,1)} %get-tuple-element.167), channel_id=1, source_target_pairs={{0,16},{4,20},{8,24},{12,28},{16,0},{20,4},{24,8},{28,12},{1,17},{... | collective-permute-start | bytes 442376 | tf_op jit(solution)/shard_map/ppermute | solution.py:448
  31.0 15.1 %collective-permute-start.8 = (bf16[1,64,1152]{2,1,0:T(8,128)(2,1)}, bf16[1,64,1152]{2,1,0:T(8,128)(2,1)}, u32[]{:S(2)}, u32[]{:S(2)}) collective-permute-start(bf16[1,64,1152]{2,1,0:T(8,128)(2,1)} %get-tuple-element.167), channel_id=1, source_target_pairs={{0,24},{4,28},{8,16},{12,20},{16,8},{20,12},{24,0},{28,4},{1,25},{... | collective-permute-start | bytes 442376 | tf_op jit(solution)/shard_map/ppermute | solution.py:448
  31.3 17.7 %collective-permute-start.4 = (bf16[1,128,2048]{2,1,0:T(8,128)(2,1)S(1)}, bf16[1,128,2048]{2,1,0:T(8,128)(2,1)}, u32[]{:S(2)}, u32[]{:S(2)}) collective-permute-start(bf16[1,128,2048]{2,1,0:T(8,128)(2,1)S(1)} %bitcast.392), channel_id=1, source_target_pairs={{0,2},{1,3},{2,0},{3,1},{4,6},{5,7},{6,4},{7,5},{8,10},{9,11},{10,... | collective-permute-start | bytes 1572872 | tf_op jit(solution)/shard_map/ppermute | solution.py:448
  33.1 5.5 %collective-permute-start.10 = (bf16[1,64,1152]{2,1,0:T(8,128)(2,1)}, bf16[1,64,1152]{2,1,0:T(8,128)(2,1)}, u32[]{:S(2)}, u32[]{:S(2)}) collective-permute-start(bf16[1,64,1152]{2,1,0:T(8,128)(2,1)} %get-tuple-element.166), channel_id=1, source_target_pairs={{0,4},{4,0},{8,12},{12,8},{16,20},{20,16},{24,28},{28,24},{1,5},{5... | collective-permute-start | bytes 442376 | tf_op jit(solution)/shard_map/ppermute | solution.py:448
  34.6 274.8 %reduce-scatter.2.cloned.1.call-start = ((), (), s32[]{:S(2)}) async-start(), calls=%async_computation.2 | async-start | bytes 5308416 | tf_op jit(solution)/shard_map/reduce_scatter | solution.py:795
  39.5 24.5 %collective-permute-start.11 = (bf16[1,2,64,1152]{3,2,1,0:T(8,128)(2,1)S(1)}, bf16[1,2,64,1152]{3,2,1,0:T(8,128)(2,1)S(1)}, u32[]{:S(2)}, u32[]{:S(2)}) collective-permute-start(bf16[1,2,64,1152]{3,2,1,0:T(8,128)(2,1)S(1)} %bitcast_dynamic-update-slice_fusion.8), channel_id=1, source_target_pairs={{0,8},{4,12},{8,0},{12,4},{16,24},{20,28},{24,16},{28,20},{1,9},{5... | collective-permute-start | bytes 884744 | tf_op jit(solution)/shard_map/ppermute | solution.py:448
  40.2 38.1 %collective-permute-start.12 = (bf16[1,2,64,1152]{3,2,1,0:T(8,128)(2,1)S(1)}, bf16[1,2,64,1152]{3,2,1,0:T(8,128)(2,1)S(1)}, u32[]{:S(2)}, u32[]{:S(2)}) collective-permute-start(bf16[1,2,64,1152]{3,2,1,0:T(8,128)(2,1)S(1)} %bitcast_dynamic-update-slice_fusion.8), channel_id=1, source_target_pairs={{0,16},{4,20},{8,24},{12,28},{16,0},{20,4},{24,8},{28,12},{1,17},{... | collective-permute-start | bytes 884744 | tf_op jit(solution)/shard_map/ppermute | solution.py:448
  44.7 33.7 %collective-permute-start.13 = (bf16[1,2,64,1152]{3,2,1,0:T(8,128)(2,1)S(1)}, bf16[1,2,64,1152]{3,2,1,0:T(8,128)(2,1)S(1)}, u32[]{:S(2)}, u32[]{:S(2)}) collective-permute-start(bf16[1,2,64,1152]{3,2,1,0:T(8,128)(2,1)S(1)} %bitcast_dynamic-update-slice_fusion.8), channel_id=1, source_target_pairs={{0,24},{4,28},{8,16},{12,20},{16,8},{20,12},{24,0},{28,4},{1,25},{... | collective-permute-start | bytes 884744 | tf_op jit(solution)/shard_map/ppermute | solution.py:448
  47.0 16.8 %collective-permute-start.9 = (bf16[1,4,64,1152]{3,2,1,0:T(8,128)(2,1)S(1)}, bf16[1,4,64,1152]{3,2,1,0:T(8,128)(2,1)S(1)}, u32[]{:S(2)}, u32[]{:S(2)}) collective-permute-start(bf16[1,4,64,1152]{3,2,1,0:T(8,128)(2,1)S(1)} %bitcast_dynamic-update-slice_fusion.10), channel_id=1, source_target_pairs={{0,4},{4,0},{8,12},{12,8},{16,20},{20,16},{24,28},{28,24},{1,5},{5... | collective-permute-start | bytes 1769480 | tf_op jit(solution)/shard_map/ppermute | solution.py:448
  51.1 29.7 %collective-permute-start.5 = (bf16[2,128,2048]{2,1,0:T(8,128)(2,1)}, bf16[2,128,2048]{2,1,0:T(8,128)(2,1)S(1)}, u32[]{:S(2)}, u32[]{:S(2)}) collective-permute-start(bf16[2,128,2048]{2,1,0:T(8,128)(2,1)} %pad_maximum_fusion), channel_id=1, source_target_pairs={{0,1},{1,0},{2,3},{3,2},{4,5},{5,4},{6,7},{7,6},{8,9},{9,8},{10,11... | collective-permute-start | bytes 3145736 | tf_op jit(solution)/shard_map/ppermute | solution.py:448
  86.9 10.4 %collective-permute-start.16 = (bf16[1,1024,256]{2,1,0:T(8,128)(2,1)}, bf16[1,1024,256]{2,1,0:T(8,128)(2,1)}, u32[]{:S(2)}, u32[]{:S(2)}) collective-permute-start(bf16[1,1024,256]{2,1,0:T(8,128)(2,1)} %bitcast.58), channel_id=1, source_target_pairs={{0,2},{1,3},{2,0},{3,1},{4,6},{5,7},{6,4},{7,5},{8,10},{9,11},{10,... | collective-permute-start | bytes 1572872 | tf_op jit(solution)/shard_map/ppermute | solution.py:448
  98.6 33.4 %collective-permute-start.17 = (bf16[2,1024,256]{2,1,0:T(8,128)(2,1)S(1)}, bf16[2,1024,256]{2,1,0:T(8,128)(2,1)S(1)}, u32[]{:S(2)}, u32[]{:S(2)}) collective-permute-start(bf16[2,1024,256]{2,1,0:T(8,128)(2,1)S(1)} %pad_maximum_fusion.1), channel_id=1, source_target_pairs={{0,1},{1,0},{2,3},{3,2},{4,5},{5,4},{6,7},{7,6},{8,9},{9,8},{10,11... | collective-permute-start | bytes 3145736 | tf_op jit(solution)/shard_map/ppermute | solution.py:448
  120.1 8.8 %collective-permute-start.14 = (bf16[1,512,256]{2,1,0:T(8,128)(2,1)S(1)}, bf16[1,512,256]{2,1,0:T(8,128)(2,1)S(1)}, u32[]{:S(2)}, u32[]{:S(2)}) collective-permute-start(bf16[1,512,256]{2,1,0:T(8,128)(2,1)S(1)} %bitcast.373), channel_id=1, source_target_pairs={{0,2},{1,3},{2,0},{3,1},{4,6},{5,7},{6,4},{7,5},{8,10},{9,11},{10,... | collective-permute-start | bytes 786440 | tf_op jit(solution)/shard_map/ppermute | solution.py:448
  148.6 14.5 %collective-permute-start.19 = (bf16[2,128,1024]{2,1,0:T(8,128)(2,1)}, bf16[2,128,1024]{2,1,0:T(8,128)(2,1)}, u32[]{:S(2)}, u32[]{:S(2)}) collective-permute-start(bf16[2,128,1024]{2,1,0:T(8,128)(2,1)} %fusion.21), channel_id=1, source_target_pairs={{0,2},{1,3},{2,0},{3,1},{4,6},{5,7},{6,4},{7,5},{8,10},{9,11},{10,... | collective-permute-start | bytes 1572872 | tf_op jit(solution)/shard_map/ppermute | solution.py:448
  173.4 95.2 %collective-permute-start.21 = (bf16[2,128,1024]{2,1,0:T(8,128)(2,1)}, bf16[2,128,1024]{2,1,0:T(8,128)(2,1)}, u32[]{:S(2)}, u32[]{:S(2)}) collective-permute-start(bf16[2,128,1024]{2,1,0:T(8,128)(2,1)} %dynamic-slice_bitcast_fusion.2), channel_id=1, source_target_pairs={{0,1},{1,0},{2,3},{3,2},{4,5},{5,4},{6,7},{7,6},{8,9},{9,8},{10,11... | collective-permute-start | bytes 1572872 | tf_op jit(solution)/shard_map/ppermute | solution.py:448
  201.4 18.7 %collective-permute-start.29 = (bf16[1,2,64,1152]{3,2,1,0:T(8,128)(2,1)S(1)}, bf16[1,2,64,1152]{3,2,1,0:T(8,128)(2,1)S(1)}, u32[]{:S(2)}, u32[]{:S(2)}) collective-permute-start(bf16[1,2,64,1152]{3,2,1,0:T(8,128)(2,1)S(1)} %get-tuple-element.145), channel_id=1, source_target_pairs={{0,24},{4,28},{8,16},{12,20},{16,8},{20,12},{24,0},{28,4},{1,25},{... | collective-permute-start | bytes 884744 | tf_op jit(solution)/shard_map/ppermute | solution.py:448
  205.9 49.4 %collective-permute-start.28 = (bf16[1,2,64,1152]{3,2,1,0:T(8,128)(2,1)S(1)}, bf16[1,2,64,1152]{3,2,1,0:T(8,128)(2,1)S(1)}, u32[]{:S(2)}, u32[]{:S(2)}) collective-permute-start(bf16[1,2,64,1152]{3,2,1,0:T(8,128)(2,1)S(1)} %get-tuple-element.146), channel_id=1, source_target_pairs={{0,16},{4,20},{8,24},{12,28},{16,0},{20,4},{24,8},{28,12},{1,17},{... | collective-permute-start | bytes 884744 | tf_op jit(solution)/shard_map/ppermute | solution.py:448
  217.5 37.9 %collective-permute-start.27 = (bf16[1,2,64,1152]{3,2,1,0:T(8,128)(2,1)S(1)}, bf16[1,2,64,1152]{3,2,1,0:T(8,128)(2,1)S(1)}, u32[]{:S(2)}, u32[]{:S(2)}) collective-permute-start(bf16[1,2,64,1152]{3,2,1,0:T(8,128)(2,1)S(1)} %get-tuple-element.144), channel_id=1, source_target_pairs={{0,8},{4,12},{8,0},{12,4},{16,24},{20,28},{24,16},{28,20},{1,9},{5... | collective-permute-start | bytes 884744 | tf_op jit(solution)/shard_map/ppermute | solution.py:448
  217.6 46.3 %collective-permute-start.23 = (bf16[1,4,64,1152]{3,2,1,0:T(8,128)(2,1)S(1)}, bf16[1,4,64,1152]{3,2,1,0:T(8,128)(2,1)S(1)}, u32[]{:S(2)}, u32[]{:S(2)}) collective-permute-start(bf16[1,4,64,1152]{3,2,1,0:T(8,128)(2,1)S(1)} %dynamic-slice_bitcast_fusion), channel_id=1, source_target_pairs={{0,4},{4,0},{8,12},{12,8},{16,20},{20,16},{24,28},{28,24},{1,5},{5... | collective-permute-start | bytes 1769480 | tf_op jit(solution)/shard_map/ppermute | solution.py:448
  255.5 8.3 %collective-permute-start.30 = (bf16[1,64,1152]{2,1,0:T(8,128)(2,1)S(1)}, bf16[1,64,1152]{2,1,0:T(8,128)(2,1)S(1)}, u32[]{:S(2)}, u32[]{:S(2)}) collective-permute-start(bf16[1,64,1152]{2,1,0:T(8,128)(2,1)S(1)} %fusion.43), channel_id=1, source_target_pairs={{0,4},{4,0},{8,12},{12,8},{16,20},{20,16},{24,28},{28,24},{1,5},{5... | collective-permute-start | bytes 442376 | tf_op jit(solution)/shard_map/ppermute | solution.py:448
  264.1 8.5 %collective-permute-start.26 = (bf16[1,64,1152]{2,1,0:T(8,128)(2,1)S(1)}, bf16[1,64,1152]{2,1,0:T(8,128)(2,1)S(1)}, u32[]{:S(2)}, u32[]{:S(2)}) collective-permute-start(bf16[1,64,1152]{2,1,0:T(8,128)(2,1)S(1)} %get-tuple-element.156), channel_id=1, source_target_pairs={{0,24},{4,28},{8,16},{12,20},{16,8},{20,12},{24,0},{28,4},{1,25},{... | collective-permute-start | bytes 442376 | tf_op jit(solution)/shard_map/ppermute | solution.py:448
  265.6 10.6 %collective-permute-start.25 = (bf16[1,64,1152]{2,1,0:T(8,128)(2,1)S(1)}, bf16[1,64,1152]{2,1,0:T(8,128)(2,1)S(1)}, u32[]{:S(2)}, u32[]{:S(2)}) collective-permute-start(bf16[1,64,1152]{2,1,0:T(8,128)(2,1)S(1)} %get-tuple-element.157), channel_id=1, source_target_pairs={{0,16},{4,20},{8,24},{12,28},{16,0},{20,4},{24,8},{28,12},{1,17},{... | collective-permute-start | bytes 442376 | tf_op jit(solution)/shard_map/ppermute | solution.py:448
  265.6 10.6 %collective-permute-start.24 = (bf16[1,64,1152]{2,1,0:T(8,128)(2,1)S(1)}, bf16[1,64,1152]{2,1,0:T(8,128)(2,1)S(1)}, u32[]{:S(2)}, u32[]{:S(2)}) collective-permute-start(bf16[1,64,1152]{2,1,0:T(8,128)(2,1)S(1)} %get-tuple-element.155), channel_id=1, source_target_pairs={{0,8},{4,12},{8,0},{12,4},{16,24},{20,28},{24,16},{28,20},{1,9},{5... | collective-permute-start | bytes 442376 | tf_op jit(solution)/shard_map/ppermute | solution.py:448
  269.9 9.2 %collective-permute-start.22 = (bf16[1,128,1024]{2,1,0:T(8,128)(2,1)S(1)}, bf16[1,128,1024]{2,1,0:T(8,128)(2,1)S(1)}, u32[]{:S(2)}, u32[]{:S(2)}) collective-permute-start(bf16[1,128,1024]{2,1,0:T(8,128)(2,1)S(1)} %dynamic-slice_convert_fusion.1), channel_id=1, source_target_pairs={{0,2},{1,3},{2,0},{3,1},{4,6},{5,7},{6,4},{7,5},{8,10},{9,11},{10,... | collective-permute-start | bytes 786440 | tf_op jit(solution)/shard_map/ppermute | solution.py:448
  277.1 24.1 %collective-permute-start.31 = (bf16[2,128,1024]{2,1,0:T(8,128)(2,1)}, bf16[2,128,1024]{2,1,0:T(8,128)(2,1)}, u32[]{:S(2)}, u32[]{:S(2)}) collective-permute-start(bf16[2,128,1024]{2,1,0:T(8,128)(2,1)} %dynamic-slice_bitcast_fusion.1), channel_id=1, source_target_pairs={{0,1},{1,0},{2,3},{3,2},{4,5},{5,4},{6,7},{7,6},{8,9},{9,8},{10,11... | collective-permute-start | bytes 1572872 | tf_op jit(solution)/shard_map/ppermute | solution.py:448
  277.1 6.5 %collective-permute-start.33 = (bf16[2,1,32,1152]{3,2,1,0:T(8,128)(2,1)S(1)}, bf16[2,1,32,1152]{3,2,1,0:T(8,128)(2,1)S(1)}, u32[]{:S(2)}, u32[]{:S(2)}) collective-permute-start(bf16[2,1,32,1152]{3,2,1,0:T(8,128)(2,1)S(1)} %get-tuple-element.164), channel_id=1, source_target_pairs={{0,2},{1,3},{2,0},{3,1},{4,6},{5,7},{6,4},{7,5},{8,10},{9,11},{10,... | collective-permute-start | bytes 442376 | tf_op jit(solution)/shard_map/ppermute | solution.py:448
  302.5 6.7 %collective-permute-start.32 = (bf16[1,128,1024]{2,1,0:T(8,128)(2,1)S(1)}, bf16[1,128,1024]{2,1,0:T(8,128)(2,1)S(1)}, u32[]{:S(2)}, u32[]{:S(2)}) collective-permute-start(bf16[1,128,1024]{2,1,0:T(8,128)(2,1)S(1)} %dynamic-slice_convert_fusion), channel_id=1, source_target_pairs={{0,2},{1,3},{2,0},{3,1},{4,6},{5,7},{6,4},{7,5},{8,10},{9,11},{10,... | collective-permute-start | bytes 786440 | tf_op jit(solution)/shard_map/ppermute | solution.py:448
  310.5 6.8 %collective-permute-start.35 = (bf16[2,1,32,2304]{3,2,1,0:T(8,128)(2,1)S(1)}, bf16[2,1,32,2304]{3,2,1,0:T(8,128)(2,1)S(1)}, u32[]{:S(2)}, u32[]{:S(2)}) collective-permute-start(bf16[2,1,32,2304]{3,2,1,0:T(8,128)(2,1)S(1)} %get-tuple-element.149), channel_id=1, source_target_pairs={{0,2},{1,3},{2,0},{3,1},{4,6},{5,7},{6,4},{7,5},{8,10},{9,11},{10,... | collective-permute-start | bytes 884744 | tf_op jit(solution)/shard_map/ppermute | solution.py:448
  (89 other events, 492.2 us)
Sparse Core Ops, SparseCore 0:
  34.7 100.8 all-gather.1
  168.8 130.9 reduce-scatter.1

commit v4 on v3

--- a/solution.py
+++ b/solution.py
@@ -724,8 +724,10 @@
     normed = (unit * norm_gain).astype(BF)
     px = dot(normed, full_in)
     px, out_away = lax.optimization_barrier((px, full_out))
-    outs_near = near_pieces(out_away, "ctx")
+    out_far = swap(out_away, "ctx", 2)
     mixed, *saved = core_fwd(px, taps, par, pos, head_gain[None, :])
+    mixed, out_far = lax.optimization_barrier((mixed, out_far))
+    outs_near = [out_away, swap(out_away, "ctx", 1), out_far, swap(out_far, "ctx", 1)]
     branch = 0.0
     for piece, weight in zip(near_pieces(mixed, "ctx"), outs_near):
         branch = branch + dot(piece, weight, 1, 1)
@@ -747,12 +749,11 @@
     d_gain_two = jnp.sum(d_two * unit_two, axis=0)
     low, high = me % 2, me // 2
     grid = (2, 2, length, D)
-    pairs = d_two.astype(BF).reshape(grid)
+    grad_mlp = mlp_grad(normed_two, g_mlp, d_hgate, d_hup, hidden)
+    pairs, _ = lax.optimization_barrier((d_two.astype(BF).reshape(grid), grad_mlp))
     got = swap(take(pairs, 1 - low, 1), "ctx", 1)
     column = take(pairs, low, 1).astype(F32) + got.astype(F32)
-    grad_mlp = mlp_grad(normed_two, g_mlp, d_hgate, d_hup, hidden)
-    met, _ = lax.optimization_barrier((swap(column.astype(BF), "ctx", 2), grad_mlp))
-    d_two_col = column + met.astype(F32)
+    d_two_col = column + swap(column.astype(BF), "ctx", 2).astype(F32)
     resid_col = take(resid.reshape(grid), low, 1)
     cot_col = take(cot_full.reshape(grid), low, 1).astype(F32)
     inv_col = lax.rsqrt(jnp.mean(resid_col * resid_col, -1, keepdims=True) + NORM_EPS)

time: 336 us -> 331 us (0.985)
  starting transfers between devices: 56.8 us -> 44 us
  waiting for transfers between devices: 124 us -> 134 us
  other arithmetic: 34.8 us -> 30 us
    ppermute x42 -> x43, starting transfers between devices: 56.5 us -> 43.7 us  [swap(): return lax.ppermute(value, axis, [(i, i ^ mask) for i in range(count)])]
    all_gather x1, waiting for transfers between devices: 0.02 us -> 11.5 us  [local(): full_mlp = lax.all_gather(w_mlp, 'dp', axis=0, tiled=True)]
    ppermute x42 -> x43, waiting for transfers between devices: 124 us -> 123 us  [swap(): return lax.ppermute(value, axis, [(i, i ^ mask) for i in range(count)])]
    unnamed x171 -> x167, local copies, waits for them, and re-layouts: 13.2 us -> 13.9 us
  transfers between devices with their start and end apart: 44 -> 45, of which waited for: 23 -> 23; matrix products, arithmetic and copies ran while one was open for 15% -> 13% of each run, Pallas kernels for 15% -> 13%
where the time goes in v4:
time: 331 us; the launch traced here: 327 us
  waiting for transfers between devices  134 us (40%)
  Pallas kernels  48.9 us (15%)
  starting transfers between devices  44 us (13%)
  local copies, waits for them, and re-layouts  31.5 us (10%)
  other arithmetic  30 us (9%)
  matrix products  21.5 us (6%)
  between operations  16.9 us (5%)
    ppermute x43, waiting for transfers between devices, swap(): return lax.ppermute(value, axis, [(i, i ^ mask) for i in range(count)])  123 us
    ppermute x43, starting transfers between devices, swap(): return lax.ppermute(value, axis, [(i, i ^ mask) for i in range(count)])  43.7 us
    dot_general x13, matrix products, dot(): lax.dot_general(a, b, (((lhs,), (rhs,)), ((), ())), preferred_element_typ...  21.5 us
    pallas_call x1, Pallas kernels, core_fwd(): pl.pallas_call(core_fwd_kernel, name='core_fwd', out_shape=(shape((rows,...  21.2 us
    pallas_call x1, Pallas kernels, core_bwd(): pl.pallas_call(core_bwd_kernel, name='core_bwd', out_shape=(shape((rows,...  16.5 us
    unnamed x167, local copies, waits for them, and re-layouts  13.9 us
    all_gather x1, waiting for transfers between devices, local(): full_mlp = lax.all_gather(w_mlp, 'dp', axis=0, tiled=True)  11.5 us
    sub x7, other arithmetic, adamw(): weights - learn_rate * (corrected / (jnp.sqrt(scaled) + adam_eps) + weigh...  7.97 us
  transfers between devices with their start and end apart: 45, of which 23 were waited for; matrix products, arithmetic and copies ran while one was open for 13% of the time, Pallas kernels for 13%

profile of v4, /device:TPU:0, one launch (start us, length us, event | category | flops | bytes accessed | tf_op | source)
XLA Modules:
  0.0 327.0 jit_solution(579541131911585938)
XLA Ops:
  10.3 3.1 collective-permute-start
  18.4 5.1 %collective-permute-done.2 = bf16[2,1,32,1152]{3,2,1,0:T(8,128)(2,1)S(1)} collective-permute-done((bf16[2,1,32,1152]{3,2,1,0:T(8,128)(2,1)S(1)}, bf16[2,1,32,1152]{3,2,1,0:T(8,128)(2,1)S(1)}, u32[]{:S(2)}, u32[]{:S(2)}) %collective-permute-start.2) | collective-permute-done | bytes 147488 | tf_op jit(solution)/shard_map/ppermute | solution.py:448
  28.4 2.6 collective-permute-start.7
  34.9 3.6 %collective-permute-done.10 = bf16[1,64,1152]{2,1,0:T(8,128)(2,1)} collective-permute-done((bf16[1,64,1152]{2,1,0:T(8,128)(2,1)}, bf16[1,64,1152]{2,1,0:T(8,128)(2,1)}, u32[]{:S(2)}, u32[]{:S(2)}) %collective-permute-start.10) | collective-permute-done | bytes 147488 | tf_op jit(solution)/shard_map/ppermute | solution.py:448
  40.2 3.5 %collective-permute-start.12 = (bf16[1,2,64,1152]{3,2,1,0:T(8,128)(2,1)S(1)}, bf16[1,2,64,1152]{3,2,1,0:T(8,128)(2,1)S(1)}, u32[]{:S(2)}, u32[]{:S(2)}) collective-permute-start(bf16[1,2,64,1152]{3,2,1,0:T(8,128)(2,1)S(1)} %bitcast_dynamic-update-slice_fusion.8), channel_id=1, source_target_pairs={{0,16},{4,20},{8,24},{12,28},{16,0},{20,4},{24,8},{28,12},{1,17},{... | collective-permute-start | bytes 884744 | tf_op jit(solution)/shard_map/ppermute | solution.py:448
  51.1 12.7 %collective-permute-done.9 = bf16[1,4,64,1152]{3,2,1,0:T(8,128)(2,1)S(1)} collective-permute-done((bf16[1,4,64,1152]{3,2,1,0:T(8,128)(2,1)S(1)}, bf16[1,4,64,1152]{3,2,1,0:T(8,128)(2,1)S(1)}, u32[]{:S(2)}, u32[]{:S(2)}) %collective-permute-start.9) | collective-permute-done | bytes 589856 | tf_op jit(solution)/shard_map/ppermute | solution.py:448
  64.0 14.3 %collective-permute-done.12 = bf16[1,2,64,1152]{3,2,1,0:T(8,128)(2,1)S(1)} collective-permute-done((bf16[1,2,64,1152]{3,2,1,0:T(8,128)(2,1)S(1)}, bf16[1,2,64,1152]{3,2,1,0:T(8,128)(2,1)S(1)}, u32[]{:S(2)}, u32[]{:S(2)}) %collective-permute-start.12) | collective-permute-done | bytes 294944 | tf_op jit(solution)/shard_map/ppermute | solution.py:448
  89.0 21.2 %core_fwd.1 = (bf16[512,256]{1,0:T(8,128)(2,1)S(1)}, f32[8,128,256]{2,1,0:T(8,128)S(1)}, f32[512,256]{1,0:T(8,128)S(1)}, f32[512,256]{1,0:T(8,128)S(1)}, f32[512...) custom-call(f32[512,896]{1,0:T(8,128)S(1)} %fusion.7.px_ref, ...), custom_call_target="tpu_custom_call" | custom-call | tf_op jit(solution)/shard_map/core_fwd/pallas_call | solution.py:308
  111.0 5.7 %collective-permute-done.15 = bf16[1,512,256]{2,1,0:T(8,128)(2,1)S(1)} collective-permute-done((bf16[1,512,256]{2,1,0:T(8,128)(2,1)S(1)}, bf16[1,512,256]{2,1,0:T(8,128)(2,1)S(1)}, u32[]{:S(2)}, u32[]{:S(2)}) %collective-permute-start.15) | collective-permute-done | bytes 262176 | tf_op jit(solution)/shard_map/ppermute | solution.py:448
  124.1 11.5 %all-gather.2.cloned.1.call-done = bf16[1024,2304]{1,0:T(8,128)(2,1)} async-done(((bf16[128,2304]{1,0:T(8,128)(2,1)}), bf16[1024,2304]{1,0:T(8,128)(2,1)}) %all-gather.2.cloned.1.call-update) | async-done | bytes 4718608 | tf_op jit(solution)/shard_map/all_gather | solution.py:696
  135.6 2.5 fusion.18
  141.1 5.4 %mlp_grad.1 = bf16[1024,2304]{1,0:T(8,128)(2,1)S(1)} custom-call(bf16[512,1024]{1,0:T(8,128)(2,1)S(1)} %multiply_convert_fusion.1.two_ref, bf16[512,1024]{1,0:T(8,128)(2,1)S(1)} %get-tuple-element.134.cot_ref, bf16[512,768]{1,0:T(8,128)(2,1)S(1)} %get-tuple-element.126.dg_ref, bf16[512,768]{1,0:T(8,128)(2,1)S(1)} %get-tuple-element.125.du_ref, ...), custom_call_target="tpu_custom_call" | custom-call | tf_op jit(solution)/shard_map/mlp_grad/pallas_call | solution.py:387
  150.5 2.8 fusion.16
  153.3 2.5 multiply_reduce_fusion
  162.0 11.2 %collective-permute-done.20 = bf16[2,128,1024]{2,1,0:T(8,128)(2,1)} collective-permute-done((bf16[2,128,1024]{2,1,0:T(8,128)(2,1)}, bf16[2,128,1024]{2,1,0:T(8,128)(2,1)}, u32[]{:S(2)}, u32[]{:S(2)}) %collective-permute-start.20) | collective-permute-done | bytes 524320 | tf_op jit(solution)/shard_map/ppermute | solution.py:448
  174.7 2.7 bitcast_dynamic-update-slice_fusion.3
  178.6 2.6 convolution_convert_fusion
  184.1 16.5 %core_bwd.1 = (bf16[512,896]{1,0:T(8,128)(2,1)S(1)}, f32[4,512]{1,0:T(4,128)S(1)}, f32[1,256]{1,0:T(1,128)S(1)}, f32[1,128]{1,0:T(1,128)S(1)}) custom-call(f32[512,896]{1,0:T(8,128)} %copy-done.1, f32[4,512]{1,0:T(4,128)S(1)} %pad_maximum_fusion.6.taps_ref, f32[2]{0:T(128)S(1)} %pad_maximum_fusion.8.par_ref, s32[512,1]{1,0:T(8,128)S(1)} %iota_subtract_fusion.pos_ref, ...), custom_call_target="tpu_custom_call" | custom-call | tf_op jit(solution)/shard_map/core_bwd/pallas_call | solution.py:332
  200.7 2.3 fusion.79
  204.5 5.8 %mix_grad.1 = bf16[1024,1152]{1,0:T(8,128)(2,1)S(1)} custom-call(bf16[512,1024]{1,0:T(8,128)(2,1)S(1)} %copy-done.3, bf16[512,896]{1,0:T(8,128)(2,1)S(1)} %copy-done.7, bf16[512,1024]{1,0:T(8,128)(2,1)S(1)} %bitcast.361, bf16[512,256]{1,0:T(8,128)(2,1)S(1)} %get-tuple-element.65.mixed_ref, f32[1024,128]{1,0:T(8,128)S(1)} %bitcast.364), custom_call_target="tpu_custom_call" | custom-call | tf_op jit(solution)/shard_map/mix_grad/pallas_call | solution.py:428
  212.8 2.3 collective-permute-start.28
  216.1 12.5 %collective-permute-done.30 = bf16[1,2,64,1152]{3,2,1,0:T(8,128)(2,1)S(1)} collective-permute-done((bf16[1,2,64,1152]{3,2,1,0:T(8,128)(2,1)S(1)}, bf16[1,2,64,1152]{3,2,1,0:T(8,128)(2,1)S(1)}, u32[]{:S(2)}, u32[]{:S(2)}) %collective-permute-start.30) | collective-permute-done | bytes 294944 | tf_op jit(solution)/shard_map/ppermute | solution.py:448
  228.6 20.8 %collective-permute-done.29 = bf16[1,2,64,1152]{3,2,1,0:T(8,128)(2,1)S(1)} collective-permute-done((bf16[1,2,64,1152]{3,2,1,0:T(8,128)(2,1)S(1)}, bf16[1,2,64,1152]{3,2,1,0:T(8,128)(2,1)S(1)}, u32[]{:S(2)}, u32[]{:S(2)}) %collective-permute-start.29) | collective-permute-done | bytes 294944 | tf_op jit(solution)/shard_map/ppermute | solution.py:448
  252.5 6.2 %collective-permute-done.31 = bf16[1,64,1152]{2,1,0:T(8,128)(2,1)S(1)} collective-permute-done((bf16[1,64,1152]{2,1,0:T(8,128)(2,1)S(1)}, bf16[1,64,1152]{2,1,0:T(8,128)(2,1)S(1)}, u32[]{:S(2)}, u32[]{:S(2)}) %collective-permute-start.31) | collective-permute-done | bytes 147488 | tf_op jit(solution)/shard_map/ppermute | solution.py:448
  260.7 2.7 collective-permute-start.25
  267.7 4.8 %collective-permute-done.26 = bf16[1,64,1152]{2,1,0:T(8,128)(2,1)S(1)} collective-permute-done((bf16[1,64,1152]{2,1,0:T(8,128)(2,1)S(1)}, bf16[1,64,1152]{2,1,0:T(8,128)(2,1)S(1)}, u32[]{:S(2)}, u32[]{:S(2)}) %collective-permute-start.26) | collective-permute-done | bytes 147488 | tf_op jit(solution)/shard_map/ppermute | solution.py:448
  276.9 2.9 collective-permute-done.34
  287.7 3.4 %collective-permute-done.40 = f32[264]{0:T(512)S(1)} collective-permute-done((f32[264]{0:T(512)S(1)}, f32[264]{0:T(512)S(1)}, u32[]{:S(2)}, u32[]{:S(2)}) %collective-permute-start.40) | collective-permute-done | bytes 1088 | tf_op jit(solution)/shard_map/ppermute | solution.py:448
  291.6 3.0 collective-permute-done.41
  300.1 4.0 %collective-permute-done.33 = bf16[1,128,1024]{2,1,0:T(8,128)(2,1)S(1)} collective-permute-done((bf16[1,128,1024]{2,1,0:T(8,128)(2,1)S(1)}, bf16[1,128,1024]{2,1,0:T(8,128)(2,1)S(1)}, u32[]{:S(2)}, u32[]{:S(2)}) %collective-permute-start.33) | collective-permute-done | bytes 262176 | tf_op jit(solution)/shard_map/ppermute | solution.py:448
  307.8 4.5 %collective-permute-done.36 = bf16[2,1,32,2304]{3,2,1,0:T(8,128)(2,1)S(1)} collective-permute-done((bf16[2,1,32,2304]{3,2,1,0:T(8,128)(2,1)S(1)}, bf16[2,1,32,2304]{3,2,1,0:T(8,128)(2,1)S(1)}, u32[]{:S(2)}, u32[]{:S(2)}) %collective-permute-start.36) | collective-permute-done | bytes 294944 | tf_op jit(solution)/shard_map/ppermute | solution.py:448
  316.9 3.0 multiply_subtract_fusion.2
  (411 shorter events, 102.5 us)
Async XLA Ops:
  7.2 128.4 %all-gather.2.cloned.1.call-start = ((), (), s32[]{:S(2)}) async-start(), calls=%async_computation.1 | async-start | bytes 5308416 | tf_op jit(solution)/shard_map/all_gather | solution.py:696
  10.3 13.4 %collective-permute-start = (bf16[2,1,32,2304]{3,2,1,0:T(8,128)(2,1)S(1)}, bf16[2,1,32,2304]{3,2,1,0:T(8,128)(2,1)S(1)}, u32[]{:S(2)}, u32[]{:S(2)}) collective-permute-start(bf16[2,1,32,2304]{3,2,1,0:T(8,128)(2,1)S(1)} %get-tuple-element.164), channel_id=1, source_target_pairs={{0,2},{1,3},{2,0},{3,1},{4,6},{5,7},{6,4},{7,5},{8,10},{9,11},{10,... | collective-permute-start | bytes 884744 | tf_op jit(solution)/shard_map/ppermute | solution.py:448
  14.3 9.2 %collective-permute-start.2 = (bf16[2,1,32,1152]{3,2,1,0:T(8,128)(2,1)S(1)}, bf16[2,1,32,1152]{3,2,1,0:T(8,128)(2,1)S(1)}, u32[]{:S(2)}, u32[]{:S(2)}) collective-permute-start(bf16[2,1,32,1152]{3,2,1,0:T(8,128)(2,1)S(1)} %get-tuple-element.176), channel_id=1, source_target_pairs={{0,2},{1,3},{2,0},{3,1},{4,6},{5,7},{6,4},{7,5},{8,10},{9,11},{10,... | collective-permute-start | bytes 442376 | tf_op jit(solution)/shard_map/ppermute | solution.py:448
  26.6 13.6 %collective-permute-start.6 = (bf16[1,64,1152]{2,1,0:T(8,128)(2,1)}, bf16[1,64,1152]{2,1,0:T(8,128)(2,1)}, u32[]{:S(2)}, u32[]{:S(2)}) collective-permute-start(bf16[1,64,1152]{2,1,0:T(8,128)(2,1)} %get-tuple-element.171), channel_id=1, source_target_pairs={{0,8},{4,12},{8,0},{12,4},{16,24},{20,28},{24,16},{28,20},{1,9},{5... | collective-permute-start | bytes 442376 | tf_op jit(solution)/shard_map/ppermute | solution.py:448
  28.4 16.3 %collective-permute-start.7 = (bf16[1,64,1152]{2,1,0:T(8,128)(2,1)}, bf16[1,64,1152]{2,1,0:T(8,128)(2,1)}, u32[]{:S(2)}, u32[]{:S(2)}) collective-permute-start(bf16[1,64,1152]{2,1,0:T(8,128)(2,1)} %get-tuple-element.171), channel_id=1, source_target_pairs={{0,16},{4,20},{8,24},{12,28},{16,0},{20,4},{24,8},{28,12},{1,17},{... | collective-permute-start | bytes 442376 | tf_op jit(solution)/shard_map/ppermute | solution.py:448
  31.0 15.1 %collective-permute-start.8 = (bf16[1,64,1152]{2,1,0:T(8,128)(2,1)}, bf16[1,64,1152]{2,1,0:T(8,128)(2,1)}, u32[]{:S(2)}, u32[]{:S(2)}) collective-permute-start(bf16[1,64,1152]{2,1,0:T(8,128)(2,1)} %get-tuple-element.171), channel_id=1, source_target_pairs={{0,24},{4,28},{8,16},{12,20},{16,8},{20,12},{24,0},{28,4},{1,25},{... | collective-permute-start | bytes 442376 | tf_op jit(solution)/shard_map/ppermute | solution.py:448
  31.3 17.7 %collective-permute-start.4 = (bf16[1,128,2048]{2,1,0:T(8,128)(2,1)S(1)}, bf16[1,128,2048]{2,1,0:T(8,128)(2,1)}, u32[]{:S(2)}, u32[]{:S(2)}) collective-permute-start(bf16[1,128,2048]{2,1,0:T(8,128)(2,1)S(1)} %bitcast.381), channel_id=1, source_target_pairs={{0,2},{1,3},{2,0},{3,1},{4,6},{5,7},{6,4},{7,5},{8,10},{9,11},{10,... | collective-permute-start | bytes 1572872 | tf_op jit(solution)/shard_map/ppermute | solution.py:448
  34.6 269.7 %reduce-scatter.2.cloned.1.call-start = ((), (), s32[]{:S(2)}) async-start(), calls=%async_computation.2 | async-start | bytes 5308416 | tf_op jit(solution)/shard_map/reduce_scatter | solution.py:796
  39.5 24.5 %collective-permute-start.11 = (bf16[1,2,64,1152]{3,2,1,0:T(8,128)(2,1)S(1)}, bf16[1,2,64,1152]{3,2,1,0:T(8,128)(2,1)S(1)}, u32[]{:S(2)}, u32[]{:S(2)}) collective-permute-start(bf16[1,2,64,1152]{3,2,1,0:T(8,128)(2,1)S(1)} %bitcast_dynamic-update-slice_fusion.8), channel_id=1, source_target_pairs={{0,8},{4,12},{8,0},{12,4},{16,24},{20,28},{24,16},{28,20},{1,9},{5... | collective-permute-start | bytes 884744 | tf_op jit(solution)/shard_map/ppermute | solution.py:448
  40.2 38.1 %collective-permute-start.12 = (bf16[1,2,64,1152]{3,2,1,0:T(8,128)(2,1)S(1)}, bf16[1,2,64,1152]{3,2,1,0:T(8,128)(2,1)S(1)}, u32[]{:S(2)}, u32[]{:S(2)}) collective-permute-start(bf16[1,2,64,1152]{3,2,1,0:T(8,128)(2,1)S(1)} %bitcast_dynamic-update-slice_fusion.8), channel_id=1, source_target_pairs={{0,16},{4,20},{8,24},{12,28},{16,0},{20,4},{24,8},{28,12},{1,17},{... | collective-permute-start | bytes 884744 | tf_op jit(solution)/shard_map/ppermute | solution.py:448
  44.6 33.7 %collective-permute-start.13 = (bf16[1,2,64,1152]{3,2,1,0:T(8,128)(2,1)S(1)}, bf16[1,2,64,1152]{3,2,1,0:T(8,128)(2,1)S(1)}, u32[]{:S(2)}, u32[]{:S(2)}) collective-permute-start(bf16[1,2,64,1152]{3,2,1,0:T(8,128)(2,1)S(1)} %bitcast_dynamic-update-slice_fusion.8), channel_id=1, source_target_pairs={{0,24},{4,28},{8,16},{12,20},{16,8},{20,12},{24,0},{28,4},{1,25},{... | collective-permute-start | bytes 884744 | tf_op jit(solution)/shard_map/ppermute | solution.py:448
  47.0 16.8 %collective-permute-start.9 = (bf16[1,4,64,1152]{3,2,1,0:T(8,128)(2,1)S(1)}, bf16[1,4,64,1152]{3,2,1,0:T(8,128)(2,1)S(1)}, u32[]{:S(2)}, u32[]{:S(2)}) collective-permute-start(bf16[1,4,64,1152]{3,2,1,0:T(8,128)(2,1)S(1)} %bitcast_dynamic-update-slice_fusion.10), channel_id=1, source_target_pairs={{0,4},{4,0},{8,12},{12,8},{16,20},{20,16},{24,28},{28,24},{1,5},{5... | collective-permute-start | bytes 1769480 | tf_op jit(solution)/shard_map/ppermute | solution.py:448
  51.1 29.7 %collective-permute-start.5 = (bf16[2,128,2048]{2,1,0:T(8,128)(2,1)}, bf16[2,128,2048]{2,1,0:T(8,128)(2,1)S(1)}, u32[]{:S(2)}, u32[]{:S(2)}) collective-permute-start(bf16[2,128,2048]{2,1,0:T(8,128)(2,1)} %pad_maximum_fusion), channel_id=1, source_target_pairs={{0,1},{1,0},{2,3},{3,2},{4,5},{5,4},{6,7},{7,6},{8,9},{9,8},{10,11... | collective-permute-start | bytes 3145736 | tf_op jit(solution)/shard_map/ppermute | solution.py:448
  86.9 23.4 %collective-permute-start.14 = (bf16[1024,256]{1,0:T(8,128)(2,1)}, bf16[1024,256]{1,0:T(8,128)(2,1)}, u32[]{:S(2)}, u32[]{:S(2)}) collective-permute-start(bf16[1024,256]{1,0:T(8,128)(2,1)} %slice.676), channel_id=1, source_target_pairs={{0,2},{1,3},{2,0},{3,1},{4,6},{5,7},{6,4},{7,5},{8,10},{9,11},{10,... | collective-permute-start | bytes 1572872 | tf_op jit(solution)/shard_map/ppermute | solution.py:448
  110.3 6.4 %collective-permute-start.15 = (bf16[1,512,256]{2,1,0:T(8,128)(2,1)S(1)}, bf16[1,512,256]{2,1,0:T(8,128)(2,1)S(1)}, u32[]{:S(2)}, u32[]{:S(2)}) collective-permute-start(bf16[1,512,256]{2,1,0:T(8,128)(2,1)S(1)} %bitcast.362), channel_id=1, source_target_pairs={{0,2},{1,3},{2,0},{3,1},{4,6},{5,7},{6,4},{7,5},{8,10},{9,11},{10,... | collective-permute-start | bytes 786440 | tf_op jit(solution)/shard_map/ppermute | solution.py:448
  110.5 9.5 %collective-permute-start.17 = (bf16[1024,256]{1,0:T(8,128)(2,1)}, bf16[1024,256]{1,0:T(8,128)(2,1)S(1)}, u32[]{:S(2)}, u32[]{:S(2)}) collective-permute-start(bf16[1024,256]{1,0:T(8,128)(2,1)} %slice.676), channel_id=1, source_target_pairs={{0,1},{1,0},{2,3},{3,2},{4,5},{5,4},{6,7},{7,6},{8,9},{9,8},{10,11... | collective-permute-start | bytes 1572872 | tf_op jit(solution)/shard_map/ppermute | solution.py:448
  110.5 10.0 %collective-permute-start.18 = (bf16[1024,256]{1,0:T(8,128)(2,1)}, bf16[1024,256]{1,0:T(8,128)(2,1)S(1)}, u32[]{:S(2)}, u32[]{:S(2)}) collective-permute-start(bf16[1024,256]{1,0:T(8,128)(2,1)} %collective-permute-done.14), channel_id=1, source_target_pairs={{0,1},{1,0},{2,3},{3,2},{4,5},{5,4},{6,7},{7,6},{8,9},{9,8},{10,11... | collective-permute-start | bytes 1572872 | tf_op jit(solution)/shard_map/ppermute | solution.py:448
  158.9 14.3 %collective-permute-start.20 = (bf16[2,128,1024]{2,1,0:T(8,128)(2,1)}, bf16[2,128,1024]{2,1,0:T(8,128)(2,1)}, u32[]{:S(2)}, u32[]{:S(2)}) collective-permute-start(bf16[2,128,1024]{2,1,0:T(8,128)(2,1)} %fusion.21), channel_id=1, source_target_pairs={{0,2},{1,3},{2,0},{3,1},{4,6},{5,7},{6,4},{7,5},{8,10},{9,11},{10,... | collective-permute-start | bytes 1572872 | tf_op jit(solution)/shard_map/ppermute | solution.py:448
  182.3 81.2 %collective-permute-start.22 = (bf16[2,128,1024]{2,1,0:T(8,128)(2,1)}, bf16[2,128,1024]{2,1,0:T(8,128)(2,1)}, u32[]{:S(2)}, u32[]{:S(2)}) collective-permute-start(bf16[2,128,1024]{2,1,0:T(8,128)(2,1)} %dynamic-slice_bitcast_fusion.2), channel_id=1, source_target_pairs={{0,1},{1,0},{2,3},{3,2},{4,5},{5,4},{6,7},{7,6},{8,9},{9,8},{10,11... | collective-permute-start | bytes 1572872 | tf_op jit(solution)/shard_map/ppermute | solution.py:448
  210.6 18.1 %collective-permute-start.30 = (bf16[1,2,64,1152]{3,2,1,0:T(8,128)(2,1)S(1)}, bf16[1,2,64,1152]{3,2,1,0:T(8,128)(2,1)S(1)}, u32[]{:S(2)}, u32[]{:S(2)}) collective-permute-start(bf16[1,2,64,1152]{3,2,1,0:T(8,128)(2,1)S(1)} %get-tuple-element.149), channel_id=1, source_target_pairs={{0,24},{4,28},{8,16},{12,20},{16,8},{20,12},{24,0},{28,4},{1,25},{... | collective-permute-start | bytes 884744 | tf_op jit(solution)/shard_map/ppermute | solution.py:448
  212.0 37.4 %collective-permute-start.29 = (bf16[1,2,64,1152]{3,2,1,0:T(8,128)(2,1)S(1)}, bf16[1,2,64,1152]{3,2,1,0:T(8,128)(2,1)S(1)}, u32[]{:S(2)}, u32[]{:S(2)}) collective-permute-start(bf16[1,2,64,1152]{3,2,1,0:T(8,128)(2,1)S(1)} %get-tuple-element.150), channel_id=1, source_target_pairs={{0,16},{4,20},{8,24},{12,28},{16,0},{20,4},{24,8},{28,12},{1,17},{... | collective-permute-start | bytes 884744 | tf_op jit(solution)/shard_map/ppermute | solution.py:448
  212.8 36.7 %collective-permute-start.28 = (bf16[1,2,64,1152]{3,2,1,0:T(8,128)(2,1)S(1)}, bf16[1,2,64,1152]{3,2,1,0:T(8,128)(2,1)S(1)}, u32[]{:S(2)}, u32[]{:S(2)}) collective-permute-start(bf16[1,2,64,1152]{3,2,1,0:T(8,128)(2,1)S(1)} %get-tuple-element.148), channel_id=1, source_target_pairs={{0,8},{4,12},{8,0},{12,4},{16,24},{20,28},{24,16},{28,20},{1,9},{5... | collective-permute-start | bytes 884744 | tf_op jit(solution)/shard_map/ppermute | solution.py:448
  215.1 43.7 %collective-permute-start.24 = (bf16[1,4,64,1152]{3,2,1,0:T(8,128)(2,1)S(1)}, bf16[1,4,64,1152]{3,2,1,0:T(8,128)(2,1)S(1)}, u32[]{:S(2)}, u32[]{:S(2)}) collective-permute-start(bf16[1,4,64,1152]{3,2,1,0:T(8,128)(2,1)S(1)} %dynamic-slice_bitcast_fusion), channel_id=1, source_target_pairs={{0,4},{4,0},{8,12},{12,8},{16,20},{20,16},{24,28},{28,24},{1,5},{5... | collective-permute-start | bytes 1769480 | tf_op jit(solution)/shard_map/ppermute | solution.py:448
  249.6 9.1 %collective-permute-start.31 = (bf16[1,64,1152]{2,1,0:T(8,128)(2,1)S(1)}, bf16[1,64,1152]{2,1,0:T(8,128)(2,1)S(1)}, u32[]{:S(2)}, u32[]{:S(2)}) collective-permute-start(bf16[1,64,1152]{2,1,0:T(8,128)(2,1)S(1)} %fusion.42), channel_id=1, source_target_pairs={{0,4},{4,0},{8,12},{12,8},{16,20},{20,16},{24,28},{28,24},{1,5},{5... | collective-permute-start | bytes 442376 | tf_op jit(solution)/shard_map/ppermute | solution.py:448
  259.0 8.7 %collective-permute-start.27 = (bf16[1,64,1152]{2,1,0:T(8,128)(2,1)S(1)}, bf16[1,64,1152]{2,1,0:T(8,128)(2,1)S(1)}, u32[]{:S(2)}, u32[]{:S(2)}) collective-permute-start(bf16[1,64,1152]{2,1,0:T(8,128)(2,1)S(1)} %get-tuple-element.160), channel_id=1, source_target_pairs={{0,24},{4,28},{8,16},{12,20},{16,8},{20,12},{24,0},{28,4},{1,25},{... | collective-permute-start | bytes 442376 | tf_op jit(solution)/shard_map/ppermute | solution.py:448
  260.7 11.7 %collective-permute-start.26 = (bf16[1,64,1152]{2,1,0:T(8,128)(2,1)S(1)}, bf16[1,64,1152]{2,1,0:T(8,128)(2,1)S(1)}, u32[]{:S(2)}, u32[]{:S(2)}) collective-permute-start(bf16[1,64,1152]{2,1,0:T(8,128)(2,1)S(1)} %get-tuple-element.161), channel_id=1, source_target_pairs={{0,16},{4,20},{8,24},{12,28},{16,0},{20,4},{24,8},{28,12},{1,17},{... | collective-permute-start | bytes 442376 | tf_op jit(solution)/shard_map/ppermute | solution.py:448
  260.7 11.7 %collective-permute-start.25 = (bf16[1,64,1152]{2,1,0:T(8,128)(2,1)S(1)}, bf16[1,64,1152]{2,1,0:T(8,128)(2,1)S(1)}, u32[]{:S(2)}, u32[]{:S(2)}) collective-permute-start(bf16[1,64,1152]{2,1,0:T(8,128)(2,1)S(1)} %get-tuple-element.159), channel_id=1, source_target_pairs={{0,8},{4,12},{8,0},{12,4},{16,24},{20,28},{24,16},{28,20},{1,9},{5... | collective-permute-start | bytes 442376 | tf_op jit(solution)/shard_map/ppermute | solution.py:448
  264.7 10.3 %collective-permute-start.23 = (bf16[1,128,1024]{2,1,0:T(8,128)(2,1)S(1)}, bf16[1,128,1024]{2,1,0:T(8,128)(2,1)S(1)}, u32[]{:S(2)}, u32[]{:S(2)}) collective-permute-start(bf16[1,128,1024]{2,1,0:T(8,128)(2,1)S(1)} %dynamic-slice_convert_fusion.1), channel_id=1, source_target_pairs={{0,2},{1,3},{2,0},{3,1},{4,6},{5,7},{6,4},{7,5},{8,10},{9,11},{10,... | collective-permute-start | bytes 786440 | tf_op jit(solution)/shard_map/ppermute | solution.py:448
  273.4 22.9 %collective-permute-start.32 = (bf16[2,128,1024]{2,1,0:T(8,128)(2,1)}, bf16[2,128,1024]{2,1,0:T(8,128)(2,1)}, u32[]{:S(2)}, u32[]{:S(2)}) collective-permute-start(bf16[2,128,1024]{2,1,0:T(8,128)(2,1)} %dynamic-slice_bitcast_fusion.1), channel_id=1, source_target_pairs={{0,1},{1,0},{2,3},{3,2},{4,5},{5,4},{6,7},{7,6},{8,9},{9,8},{10,11... | collective-permute-start | bytes 1572872 | tf_op jit(solution)/shard_map/ppermute | solution.py:448
  273.5 6.3 %collective-permute-start.34 = (bf16[2,1,32,1152]{3,2,1,0:T(8,128)(2,1)S(1)}, bf16[2,1,32,1152]{3,2,1,0:T(8,128)(2,1)S(1)}, u32[]{:S(2)}, u32[]{:S(2)}) collective-permute-start(bf16[2,1,32,1152]{3,2,1,0:T(8,128)(2,1)S(1)} %get-tuple-element.168), channel_id=1, source_target_pairs={{0,2},{1,3},{2,0},{3,1},{4,6},{5,7},{6,4},{7,5},{8,10},{9,11},{10,... | collective-permute-start | bytes 442376 | tf_op jit(solution)/shard_map/ppermute | solution.py:448
  297.6 6.4 %collective-permute-start.33 = (bf16[1,128,1024]{2,1,0:T(8,128)(2,1)S(1)}, bf16[1,128,1024]{2,1,0:T(8,128)(2,1)S(1)}, u32[]{:S(2)}, u32[]{:S(2)}) collective-permute-start(bf16[1,128,1024]{2,1,0:T(8,128)(2,1)S(1)} %dynamic-slice_convert_fusion), channel_id=1, source_target_pairs={{0,2},{1,3},{2,0},{3,1},{4,6},{5,7},{6,4},{7,5},{8,10},{9,11},{10,... | collective-permute-start | bytes 786440 | tf_op jit(solution)/shard_map/ppermute | solution.py:448
  305.5 6.8 %collective-permute-start.36 = (bf16[2,1,32,2304]{3,2,1,0:T(8,128)(2,1)S(1)}, bf16[2,1,32,2304]{3,2,1,0:T(8,128)(2,1)S(1)}, u32[]{:S(2)}, u32[]{:S(2)}) collective-permute-start(bf16[2,1,32,2304]{3,2,1,0:T(8,128)(2,1)S(1)} %get-tuple-element.153), channel_id=1, source_target_pairs={{0,2},{1,3},{2,0},{3,1},{4,6},{5,7},{6,4},{7,5},{8,10},{9,11},{10,... | collective-permute-start | bytes 884744 | tf_op jit(solution)/shard_map/ppermute | solution.py:448
  (88 other events, 468.2 us)
Sparse Core Ops, SparseCore 0:
  34.7 100.8 all-gather.1
  177.6 115.0 reduce-scatter.1
